TPU v7x, 512 devices: a whole 4x4x16 slice. The times are simulated.
512 devices in a mesh: space: 16 (over y_hi, x, core), term: 32 (over y_lo, z).
Axes of the slice: x: 4, y: 4 (y_hi: 2, y_lo: 2; y = y_hi * 2 + y_lo), z: 16, core: 2. Of those that a mesh axis runs over, the one named last changes fastest.
Arguments:
- chaos_field: bfloat16 [256, 2, 8192], P('term', None, 'space'), may hold values from -6 to 6
- stiff_blocks: bfloat16 [64, 32, 6, 256, 256], P('term', 'space'), may hold values from -0.15625 to 0.15625
- stiff_offsets: int32 [64, 32, 6], P('term', 'space'), may hold values from -2 to 2
- triple_blocks: bfloat16 [64, 24, 32, 32], P('term'), may hold values from -0.078125 to 0.078125
- triple_pattern: int32 [64, 24, 2], P('term'), may hold values from 0 to 7, as said below
Outputs:
- applied: float32 [256, 2, 8192], P('term', None, 'space')
Inputs may be any that keep to these rules, and one draw needn't show every extreme that they name: `triple_pattern`: within one term the 24 pairs of block row and block column are distinct.
All inputs are finite; a program needn't handle non-finite values.
Results may differ from a plain program's by a relative error of at most 0.0029.
Values may be sent and summed in bfloat16 or wider, within the bound.
A program may use at most 64 MiB of HBM per device.

v0:
```python
import jax
import jax.numpy as jnp
from jax import lax
from jax.sharding import PartitionSpec as P


def with_halo(block, sides, width):
    for axis, dim in sides:
        count = lax.axis_size(axis)
        forward = [(i, i + 1) for i in range(count - 1)]
        backward = [(target, source) for source, target in forward]
        low = lax.ppermute(
            lax.slice_in_dim(block, block.shape[dim] - width, None, axis=dim), axis, forward
        )
        high = lax.ppermute(lax.slice_in_dim(block, 0, width, axis=dim), axis, backward)
        block = jnp.concatenate([low, block, high], axis=dim)
    return block


def per_device(chaos_field, stiff_blocks, stiff_offsets, triple_blocks, triple_pattern):
    local_rows = chaos_field.shape[0]
    load_count = chaos_field.shape[1]
    cell_count = chaos_field.shape[2]
    term_count = stiff_blocks.shape[0]
    block_width = stiff_blocks.shape[3]
    block_rows = cell_count // block_width
    total_rows = local_rows * lax.axis_size("term")
    rim_cells = 2 * block_width
    gathered = lax.all_gather(chaos_field, "term", axis=0, tiled=True)
    extended = with_halo(gathered, (("space", 2),), rim_cells)
    row_count = extended.shape[0]
    grid_panel = extended.reshape(row_count, load_count, block_rows + 4, block_width)
    base_index = jnp.arange(block_rows, dtype=jnp.int32)[:, None] + 2
    found_images = []
    for term_slot in range(term_count):
        picked = jnp.take(grid_panel, base_index + stiff_offsets[term_slot], axis=2)
        product = jnp.einsum(
            "bsdc,prbsc->prbd", stiff_blocks[term_slot], picked, preferred_element_type=jnp.float32
        )
        found_images.append(product.astype(jnp.bfloat16))
    images = jnp.stack(found_images).reshape(term_count, row_count, load_count, cell_count)
    block_size = triple_blocks.shape[2]
    levels = jnp.arange(total_rows // block_size, dtype=jnp.int32)
    row_hot = (triple_pattern[:, :, 0:1] == levels).astype(jnp.float32)
    col_hot = (triple_pattern[:, :, 1:2] == levels).astype(jnp.float32)
    dense = jnp.einsum("kna,knb,knxy->kaxby", row_hot, col_hot, triple_blocks.astype(jnp.float32))
    dense = dense.reshape(term_count, total_rows, total_rows).astype(jnp.bfloat16)
    flat_images = images.reshape(term_count, total_rows, load_count * cell_count)
    summed = lax.psum_scatter(
        jnp.einsum("kij,kjm->im", dense, flat_images, preferred_element_type=jnp.float32),
        "term",
        scatter_dimension=0,
        tiled=True,
    )
    return summed.reshape(local_rows, load_count, cell_count)


def solution(mesh):
    return jax.shard_map(
        per_device,
        mesh=mesh,
        in_specs=(
            P("term", None, "space"),
            P("term", "space", None, None, None),
            P("term", "space", None),
            P("term", None, None, None),
            P("term", None, None),
        ),
        out_specs=P("term", None, "space"),
        check_vma=False,
    )
```

profile of v0, /device:TPU:4, one launch (start us, length us, event | category | flops | bytes accessed | tf_op | source)
XLA Modules:
  0.0 246.4 jit_solution(5673725449225047085)
XLA Ops:
  6.5 0.0 copy-start
  6.5 0.0 reduce-scatter.2.cloned.1.call-start
  6.5 72.0 %all_gather.3 = bf16[256,2,512]{2,1,0:T(2,128)(2,1)S(1)} all-gather(bf16[8,2,512]{2,1,0:T(2,128)(2,1)} %param.7), channel_id=1, replica_groups=mesh['space'=16,'term'=32] {'term'}, dimensions={0}, use_global_device_ids=true | all-gather | bytes 540672 | tf_op jit(solution)/shard_map/all_gather | solution.py:29
  78.6 0.5 copy.22
  79.1 1.9 collective-permute-start
  81.0 3.6 %collective-permute-start.1 = (bf16[256,2,512]{0,2,1:T(8,128)(2,1)S(1)}, bf16[256,2,512]{0,2,1:T(8,128)(2,1)}, u32[]{:S(2)}, u32[]{:S(2)}) collective-permute-start(bf16[256,2,512]{0,2,1:T(8,128)(2,1)S(1)} %copy.22), channel_id=1, source_target_pairs={{32,0},{64,32},{96,64},{128,96},{160,128},{192,160},{224,192},{256... | collective-permute-start | bytes 1572872 | tf_op jit(solution)/shard_map/ppermute | solution.py:15
  84.7 0.8 fusion.58
  85.5 0.8 compare_and_fusion.1
  86.2 0.1 reshape.44
  86.3 0.1 reshape.48
  86.4 0.0 copy-done
  86.4 0.4 fusion.14
  86.8 0.7 copy.21
  87.5 1.4 convert_element_type.26
  89.0 0.6 collective-permute-done
  89.6 0.0 copy-start.1
  89.6 0.8 copy-done.1
  90.4 1.0 collective-permute-done.1
  91.4 1.3 pad_maximum_fusion
  92.7 0.7 copy.25
  93.4 2.5 %gather_fusion = bf16[12,256,2,256]{3,1,2,0:T(8,128)(2,1)} fusion(bf16[256,2,6,256]{3,0,2,1:T(8,128)(2,1)S(1)} %copy.25, s32[1024]{0:T(1024)S(1)} %pad_clamp_fusion.1), kind=kCustom, calls=%fused_computation.clone | custom fusion | bytes 6291504 | tf_op jit(solution)/shard_map/jit(_take)/gather | solution.py:36
  95.9 3.4 %fusion.35 = bf16[256,2,2,256]{0,3,1,2:T(8,128)(2,1)S(1)} fusion(bf16[2,2,6,256,256]{4,3,2,1,0:T(8,128)(2,1)} %param.8, bf16[2,6,256,2,256]{4,2,3,1,0:T(8,128)(2,1)} %bitcast.102, pred[2,6]{1,0:T(4,128)(4,1)S(1)} %get-tuple-element.6), kind=kOutput, calls=%fused_computation.24 | convolution fusion | flops 807141376 | bytes 5242892 | tf_op jit(solution)/shard_map/bsdc,prbsc->prbd/dot_general | solution.py:37
  99.3 0.2 copy.31
  99.6 2.5 %gather_fusion.1 = bf16[12,256,2,256]{3,1,2,0:T(8,128)(2,1)} fusion(bf16[256,2,6,256]{3,0,2,1:T(8,128)(2,1)S(1)} %copy.25, s32[1024]{0:T(1024)S(1)} %pad_clamp_fusion), kind=kCustom, calls=%fused_computation.1.clone | custom fusion | bytes 6291504 | tf_op jit(solution)/shard_map/jit(_take)/gather | solution.py:36
  102.0 0.0 copy-start.2
  102.0 3.5 %fusion.40 = bf16[256,2,2,256]{0,3,1,2:T(8,128)(2,1)S(1)} fusion(bf16[2,2,6,256,256]{4,3,2,1,0:T(8,128)(2,1)} %param.8, bf16[2,6,256,2,256]{4,2,3,1,0:T(8,128)(2,1)} %bitcast.101, pred[2,6]{1,0:T(4,128)(4,1)S(1)} %get-tuple-element.10), kind=kOutput, calls=%fused_computation.25 | convolution fusion | flops 807141376 | bytes 5242892 | tf_op jit(solution)/shard_map/bsdc,prbsc->prbd/dot_general | solution.py:37
  105.6 0.2 copy.32
  105.8 0.0 copy-done.2
  105.8 1.4 convolution_bitcast_fusion
  107.2 0.0 reduce-scatter.2.cloned.1.call-update
  107.2 130.9 %reduce-scatter.2.cloned.1.call-done = f32[8,1024]{1,0:T(8,128)} async-done(((f32[256,1024]{1,0:T(8,128)}), f32[8,1024]{1,0:T(8,128)}) %reduce-scatter.2.cloned.1.call-update) | async-done | bytes 32784 | tf_op jit(solution)/shard_map/reduce_scatter | solution.py:49
  238.2 1.4 copy.33
  (6 shorter events, 0.1 us)
Async XLA Ops:
  6.5 79.9 %copy-start = (bf16[2,24,32,32]{3,2,1,0:T(8,128)(2,1)S(1)}, bf16[2,24,32,32]{3,2,1,0:T(8,128)(2,1)}, u32[]{:S(2)}) copy-start(bf16[2,24,32,32]{3,2,1,0:T(8,128)(2,1)} %param.10) | copy-start | bytes 294916
  6.5 231.6 %reduce-scatter.2.cloned.1.call-start = ((), (), s32[]{:S(2)}) async-start(), calls=%async_computation.1 | async-start | bytes 1081344 | tf_op jit(solution)/shard_map/reduce_scatter | solution.py:49
  79.1 10.5 %collective-permute-start = (bf16[256,2,512]{0,2,1:T(8,128)(2,1)S(1)}, bf16[256,2,512]{0,2,1:T(8,128)(2,1)S(1)}, u32[]{:S(2)}, u32[]{:S(2)}) collective-permute-start(bf16[256,2,512]{0,2,1:T(8,128)(2,1)S(1)} %copy.22), channel_id=1, source_target_pairs={{0,32},{32,64},{64,96},{96,128},{128,160},{160,192},{192,224},{224... | collective-permute-start | bytes 1572872 | tf_op jit(solution)/shard_map/ppermute | solution.py:12
  81.0 10.3 %collective-permute-start.1 = (bf16[256,2,512]{0,2,1:T(8,128)(2,1)S(1)}, bf16[256,2,512]{0,2,1:T(8,128)(2,1)}, u32[]{:S(2)}, u32[]{:S(2)}) collective-permute-start(bf16[256,2,512]{0,2,1:T(8,128)(2,1)S(1)} %copy.22), channel_id=1, source_target_pairs={{32,0},{64,32},{96,64},{128,96},{160,128},{192,160},{224,192},{256... | collective-permute-start | bytes 1572872 | tf_op jit(solution)/shard_map/ppermute | solution.py:15
  89.6 0.8 copy-start.1
  102.0 3.7 %copy-start.2 = (bf16[2,256,256]{2,1,0:T(8,128)(2,1)S(1)}, bf16[2,256,256]{2,1,0:T(8,128)(2,1)}, u32[]{:S(2)}) copy-start(bf16[2,256,256]{2,1,0:T(8,128)(2,1)} %convert_element_type.26) | copy-start | bytes 786436
Sparse Core Ops, SparseCore 0:
  107.4 130.7 reduce-scatter.1
where the time goes:
time: 247 us; the launch traced here: 246 us
  waiting for transfers between devices  133 us (54%)
  blocking collectives  72 us (29%)
  between operations  13.5 us (5%)
  local copies, waits for them, and re-layouts  11.9 us (5%)
  matrix products  8.74 us (4%)
  starting transfers between devices  5.57 us (2%)
    reduce_scatter x1, waiting for transfers between devices, per_device(): lax.psum_scatter(jnp.einsum('kij,kjm->im', dense, flat_images, preferred_...  131 us
    all_gather x1, blocking collectives, per_device(): gathered = lax.all_gather(chaos_field, 'term', axis=0, tiled=True)  72 us
    dot_general x2, matrix products, per_device(): jnp.einsum('bsdc,prbsc->prbd', stiff_blocks[term_slot], picked, preferred...  6.91 us
    gather x2, local copies, waits for them, and re-layouts, per_device(): picked = jnp.take(grid_panel, base_index + stiff_offsets[term_slot], axis=2)  4.98 us
  transfers between devices with their start and end apart: 3, of which 3 were waited for; matrix products, arithmetic and copies ran while one was open for 2% of the time, Pallas kernels for 0%

commit v1 on v0

--- a/solution.py
+++ b/solution.py
@@ -1,7 +1,120 @@
 import jax
 import jax.numpy as jnp
 from jax import lax
+from jax.experimental import pallas as pl
+from jax.experimental.pallas import tpu as pltpu
 from jax.sharding import PartitionSpec as P
+
+MESH_ID = pl.DeviceIdType.MESH
+
+
+def greet_peers(count):
+    me = lax.axis_index("term")
+    row = lax.axis_index("space")
+    barrier = pltpu.get_barrier_semaphore()
+
+    def greet(step, carry):
+        peer = lax.rem(me + step, count)
+        pl.semaphore_signal(barrier, 1, device_id=(row, peer), device_id_type=MESH_ID)
+        return carry
+
+    lax.fori_loop(1, count, greet, 0)
+    pl.semaphore_wait(barrier, count - 1)
+    return me, row
+
+
+def gather_kernel(block_ref, out_ref, send_sems, recv_sems):
+    count = out_ref.shape[0]
+    me, row = greet_peers(count)
+
+    def outgoing(step):
+        peer = lax.rem(me + step, count)
+        return pltpu.make_async_remote_copy(
+            block_ref, out_ref.at[me], send_sems.at[step], recv_sems.at[me],
+            device_id=(row, peer), device_id_type=MESH_ID,
+        )
+
+    def incoming(step):
+        source = lax.rem(me + count - step, count)
+        return pltpu.make_async_remote_copy(
+            block_ref, out_ref.at[source], send_sems.at[step], recv_sems.at[source],
+            device_id=(row, source), device_id_type=MESH_ID,
+        )
+
+    def start(step, carry):
+        outgoing(step).start()
+        return carry
+
+    lax.fori_loop(1, count, start, 0)
+    out_ref[me] = block_ref[...]
+
+    def finish(step, carry):
+        outgoing(step).wait_send()
+        incoming(step).wait_recv()
+        return carry
+
+    lax.fori_loop(1, count, finish, 0)
+
+
+def gather_term(block):
+    count = lax.axis_size("term")
+    return pl.pallas_call(
+        gather_kernel,
+        out_shape=jax.ShapeDtypeStruct((count,) + block.shape, block.dtype),
+        in_specs=[pl.BlockSpec(memory_space=pltpu.VMEM)],
+        out_specs=pl.BlockSpec(memory_space=pltpu.VMEM),
+        scratch_shapes=[pltpu.SemaphoreType.DMA((count,)), pltpu.SemaphoreType.DMA((count,))],
+        compiler_params=pltpu.CompilerParams(collective_id=0, has_side_effects=True),
+    )(block)
+
+
+def scatter_kernel(part_ref, out_ref, slots, send_sems, recv_sems):
+    count = part_ref.shape[0]
+    me, row = greet_peers(count)
+
+    def outgoing(step):
+        peer = lax.rem(me + step, count)
+        return pltpu.make_async_remote_copy(
+            part_ref.at[peer], slots.at[me], send_sems.at[step], recv_sems.at[me],
+            device_id=(row, peer), device_id_type=MESH_ID,
+        )
+
+    def incoming(step):
+        source = lax.rem(me + count - step, count)
+        return pltpu.make_async_remote_copy(
+            part_ref.at[source], slots.at[source], send_sems.at[step], recv_sems.at[source],
+            device_id=(row, source), device_id_type=MESH_ID,
+        )
+
+    def start(step, carry):
+        outgoing(step).start()
+        return carry
+
+    lax.fori_loop(1, count, start, 0)
+
+    def finish(step, total):
+        outgoing(step).wait_send()
+        incoming(step).wait_recv()
+        source = lax.rem(me + count - step, count)
+        return total + slots[source]
+
+    out_ref[...] = lax.fori_loop(1, count, finish, part_ref[me])
+
+
+def scatter_term(parts):
+    count = parts.shape[0]
+    return pl.pallas_call(
+        scatter_kernel,
+        out_shape=jax.ShapeDtypeStruct(parts.shape[1:], parts.dtype),
+        in_specs=[pl.BlockSpec(memory_space=pltpu.VMEM)],
+        out_specs=pl.BlockSpec(memory_space=pltpu.VMEM),
+        scratch_shapes=[
+            pltpu.VMEM(parts.shape, parts.dtype),
+            pltpu.SemaphoreType.DMA((count,)),
+            pltpu.SemaphoreType.DMA((count,)),
+        ],
+        compiler_params=pltpu.CompilerParams(collective_id=1, has_side_effects=True),
+    )(parts)
 
 
 def with_halo(block, sides, width):
@@ -24,9 +137,11 @@
     term_count = stiff_blocks.shape[0]
     block_width = stiff_blocks.shape[3]
     block_rows = cell_count // block_width
-    total_rows = local_rows * lax.axis_size("term")
+    groups = lax.axis_size("term")
+    total_rows = local_rows * groups
     rim_cells = 2 * block_width
-    gathered = lax.all_gather(chaos_field, "term", axis=0, tiled=True)
+    gathered = gather_term(chaos_field.reshape(local_rows * load_count, cell_count))
+    gathered = gathered.reshape(total_rows, load_count, cell_count)
     extended = with_halo(gathered, (("space", 2),), rim_cells)
     row_count = extended.shape[0]
     grid_panel = extended.reshape(row_count, load_count, block_rows + 4, block_width)
@@ -46,12 +161,8 @@
     dense = jnp.einsum("kna,knb,knxy->kaxby", row_hot, col_hot, triple_blocks.astype(jnp.float32))
     dense = dense.reshape(term_count, total_rows, total_rows).astype(jnp.bfloat16)
     flat_images = images.reshape(term_count, total_rows, load_count * cell_count)
-    summed = lax.psum_scatter(
-        jnp.einsum("kij,kjm->im", dense, flat_images, preferred_element_type=jnp.float32),
-        "term",
-        scatter_dimension=0,
-        tiled=True,
-    )
+    partial = jnp.einsum("kij,kjm->im", dense, flat_images, preferred_element_type=jnp.float32)
+    summed = scatter_term(partial.reshape(groups, local_rows, load_count * cell_count))
     return summed.reshape(local_rows, load_count, cell_count)
 
 

time: 247 us -> 135 us (0.55)
  the two profiles are of different devices: /device:TPU:4 before, /device:TPU:7 now
where the time goes in v1:
time: 135 us; the launch traced here: 134 us
  Pallas kernels  94.2 us (70%)
  local copies, waits for them, and re-layouts  16.6 us (12%)
  starting transfers between devices  8.98 us (7%)
  matrix products  8.76 us (6%)
  waiting for transfers between devices  4.08 us (3%)
  other arithmetic  1.47 us (1%)
    pallas_call x1, Pallas kernels, scatter_term(): pl.pallas_call(scatter_kernel, out_shape=jax.ShapeDtypeStruct(parts.shape...  54.7 us
    pallas_call x1, Pallas kernels, gather_term(): pl.pallas_call(gather_kernel, out_shape=jax.ShapeDtypeStruct((count,) + b...  39.6 us
    ppermute x1, starting transfers between devices, with_halo(): lax.ppermute(lax.slice_in_dim(block, block.shape[dim] - width, None, axis...  7.06 us
    dot_general x2, matrix products, per_device(): jnp.einsum('bsdc,prbsc->prbd', stiff_blocks[term_slot], picked, preferred...  6.92 us
    gather x2, local copies, waits for them, and re-layouts, per_device(): picked = jnp.take(grid_panel, base_index + stiff_offsets[term_slot], axis=2)  4.98 us
    ppermute x1, waiting for transfers between devices, with_halo(): lax.ppermute(lax.slice_in_dim(block, 0, width, axis=dim), axis, backward)  4.08 us
  transfers between devices with their start and end apart: 2, of which 1 were waited for; matrix products, arithmetic and copies ran while one was open for 5% of the time, Pallas kernels for 0%

profile of v1, /device:TPU:7, one launch (start us, length us, event | category | flops | bytes accessed | tf_op | source)
XLA Modules:
  0.0 134.3 jit_solution(11395693411879930285)
XLA Ops:
  0.0 0.0 copy-start
  0.0 1.4 %reshape.32.block_ref = bf16[16,512]{1,0:T(8,128)(2,1)} reshape(bf16[8,2,512]{2,1,0:T(2,128)(2,1)} %param.7) | data formatting | bytes 32768 | tf_op jit(solution)/shard_map/reshape | solution.py:143
  1.4 39.6 %shard_map.55 = bf16[32,16,512]{2,1,0:T(8,128)(2,1)} custom-call(bf16[16,512]{1,0:T(8,128)(2,1)} %reshape.32.block_ref), custom_call_target="tpu_custom_call" | custom-call | tf_op jit(solution)/shard_map/pallas_call | solution.py:61
  41.0 1.2 reshape.33
  42.2 0.5 copy.21
  42.8 7.1 %collective-permute-start = (bf16[256,2,512]{0,2,1:T(8,128)(2,1)S(1)}, bf16[256,2,512]{0,2,1:T(8,128)(2,1)S(1)}, u32[]{:S(2)}, u32[]{:S(2)}) collective-permute-start(bf16[256,2,512]{0,2,1:T(8,128)(2,1)S(1)} %copy.21), channel_id=1, source_target_pairs={{0,32},{32,64},{64,96},{96,128},{128,160},{160,192},{192,224},{224... | collective-permute-start | bytes 1572872 | tf_op jit(solution)/shard_map/ppermute | solution.py:125
  49.8 1.9 %collective-permute-start.1 = (bf16[256,2,512]{0,2,1:T(8,128)(2,1)S(1)}, bf16[256,2,512]{0,2,1:T(8,128)(2,1)S(1)}, u32[]{:S(2)}, u32[]{:S(2)}) collective-permute-start(bf16[256,2,512]{0,2,1:T(8,128)(2,1)S(1)} %copy.21), channel_id=1, source_target_pairs={{32,0},{64,32},{96,64},{128,96},{160,128},{192,160},{224,192},{256... | collective-permute-start | bytes 1572872 | tf_op jit(solution)/shard_map/ppermute | solution.py:128
  51.8 0.8 fusion.58
  52.5 1.3 compare_and_fusion.1
  53.8 1.2 concatenate.12
  55.0 0.1 copy.24
  55.1 0.1 reshape.55
  55.2 0.1 reshape.59
  55.2 0.0 copy-done
  55.2 0.4 fusion.14
  55.7 0.7 copy.20
  56.4 1.4 %convert_element_type.26 = bf16[2,256,256]{2,1,0:T(8,128)(2,1)} reshape(bf16[2,8,32,8,32]{4,3,2,1,0:T(8,128)(2,1)S(1)} %copy.20) | data formatting | bytes 524288 | tf_op jit(solution)/shard_map/convert_element_type | solution.py:162
  57.8 0.0 collective-permute-done
  57.8 0.0 copy-start.2
  57.8 0.8 copy-done.2
  58.6 1.2 copy.23
  59.9 4.1 %collective-permute-done.1 = bf16[256,2,512]{0,2,1:T(8,128)(2,1)S(1)} collective-permute-done((bf16[256,2,512]{0,2,1:T(8,128)(2,1)S(1)}, bf16[256,2,512]{0,2,1:T(8,128)(2,1)S(1)}, u32[]{:S(2)}, u32[]{:S(2)}) %collective-permute-start.1) | collective-permute-done | bytes 524320 | tf_op jit(solution)/shard_map/ppermute | solution.py:128
  64.0 0.2 copy.25
  64.2 0.2 pad_maximum_fusion
  64.3 0.0 copy-start.3
  64.3 2.5 %gather_fusion = bf16[12,256,2,256]{3,1,2,0:T(8,128)(2,1)} fusion(bf16[256,2,6,256]{3,0,2,1:T(8,128)(2,1)S(1)} %pad_maximum_fusion, s32[1024]{0:T(1024)S(1)} %pad_clamp_fusion.1), kind=kCustom, calls=%fused_computation.clone | custom fusion | bytes 6291504 | tf_op jit(solution)/shard_map/jit(_take)/gather | solution.py:151
  66.8 0.0 copy-done.3
  66.8 3.4 %fusion.35 = bf16[256,2,2,256]{0,3,1,2:T(8,128)(2,1)S(1)} fusion(bf16[2,2,6,256,256]{4,3,2,1,0:T(8,128)(2,1)} %param.8, bf16[2,6,256,2,256]{4,2,3,1,0:T(8,128)(2,1)} %bitcast.111, pred[2,6]{1,0:T(4,128)(4,1)S(1)} %copy-done.3), kind=kOutput, calls=%fused_computation.24 | convolution fusion | flops 807141376 | bytes 5242892 | tf_op jit(solution)/shard_map/bsdc,prbsc->prbd/dot_general | solution.py:152
  70.3 0.2 copy.30
  70.5 2.5 %gather_fusion.1 = bf16[12,256,2,256]{3,1,2,0:T(8,128)(2,1)} fusion(bf16[256,2,6,256]{3,0,2,1:T(8,128)(2,1)S(1)} %pad_maximum_fusion, s32[1024]{0:T(1024)S(1)} %pad_clamp_fusion), kind=kCustom, calls=%fused_computation.1.clone | custom fusion | bytes 6291504 | tf_op jit(solution)/shard_map/jit(_take)/gather | solution.py:151
  73.0 0.0 copy-start.1
  73.0 3.5 %fusion.40 = bf16[256,2,2,256]{0,3,1,2:T(8,128)(2,1)S(1)} fusion(bf16[2,2,6,256,256]{4,3,2,1,0:T(8,128)(2,1)} %param.8, bf16[2,6,256,2,256]{4,2,3,1,0:T(8,128)(2,1)} %bitcast.110, pred[2,6]{1,0:T(4,128)(4,1)S(1)} %get-tuple-element.10), kind=kOutput, calls=%fused_computation.25 | convolution fusion | flops 807141376 | bytes 5242892 | tf_op jit(solution)/shard_map/bsdc,prbsc->prbd/dot_general | solution.py:152
  76.6 0.2 copy.31
  76.8 0.0 copy-done.1
  76.8 1.4 %convolution_bitcast_fusion.part_ref = f32[32,8,1024]{2,1,0:T(8,128)} fusion(bf16[1,256,1024]{2,1,0:T(8,128)(2,1)S(1)} %copy.31, bf16[1,256,1024]{2,1,0:T(8,128)(2,1)S(1)} %copy.30, bf16[2,256,256]{2,1,0:T(8,128)(2,1)S(1)} %copy-done.1), kind=kOutput, calls=%fused_computation.21 | convolution fusion | flops 268959744 | bytes 2359296 | tf_op jit(solution)/shard_map/kij,kjm->im/dot_general | solution.py:164
  78.2 54.7 %shard_map.56 = f32[8,1024]{1,0:T(8,128)} custom-call(f32[32,8,1024]{2,1,0:T(8,128)} %convolution_bitcast_fusion.part_ref), custom_call_target="tpu_custom_call" | custom-call | tf_op jit(solution)/shard_map/pallas_call | solution.py:106
  132.9 1.4 %copy.32 = f32[8,2,512]{2,1,0:T(2,128)} copy(f32[8,2,512]{2,0,1:T(8,128)} %bitcast.116) | data formatting | bytes 65536 | tf_op jit(solution)/shard_map/reshape | solution.py:166
  (6 shorter events, 0.1 us)
Async XLA Ops:
  0.0 55.2 %copy-start = (bf16[2,24,32,32]{3,2,1,0:T(8,128)(2,1)S(1)}, bf16[2,24,32,32]{3,2,1,0:T(8,128)(2,1)}, u32[]{:S(2)}) copy-start(bf16[2,24,32,32]{3,2,1,0:T(8,128)(2,1)} %param.10) | copy-start | bytes 294916
  42.8 15.0 %collective-permute-start = (bf16[256,2,512]{0,2,1:T(8,128)(2,1)S(1)}, bf16[256,2,512]{0,2,1:T(8,128)(2,1)S(1)}, u32[]{:S(2)}, u32[]{:S(2)}) collective-permute-start(bf16[256,2,512]{0,2,1:T(8,128)(2,1)S(1)} %copy.21), channel_id=1, source_target_pairs={{0,32},{32,64},{64,96},{96,128},{128,160},{160,192},{192,224},{224... | collective-permute-start | bytes 1572872 | tf_op jit(solution)/shard_map/ppermute | solution.py:125
  49.8 14.1 %collective-permute-start.1 = (bf16[256,2,512]{0,2,1:T(8,128)(2,1)S(1)}, bf16[256,2,512]{0,2,1:T(8,128)(2,1)S(1)}, u32[]{:S(2)}, u32[]{:S(2)}) collective-permute-start(bf16[256,2,512]{0,2,1:T(8,128)(2,1)S(1)} %copy.21), channel_id=1, source_target_pairs={{32,0},{64,32},{96,64},{128,96},{160,128},{192,160},{224,192},{256... | collective-permute-start | bytes 1572872 | tf_op jit(solution)/shard_map/ppermute | solution.py:128
  57.8 0.8 copy-start.2
  64.3 2.5 %copy-start.3 = (pred[2,6]{1,0:T(4,128)(4,1)S(1)}, pred[2,6]{1,0:T(4,128)(4,1)}, u32[]{:S(2)}) copy-start(pred[2,6]{1,0:T(4,128)(4,1)} %get-tuple-element.6) | copy-start | bytes 40
  73.0 3.7 %copy-start.1 = (bf16[2,256,256]{2,1,0:T(8,128)(2,1)S(1)}, bf16[2,256,256]{2,1,0:T(8,128)(2,1)}, u32[]{:S(2)}) copy-start(bf16[2,256,256]{2,1,0:T(8,128)(2,1)} %convert_element_type.26) | copy-start | bytes 786436

commit v2 on v1

--- a/solution.py
+++ b/solution.py
@@ -68,7 +68,7 @@
     )(block)
 
 
-def scatter_kernel(part_ref, out_ref, slots, send_sems, recv_sems):
+def scatter_kernel(part_ref, own_ref, out_ref, slots, send_sems, recv_sems):
     count = part_ref.shape[0]
     me, row = greet_peers(count)
 
@@ -96,25 +96,26 @@
         outgoing(step).wait_send()
         incoming(step).wait_recv()
         source = lax.rem(me + count - step, count)
-        return total + slots[source]
+        return total + slots[source].astype(jnp.float32)
 
-    out_ref[...] = lax.fori_loop(1, count, finish, part_ref[me])
+    out_ref[...] = lax.fori_loop(1, count, finish, own_ref[me])
 
 
 def scatter_term(parts):
     count = parts.shape[0]
+    sent = parts.astype(jnp.bfloat16)
     return pl.pallas_call(
         scatter_kernel,
         out_shape=jax.ShapeDtypeStruct(parts.shape[1:], parts.dtype),
-        in_specs=[pl.BlockSpec(memory_space=pltpu.VMEM)],
+        in_specs=[pl.BlockSpec(memory_space=pltpu.VMEM)] * 2,
         out_specs=pl.BlockSpec(memory_space=pltpu.VMEM),
         scratch_shapes=[
-            pltpu.VMEM(parts.shape, parts.dtype),
+            pltpu.VMEM(sent.shape, sent.dtype),
             pltpu.SemaphoreType.DMA((count,)),
             pltpu.SemaphoreType.DMA((count,)),
         ],
         compiler_params=pltpu.CompilerParams(collective_id=1, has_side_effects=True),
-    )(parts)
+    )(sent, parts)
 
 
 def with_halo(block, sides, width):

time: 135 us -> 112 us (0.83)
  Pallas kernels: 94.2 us -> 71.8 us
    pallas_call x1, Pallas kernels: 54.7 us -> 32.2 us  [scatter_term(): pl.pallas_call(scatter_kernel, out_shape=jax.ShapeDtypeStruct(parts.shape...]
  transfers between devices with their start and end apart: 2 -> 2, of which waited for: 1 -> 1; matrix products, arithmetic and copies ran while one was open for 5% -> 6% of each run, Pallas kernels for 0% -> 0%
where the time goes in v2:
time: 112 us
  Pallas kernels  71.8 us (64%)
  local copies, waits for them, and re-layouts  16.5 us (15%)
  starting transfers between devices  8.98 us (8%)
  matrix products  8.93 us (8%)
  waiting for transfers between devices  4.09 us (4%)
  other arithmetic  1.47 us (1%)
    pallas_call x1, Pallas kernels, gather_term(): pl.pallas_call(gather_kernel, out_shape=jax.ShapeDtypeStruct((count,) + b...  39.6 us
    pallas_call x1, Pallas kernels, scatter_term(): pl.pallas_call(scatter_kernel, out_shape=jax.ShapeDtypeStruct(parts.shape...  32.2 us
    ppermute x1, starting transfers between devices, with_halo(): lax.ppermute(lax.slice_in_dim(block, block.shape[dim] - width, None, axis...  7.06 us
    dot_general x2, matrix products, per_device(): jnp.einsum('bsdc,prbsc->prbd', stiff_blocks[term_slot], picked, preferred...  6.9 us
    gather x2, local copies, waits for them, and re-layouts, per_device(): picked = jnp.take(grid_panel, base_index + stiff_offsets[term_slot], axis=2)  4.97 us
    ppermute x1, waiting for transfers between devices, with_halo(): lax.ppermute(lax.slice_in_dim(block, 0, width, axis=dim), axis, backward)  4.09 us
    concatenate x4, local copies, waits for them, and re-layouts, with_halo(): block = jnp.concatenate([low, block, high], axis=dim)  2.68 us
  transfers between devices with their start and end apart: 2, of which 1 were waited for; matrix products, arithmetic and copies ran while one was open for 6% of the time, Pallas kernels for 0%

profile of v2, /device:TPU:7, one launch (start us, length us, event | category | flops | bytes accessed | tf_op | source)
XLA Modules:
  0.0 112.0 jit_solution(16967263395756436924)
XLA Ops:
  0.0 0.0 copy-start
  0.0 1.4 %reshape.32.block_ref = bf16[16,512]{1,0:T(8,128)(2,1)} reshape(bf16[8,2,512]{2,1,0:T(2,128)(2,1)} %param.7) | data formatting | bytes 32768 | tf_op jit(solution)/shard_map/reshape | solution.py:144
  1.4 39.6 %shard_map.55 = bf16[32,16,512]{2,1,0:T(8,128)(2,1)} custom-call(bf16[16,512]{1,0:T(8,128)(2,1)} %reshape.32.block_ref), custom_call_target="tpu_custom_call" | custom-call | tf_op jit(solution)/shard_map/pallas_call | solution.py:61
  41.0 1.2 %reshape.33 = bf16[256,2,512]{2,1,0:T(2,128)(2,1)S(1)} reshape(bf16[32,16,512]{2,1,0:T(8,128)(2,1)} %shard_map.55) | data formatting | bytes 1048576 | tf_op jit(solution)/shard_map/reshape | solution.py:145
  42.2 0.5 copy.21
  42.8 7.1 %collective-permute-start = (bf16[256,2,512]{0,2,1:T(8,128)(2,1)S(1)}, bf16[256,2,512]{0,2,1:T(8,128)(2,1)S(1)}, u32[]{:S(2)}, u32[]{:S(2)}) collective-permute-start(bf16[256,2,512]{0,2,1:T(8,128)(2,1)S(1)} %copy.21), channel_id=1, source_target_pairs={{0,32},{32,64},{64,96},{96,128},{128,160},{160,192},{192,224},{224... | collective-permute-start | bytes 1572872 | tf_op jit(solution)/shard_map/ppermute | solution.py:126
  49.8 1.9 %collective-permute-start.1 = (bf16[256,2,512]{0,2,1:T(8,128)(2,1)S(1)}, bf16[256,2,512]{0,2,1:T(8,128)(2,1)S(1)}, u32[]{:S(2)}, u32[]{:S(2)}) collective-permute-start(bf16[256,2,512]{0,2,1:T(8,128)(2,1)S(1)} %copy.21), channel_id=1, source_target_pairs={{32,0},{64,32},{96,64},{128,96},{160,128},{192,160},{224,192},{256... | collective-permute-start | bytes 1572872 | tf_op jit(solution)/shard_map/ppermute | solution.py:129
  51.8 0.8 fusion.58
  52.5 1.3 %compare_and_fusion.1 = (pred[2,6]{1,0:T(4,128)(4,1)}, s32[2,6]{1,0:T(2,128)S(1)}, pred[2,6]{1,0:T(4,128)(4,1)S(1)}, s32[2,6]{1,0:T(2,128)S(1)}) fusion(s32[2,2,6]{2,1,0:T(2,128)} %param.9, s32[2]{0:T(128)S(1)} %iota_add_fusion), kind=kLoop, calls=%fused_computation.44 | loop fusion | flops 168 | bytes 224 | tf_op jit(solution)/shard_map/jit(_take)/and | solution.py:152
  53.8 1.2 %concatenate.12 = bf16[256,2,2,256]{3,2,1,0:T(2,128)(2,1)S(1)} reshape(bf16[32,16,512]{2,1,0:T(8,128)(2,1)} %shard_map.55) | data formatting | bytes 1048576 | tf_op jit(solution)/shard_map/concatenate | solution.py:130
  55.0 0.1 copy.24
  55.1 0.1 reshape.55
  55.2 0.1 reshape.59
  55.2 0.0 copy-done
  55.2 0.4 fusion.14
  55.7 0.7 copy.20
  56.4 1.4 %convert_element_type.29 = bf16[2,256,256]{2,1,0:T(8,128)(2,1)} reshape(bf16[2,8,32,8,32]{4,3,2,1,0:T(8,128)(2,1)S(1)} %copy.20) | data formatting | bytes 524288 | tf_op jit(solution)/shard_map/convert_element_type | solution.py:163
  57.8 0.0 collective-permute-done
  57.8 0.0 copy-start.2
  57.8 0.8 copy-done.2
  58.6 1.2 %copy.23 = bf16[256,2,2,256]{3,0,2,1:T(8,128)(2,1)S(1)} copy(bf16[256,2,2,256]{0,3,2,1:T(8,128)(2,1)} %bitcast.119) | data formatting | bytes 1048576 | tf_op jit(solution)/shard_map/concatenate | solution.py:130
  59.9 4.1 %collective-permute-done.1 = bf16[256,2,512]{0,2,1:T(8,128)(2,1)S(1)} collective-permute-done((bf16[256,2,512]{0,2,1:T(8,128)(2,1)S(1)}, bf16[256,2,512]{0,2,1:T(8,128)(2,1)S(1)}, u32[]{:S(2)}, u32[]{:S(2)}) %collective-permute-start.1) | collective-permute-done | bytes 524320 | tf_op jit(solution)/shard_map/ppermute | solution.py:129
  63.9 0.2 copy.25
  64.2 0.2 pad_maximum_fusion
  64.3 0.0 copy-start.3
  64.3 2.5 %gather_fusion = bf16[12,256,2,256]{3,1,2,0:T(8,128)(2,1)} fusion(bf16[256,2,6,256]{3,0,2,1:T(8,128)(2,1)S(1)} %pad_maximum_fusion, s32[1024]{0:T(1024)S(1)} %pad_clamp_fusion.1), kind=kCustom, calls=%fused_computation.clone | custom fusion | bytes 6291504 | tf_op jit(solution)/shard_map/jit(_take)/gather | solution.py:152
  66.8 0.0 copy-done.3
  66.8 3.4 %fusion.35 = bf16[256,2,2,256]{0,3,1,2:T(8,128)(2,1)S(1)} fusion(bf16[2,2,6,256,256]{4,3,2,1,0:T(8,128)(2,1)} %param.8, bf16[2,6,256,2,256]{4,2,3,1,0:T(8,128)(2,1)} %bitcast.115, pred[2,6]{1,0:T(4,128)(4,1)S(1)} %copy-done.3), kind=kOutput, calls=%fused_computation.24 | convolution fusion | flops 807141376 | bytes 5242892 | tf_op jit(solution)/shard_map/bsdc,prbsc->prbd/dot_general | solution.py:153
  70.3 0.2 copy.30
  70.5 2.5 %gather_fusion.1 = bf16[12,256,2,256]{3,1,2,0:T(8,128)(2,1)} fusion(bf16[256,2,6,256]{3,0,2,1:T(8,128)(2,1)S(1)} %pad_maximum_fusion, s32[1024]{0:T(1024)S(1)} %pad_clamp_fusion), kind=kCustom, calls=%fused_computation.1.clone | custom fusion | bytes 6291504 | tf_op jit(solution)/shard_map/jit(_take)/gather | solution.py:152
  73.0 0.0 copy-start.1
  73.0 3.5 %fusion.40 = bf16[256,2,2,256]{0,3,1,2:T(8,128)(2,1)S(1)} fusion(bf16[2,2,6,256,256]{4,3,2,1,0:T(8,128)(2,1)} %param.8, bf16[2,6,256,2,256]{4,2,3,1,0:T(8,128)(2,1)} %bitcast.114, pred[2,6]{1,0:T(4,128)(4,1)S(1)} %get-tuple-element.10), kind=kOutput, calls=%fused_computation.25 | convolution fusion | flops 807141376 | bytes 5242892 | tf_op jit(solution)/shard_map/bsdc,prbsc->prbd/dot_general | solution.py:153
  76.5 0.2 copy.31
  76.8 0.0 copy-done.1
  76.8 1.6 %fusion.59 = (bf16[32,8,1024]{2,1,0:T(8,128)(2,1)}, f32[32,8,1024]{2,1,0:T(8,128)}) fusion(bf16[1,256,1024]{2,1,0:T(8,128)(2,1)S(1)} %copy.31, bf16[1,256,1024]{2,1,0:T(8,128)(2,1)S(1)} %copy.30, bf16[2,256,256]{2,1,0:T(8,128)(2,1)S(1)} %copy-done.1), kind=kOutput, calls=%fused_computation.52 | convolution fusion | flops 269221888 | bytes 2883584 | tf_op jit(solution)/shard_map/kij,kjm->im/dot_general | solution.py:165
  78.4 32.2 %shard_map.56 = f32[8,1024]{1,0:T(8,128)} custom-call(bf16[32,8,1024]{2,1,0:T(8,128)(2,1)} %get-tuple-element.14.part_ref, f32[32,8,1024]{2,1,0:T(8,128)} %get-tuple-element.15.own_ref), custom_call_target="tpu_custom_call" | custom-call | tf_op jit(solution)/shard_map/pallas_call | solution.py:107
  110.6 1.4 %copy.32 = f32[8,2,512]{2,1,0:T(2,128)} copy(f32[8,2,512]{2,0,1:T(8,128)} %bitcast.120) | data formatting | bytes 65536 | tf_op jit(solution)/shard_map/reshape | solution.py:167
  (6 shorter events, 0.1 us)
Async XLA Ops:
  0.0 55.2 %copy-start = (bf16[2,24,32,32]{3,2,1,0:T(8,128)(2,1)S(1)}, bf16[2,24,32,32]{3,2,1,0:T(8,128)(2,1)}, u32[]{:S(2)}) copy-start(bf16[2,24,32,32]{3,2,1,0:T(8,128)(2,1)} %param.10) | copy-start | bytes 294916
  42.8 15.0 %collective-permute-start = (bf16[256,2,512]{0,2,1:T(8,128)(2,1)S(1)}, bf16[256,2,512]{0,2,1:T(8,128)(2,1)S(1)}, u32[]{:S(2)}, u32[]{:S(2)}) collective-permute-start(bf16[256,2,512]{0,2,1:T(8,128)(2,1)S(1)} %copy.21), channel_id=1, source_target_pairs={{0,32},{32,64},{64,96},{96,128},{128,160},{160,192},{192,224},{224... | collective-permute-start | bytes 1572872 | tf_op jit(solution)/shard_map/ppermute | solution.py:126
  49.8 14.1 %collective-permute-start.1 = (bf16[256,2,512]{0,2,1:T(8,128)(2,1)S(1)}, bf16[256,2,512]{0,2,1:T(8,128)(2,1)S(1)}, u32[]{:S(2)}, u32[]{:S(2)}) collective-permute-start(bf16[256,2,512]{0,2,1:T(8,128)(2,1)S(1)} %copy.21), channel_id=1, source_target_pairs={{32,0},{64,32},{96,64},{128,96},{160,128},{192,160},{224,192},{256... | collective-permute-start | bytes 1572872 | tf_op jit(solution)/shard_map/ppermute | solution.py:129
  57.8 0.8 copy-start.2
  64.3 2.5 %copy-start.3 = (pred[2,6]{1,0:T(4,128)(4,1)S(1)}, pred[2,6]{1,0:T(4,128)(4,1)}, u32[]{:S(2)}) copy-start(pred[2,6]{1,0:T(4,128)(4,1)} %get-tuple-element.6) | copy-start | bytes 40
  73.0 3.7 %copy-start.1 = (bf16[2,256,256]{2,1,0:T(8,128)(2,1)S(1)}, bf16[2,256,256]{2,1,0:T(8,128)(2,1)}, u32[]{:S(2)}) copy-start(bf16[2,256,256]{2,1,0:T(8,128)(2,1)} %convert_element_type.29) | copy-start | bytes 786436

commit v3 on v2

--- a/solution.py
+++ b/solution.py
@@ -118,6 +118,54 @@
     )(sent, parts)
 
 
+def image_kernel(offs_ref, panel_ref, stiff_ref, triple_ref, out_ref):
+    term = pl.program_id(0)
+    block = pl.program_id(1)
+    block_rows = pl.num_programs(1)
+    band = stiff_ref.shape[2]
+    width = stiff_ref.shape[-1]
+    loads, rows, span = panel_ref.shape
+    rim = (span // width - block_rows) // 2
+
+    @pl.when((term == 0) & (block == 0))
+    def _():
+        out_ref[...] = jnp.zeros_like(out_ref)
+
+    for load in range(loads):
+        total = jnp.zeros((rows, width), jnp.float32)
+        for slot in range(band):
+            place = block + rim + offs_ref[(term * block_rows + block) * band + slot]
+            start = pl.multiple_of(place * width, width)
+            total += lax.dot_general(
+                panel_ref[load, :, pl.ds(start, width)], stiff_ref[0, 0, slot],
+                (((1,), (1,)), ((), ())), preferred_element_type=jnp.float32,
+            )
+        image = total.astype(jnp.bfloat16)
+        column = pl.multiple_of((load * block_rows + block) * width, width)
+        out_ref[:, pl.ds(column, width)] += jnp.dot(
+            triple_ref[0], image, preferred_element_type=jnp.float32
+        )
+
+
+def image_contract(offsets, panel, stiff_blocks, dense):
+    term_count, block_rows, band, width, _ = stiff_blocks.shape
+    loads, rows, span = panel.shape
+    return pl.pallas_call(
+        image_kernel,
+        out_shape=jax.ShapeDtypeStruct((rows, loads * block_rows * width), jnp.float32),
+        grid_spec=pltpu.PrefetchScalarGridSpec(
+            num_scalar_prefetch=1,
+            grid=(term_count, block_rows),
+            in_specs=[
+                pl.BlockSpec((loads, rows, span), lambda k, b, offs: (0, 0, 0)),
+                pl.BlockSpec((1, 1, band, width, width), lambda k, b, offs: (k, b, 0, 0, 0)),
+                pl.BlockSpec((1, rows, rows), lambda k, b, offs: (k, 0, 0)),
+            ],
+            out_specs=pl.BlockSpec((rows, loads * block_rows * width), lambda k, b, offs: (0, 0)),
+        ),
+    )(offsets.reshape(-1), panel, stiff_blocks, dense)
+
+
 def with_halo(block, sides, width):
     for axis, dim in sides:
         count = lax.axis_size(axis)
@@ -142,27 +190,16 @@
     total_rows = local_rows * groups
     rim_cells = 2 * block_width
     gathered = gather_term(chaos_field.reshape(local_rows * load_count, cell_count))
-    gathered = gathered.reshape(total_rows, load_count, cell_count)
-    extended = with_halo(gathered, (("space", 2),), rim_cells)
-    row_count = extended.shape[0]
-    grid_panel = extended.reshape(row_count, load_count, block_rows + 4, block_width)
-    base_index = jnp.arange(block_rows, dtype=jnp.int32)[:, None] + 2
-    found_images = []
-    for term_slot in range(term_count):
-        picked = jnp.take(grid_panel, base_index + stiff_offsets[term_slot], axis=2)
-        product = jnp.einsum(
-            "bsdc,prbsc->prbd", stiff_blocks[term_slot], picked, preferred_element_type=jnp.float32
-        )
-        found_images.append(product.astype(jnp.bfloat16))
-    images = jnp.stack(found_images).reshape(term_count, row_count, load_count, cell_count)
+    panel = gathered.reshape(groups, local_rows, load_count, cell_count).transpose(2, 0, 1, 3)
+    panel = panel.reshape(load_count, total_rows, cell_count)
+    extended = with_halo(panel, (("space", 2),), rim_cells)
     block_size = triple_blocks.shape[2]
     levels = jnp.arange(total_rows // block_size, dtype=jnp.int32)
     row_hot = (triple_pattern[:, :, 0:1] == levels).astype(jnp.float32)
     col_hot = (triple_pattern[:, :, 1:2] == levels).astype(jnp.float32)
     dense = jnp.einsum("kna,knb,knxy->kaxby", row_hot, col_hot, triple_blocks.astype(jnp.float32))
     dense = dense.reshape(term_count, total_rows, total_rows).astype(jnp.bfloat16)
-    flat_images = images.reshape(term_count, total_rows, load_count * cell_count)
-    partial = jnp.einsum("kij,kjm->im", dense, flat_images, preferred_element_type=jnp.float32)
+    partial = image_contract(stiff_offsets, extended, stiff_blocks, dense)
     summed = scatter_term(partial.reshape(groups, local_rows, load_count * cell_count))
     return summed.reshape(local_rows, load_count, cell_count)
 

time: 112 us -> 109 us (0.973)
  local copies, waits for them, and re-layouts: 16.5 us -> 7.56 us
  matrix products: 8.93 us -> 0.42 us
  Pallas kernels: 71.8 us -> 79.3 us
  waiting for transfers between devices: 4.09 us -> 8.27 us
  other arithmetic: 1.47 us -> 3.35 us
    pallas_call x0 -> x1, Pallas kernels: none -> 8.93 us  [image_contract(): pl.pallas_call(image_kernel, out_shape=jax.ShapeDtypeStruct((rows, loads...]
    dot_general x3 -> x0, matrix products: 8.5 us -> none  [the longest x2 6.9 us: per_device(): jnp.einsum('bsdc,prbsc->prbd', stiff_blocks[term_slot], picked, preferred...]
    gather x2 -> x0, local copies, waits for them, and re-layouts: 4.97 us -> none  [per_device(): picked = jnp.take(grid_panel, base_index + stiff_offsets[term_slot], axis=2)]
    ppermute x1, waiting for transfers between devices: 4.09 us -> 8.01 us  [with_halo(): lax.ppermute(lax.slice_in_dim(block, 0, width, axis=dim), axis, backward)]
    concatenate x4 -> x0, local copies, waits for them, and re-layouts: 2.68 us -> none  [with_halo(): block = jnp.concatenate([low, block, high], axis=dim)]
    convert_element_type x0 -> x1, other arithmetic: none -> 2.09 us  [scatter_term(): sent = parts.astype(jnp.bfloat16)]
    pallas_call x1, Pallas kernels: 32.2 us -> 30.8 us  [scatter_term(): pl.pallas_call(scatter_kernel, out_shape=jax.ShapeDtypeStruct(parts.shape...]
    and x1 -> x0, other arithmetic: 1.28 us -> none  [per_device(): picked = jnp.take(grid_panel, base_index + stiff_offsets[term_slot], axis=2)]
  transfers between devices with their start and end apart: 2 -> 2, of which waited for: 1 -> 2; matrix products, arithmetic and copies ran while one was open for 6% -> 4% of each run, Pallas kernels for 0% -> 0%
where the time goes in v3:
time: 109 us; the launch traced here: 108 us
  Pallas kernels  79.3 us (73%)
  starting transfers between devices  8.98 us (8%)
  waiting for transfers between devices  8.27 us (8%)
  local copies, waits for them, and re-layouts  7.56 us (7%)
  other arithmetic  3.35 us (3%)
    pallas_call x1, Pallas kernels, gather_term(): pl.pallas_call(gather_kernel, out_shape=jax.ShapeDtypeStruct((count,) + b...  39.6 us
    pallas_call x1, Pallas kernels, scatter_term(): pl.pallas_call(scatter_kernel, out_shape=jax.ShapeDtypeStruct(parts.shape...  30.8 us
    pallas_call x1, Pallas kernels, image_contract(): pl.pallas_call(image_kernel, out_shape=jax.ShapeDtypeStruct((rows, loads...  8.93 us
    ppermute x1, waiting for transfers between devices, with_halo(): lax.ppermute(lax.slice_in_dim(block, 0, width, axis=dim), axis, backward)  8.01 us
    ppermute x1, starting transfers between devices, with_halo(): lax.ppermute(lax.slice_in_dim(block, block.shape[dim] - width, None, axis...  7.06 us
  transfers between devices with their start and end apart: 2, of which 2 were waited for; matrix products, arithmetic and copies ran while one was open for 4% of the time, Pallas kernels for 0%

profile of v3, /device:TPU:7, one launch (start us, length us, event | category | flops | bytes accessed | tf_op | source)
XLA Modules:
  0.0 107.9 jit_solution(4116931642627868516)
XLA Ops:
  0.0 0.0 copy-start
  0.0 1.4 %reshape.21.block_ref = bf16[16,512]{1,0:T(8,128)(2,1)} reshape(bf16[8,2,512]{2,1,0:T(2,128)(2,1)} %param.5) | data formatting | bytes 32768 | tf_op jit(solution)/shard_map/reshape | solution.py:192
  1.4 39.6 %shard_map.55 = bf16[32,16,512]{2,1,0:T(8,128)(2,1)} custom-call(bf16[16,512]{1,0:T(8,128)(2,1)} %reshape.21.block_ref), custom_call_target="tpu_custom_call" | custom-call | tf_op jit(solution)/shard_map/pallas_call | solution.py:61
  41.0 1.2 %reshape.22 = bf16[32,8,2,512]{3,2,1,0:T(2,128)(2,1)S(1)} reshape(bf16[32,16,512]{2,1,0:T(8,128)(2,1)} %shard_map.55) | data formatting | bytes 1048576 | tf_op jit(solution)/shard_map/reshape | solution.py:193
  42.2 0.0 copy-start.1
  42.2 0.1 copy.17
  42.3 7.1 %collective-permute-start = (bf16[2,256,512]{2,1,0:T(8,128)(2,1)S(1)}, bf16[2,256,512]{2,1,0:T(8,128)(2,1)S(1)}, u32[]{:S(2)}, u32[]{:S(2)}) collective-permute-start(bf16[2,256,512]{2,1,0:T(8,128)(2,1)S(1)} %bitcast.22), channel_id=1, source_target_pairs={{0,32},{32,64},{64,96},{96,128},{128,160},{160,192},{192,224},{224... | collective-permute-start | bytes 1572872 | tf_op jit(solution)/shard_map/ppermute | solution.py:174
  49.3 1.9 %collective-permute-start.1 = (bf16[2,256,512]{2,1,0:T(8,128)(2,1)S(1)}, bf16[2,256,512]{2,1,0:T(8,128)(2,1)S(1)}, u32[]{:S(2)}, u32[]{:S(2)}) collective-permute-start(bf16[2,256,512]{2,1,0:T(8,128)(2,1)S(1)} %bitcast.23), channel_id=1, source_target_pairs={{32,0},{64,32},{96,64},{128,96},{160,128},{192,160},{224,192},{256... | collective-permute-start | bytes 1572872 | tf_op jit(solution)/shard_map/ppermute | solution.py:177
  51.3 0.8 fusion.8
  52.0 0.0 copy-done
  52.0 0.4 fusion
  52.5 0.7 copy.8
  53.2 1.4 %convert_element_type.15.triple_ref = bf16[2,256,256]{2,1,0:T(8,128)(2,1)} reshape(bf16[2,8,32,8,32]{4,3,2,1,0:T(8,128)(2,1)S(1)} %copy.8) | data formatting | bytes 524288 | tf_op jit(solution)/shard_map/convert_element_type | solution.py:201
  54.6 0.0 copy-done.1
  54.6 0.6 reshape.20.offs_ref
  55.2 0.3 collective-permute-done
  55.4 8.0 %collective-permute-done.1 = bf16[2,256,512]{2,1,0:T(8,128)(2,1)S(1)} collective-permute-done((bf16[2,256,512]{2,1,0:T(8,128)(2,1)S(1)}, bf16[2,256,512]{2,1,0:T(8,128)(2,1)S(1)}, u32[]{:S(2)}, u32[]{:S(2)}) %collective-permute-start.1) | collective-permute-done | bytes 524320 | tf_op jit(solution)/shard_map/ppermute | solution.py:177
  63.5 1.3 %pad_maximum_fusion.panel_ref = bf16[2,256,1536]{2,1,0:T(8,128)(2,1)} fusion(bf16[2,256,512]{2,1,0:T(8,128)(2,1)S(1)} %collective-permute-done.1, bf16[2,256,512]{2,1,0:T(8,128)(2,1)S(1)} %bitcast.24, bf16[2,256,512]{2,1,0:T(8,128)(2,1)S(1)} %collective-permute-done), kind=kLoop, calls=%fused_computation | loop fusion | flops 4718592 | bytes 3145728 | tf_op jit(solution)/shard_map/concatenate | solution.py:178
  64.7 8.9 %shard_map.56 = f32[256,1024]{1,0:T(8,128)} custom-call(s32[24]{0:T(128)} %reshape.20.offs_ref, bf16[2,256,1536]{2,1,0:T(8,128)(2,1)} %pad_maximum_fusion.panel_ref, bf16[2,2,6,256,256]{4,3,2,1,0:T(8,128)(2,1)} %stiff_ref.1, bf16[2,256,256]{2,1,0:T(8,128)(2,1)} %convert_element_type.15.triple_ref), custom_call_target="tpu_custom_call" | custom-call | tf_op jit(solution)/shard_map/pallas_call | solution.py:153
  73.7 2.1 %bitcast_convert_fusion.part_ref = bf16[32,8,1024]{2,1,0:T(8,128)(2,1)} fusion(f32[256,1024]{1,0:T(8,128)} %shard_map.56), kind=kLoop, calls=%fused_computation.13 | loop fusion | flops 262144 | bytes 1572864 | tf_op jit(solution)/shard_map/convert_element_type | solution.py:106
  75.7 30.8 %shard_map.57 = f32[8,1024]{1,0:T(8,128)} custom-call(bf16[32,8,1024]{2,1,0:T(8,128)(2,1)} %bitcast_convert_fusion.part_ref, f32[32,8,1024]{2,1,0:T(8,128)} %bitcast.21), custom_call_target="tpu_custom_call" | custom-call | tf_op jit(solution)/shard_map/pallas_call | solution.py:107
  106.5 1.4 %copy.9 = f32[8,2,512]{2,1,0:T(2,128)} copy(f32[8,2,512]{2,0,1:T(8,128)} %bitcast.25) | data formatting | bytes 65536 | tf_op jit(solution)/shard_map/reshape | solution.py:204
  (1 shorter events, 0.0 us)
Async XLA Ops:
  0.0 52.0 %copy-start = (bf16[2,24,32,32]{3,2,1,0:T(8,128)(2,1)S(1)}, bf16[2,24,32,32]{3,2,1,0:T(8,128)(2,1)}, u32[]{:S(2)}) copy-start(bf16[2,24,32,32]{3,2,1,0:T(8,128)(2,1)} %param.8) | copy-start | bytes 294916
  42.2 12.4 %copy-start.1 = (s32[2,2,6]{2,1,0:T(2,128)S(1)}, s32[2,2,6]{2,1,0:T(2,128)}, u32[]{:S(2)}) copy-start(s32[2,2,6]{2,1,0:T(2,128)} %param.7) | copy-start | bytes 292
  42.3 13.2 %collective-permute-start = (bf16[2,256,512]{2,1,0:T(8,128)(2,1)S(1)}, bf16[2,256,512]{2,1,0:T(8,128)(2,1)S(1)}, u32[]{:S(2)}, u32[]{:S(2)}) collective-permute-start(bf16[2,256,512]{2,1,0:T(8,128)(2,1)S(1)} %bitcast.22), channel_id=1, source_target_pairs={{0,32},{32,64},{64,96},{96,128},{128,160},{160,192},{192,224},{224... | collective-permute-start | bytes 1572872 | tf_op jit(solution)/shard_map/ppermute | solution.py:174
  49.3 14.1 %collective-permute-start.1 = (bf16[2,256,512]{2,1,0:T(8,128)(2,1)S(1)}, bf16[2,256,512]{2,1,0:T(8,128)(2,1)S(1)}, u32[]{:S(2)}, u32[]{:S(2)}) collective-permute-start(bf16[2,256,512]{2,1,0:T(8,128)(2,1)S(1)} %bitcast.23), channel_id=1, source_target_pairs={{32,0},{64,32},{96,64},{128,96},{160,128},{192,160},{224,192},{256... | collective-permute-start | bytes 1572872 | tf_op jit(solution)/shard_map/ppermute | solution.py:177

commit v4 on v3

--- a/solution.py
+++ b/solution.py
@@ -23,37 +23,92 @@
     return me, row
 
 
-def gather_kernel(block_ref, out_ref, send_sems, recv_sems):
+CLASSES = 4
+
+
+def gather_kernel(block_ref, out_ref, local_sem, send_near, recv_near, send_far, recv_far):
     count = out_ref.shape[0]
-    me, row = greet_peers(count)
-
-    def outgoing(step):
-        peer = lax.rem(me + step, count)
-        return pltpu.make_async_remote_copy(
-            block_ref, out_ref.at[me], send_sems.at[step], recv_sems.at[me],
-            device_id=(row, peer), device_id_type=MESH_ID,
-        )
-
-    def incoming(step):
-        source = lax.rem(me + count - step, count)
-        return pltpu.make_async_remote_copy(
-            block_ref, out_ref.at[source], send_sems.at[step], recv_sems.at[source],
-            device_id=(row, source), device_id_type=MESH_ID,
-        )
-
-    def start(step, carry):
-        outgoing(step).start()
-        return carry
-
-    lax.fori_loop(1, count, start, 0)
-    out_ref[me] = block_ref[...]
-
-    def finish(step, carry):
-        outgoing(step).wait_send()
-        incoming(step).wait_recv()
-        return carry
-
-    lax.fori_loop(1, count, finish, 0)
+    chunk = count // CLASSES
+    me = lax.axis_index("term")
+    row = lax.axis_index("space")
+    stride, lane = me // CLASSES, me % CLASSES
+    barrier = pltpu.get_barrier_semaphore()
+
+    def far_peer(step):
+        return lax.rem(stride + step, chunk) * CLASSES + lane
+
+    def near_peer(step):
+        return stride * CLASSES + lax.rem(lane + step, CLASSES)
+
+    def greet_far(step, carry):
+        pl.semaphore_signal(barrier, 1, device_id=(row, far_peer(step)), device_id_type=MESH_ID)
+        return carry
+
+    def greet_near(step, carry):
+        pl.semaphore_signal(barrier, 1, device_id=(row, near_peer(step)), device_id_type=MESH_ID)
+        return carry
+
+    lax.fori_loop(1, chunk, greet_far, 0)
+    lax.fori_loop(1, CLASSES, greet_near, 0)
+    pl.semaphore_wait(barrier, chunk + CLASSES - 2)
+
+    mine = lane * chunk + stride
+    local = pltpu.make_async_copy(block_ref, out_ref.at[mine], local_sem)
+    local.start()
+
+    def far_out(step):
+        return pltpu.make_async_remote_copy(
+            block_ref, out_ref.at[mine], send_far.at[step], recv_far.at[stride],
+            device_id=(row, far_peer(step)), device_id_type=MESH_ID,
+        )
+
+    def far_in(step):
+        source = lax.rem(stride + chunk - step, chunk)
+        return pltpu.make_async_remote_copy(
+            block_ref, out_ref.at[lane * chunk + source], send_far.at[step], recv_far.at[source],
+            device_id=(row, source * CLASSES + lane), device_id_type=MESH_ID,
+        )
+
+    def far_start(step, carry):
+        far_out(step).start()
+        return carry
+
+    def far_finish(step, carry):
+        far_out(step).wait_send()
+        far_in(step).wait_recv()
+        return carry
+
+    lax.fori_loop(1, chunk, far_start, 0)
+    local.wait()
+    lax.fori_loop(1, chunk, far_finish, 0)
+
+    own = out_ref.at[pl.ds(lane * chunk, chunk)]
+
+    def near_out(step):
+        return pltpu.make_async_remote_copy(
+            own, own, send_near.at[step], recv_near.at[lane],
+            device_id=(row, near_peer(step)), device_id_type=MESH_ID,
+        )
+
+    def near_in(step):
+        source = lax.rem(lane + CLASSES - step, CLASSES)
+        theirs = out_ref.at[pl.ds(source * chunk, chunk)]
+        return pltpu.make_async_remote_copy(
+            theirs, theirs, send_near.at[step], recv_near.at[source],
+            device_id=(row, stride * CLASSES + source), device_id_type=MESH_ID,
+        )
+
+    def near_start(step, carry):
+        near_out(step).start()
+        return carry
+
+    def near_finish(step, carry):
+        near_out(step).wait_send()
+        near_in(step).wait_recv()
+        return carry
+
+    lax.fori_loop(1, CLASSES, near_start, 0)
+    lax.fori_loop(1, CLASSES, near_finish, 0)
 
 
 def gather_term(block):
@@ -63,7 +118,13 @@
         out_shape=jax.ShapeDtypeStruct((count,) + block.shape, block.dtype),
         in_specs=[pl.BlockSpec(memory_space=pltpu.VMEM)],
         out_specs=pl.BlockSpec(memory_space=pltpu.VMEM),
-        scratch_shapes=[pltpu.SemaphoreType.DMA((count,)), pltpu.SemaphoreType.DMA((count,))],
+        scratch_shapes=[
+            pltpu.SemaphoreType.DMA(()),
+            pltpu.SemaphoreType.DMA((CLASSES,)),
+            pltpu.SemaphoreType.DMA((CLASSES,)),
+            pltpu.SemaphoreType.DMA((count // CLASSES,)),
+            pltpu.SemaphoreType.DMA((count // CLASSES,)),
+        ],
         compiler_params=pltpu.CompilerParams(collective_id=0, has_side_effects=True),
     )(block)
 
@@ -198,7 +259,9 @@
     row_hot = (triple_pattern[:, :, 0:1] == levels).astype(jnp.float32)
     col_hot = (triple_pattern[:, :, 1:2] == levels).astype(jnp.float32)
     dense = jnp.einsum("kna,knb,knxy->kaxby", row_hot, col_hot, triple_blocks.astype(jnp.float32))
-    dense = dense.reshape(term_count, total_rows, total_rows).astype(jnp.bfloat16)
+    dense = dense.reshape(term_count, total_rows, groups // CLASSES, CLASSES, local_rows)
+    dense = dense.transpose(0, 1, 3, 2, 4).reshape(term_count, total_rows, total_rows)
+    dense = dense.astype(jnp.bfloat16)
     partial = image_contract(stiff_offsets, extended, stiff_blocks, dense)
     summed = scatter_term(partial.reshape(groups, local_rows, load_count * cell_count))
     return summed.reshape(local_rows, load_count, cell_count)

time: 109 us -> 105 us (0.963)
  Pallas kernels: 79.3 us -> 74.7 us
    pallas_call x1, Pallas kernels: 39.6 us -> 33.2 us  [gather_term(): pl.pallas_call(gather_kernel, out_shape=jax.ShapeDtypeStruct((count,) + b...]
    pallas_call x1, Pallas kernels: 30.8 us -> 32.5 us  [scatter_term(): pl.pallas_call(scatter_kernel, out_shape=jax.ShapeDtypeStruct(parts.shape...]
    convert_element_type x2 -> x4, local copies, waits for them, and re-layouts: 2.11 us -> 2.55 us  [per_device(): dense = dense.astype(jnp.bfloat16)]
  transfers between devices with their start and end apart: 2 -> 2, of which waited for: 2 -> 1; matrix products, arithmetic and copies ran while one was open for 4% -> 4% of each run, Pallas kernels for 0% -> 0%
where the time goes in v4:
time: 105 us; the launch traced here: 104 us
  Pallas kernels  74.7 us (71%)
  starting transfers between devices  8.94 us (9%)
  local copies, waits for them, and re-layouts  7.99 us (8%)
  waiting for transfers between devices  7.92 us (8%)
  other arithmetic  4.39 us (4%)
    pallas_call x1, Pallas kernels, gather_term(): pl.pallas_call(gather_kernel, out_shape=jax.ShapeDtypeStruct((count,) + b...  33.2 us
    pallas_call x1, Pallas kernels, scatter_term(): pl.pallas_call(scatter_kernel, out_shape=jax.ShapeDtypeStruct(parts.shape...  32.5 us
    pallas_call x1, Pallas kernels, image_contract(): pl.pallas_call(image_kernel, out_shape=jax.ShapeDtypeStruct((rows, loads...  8.94 us
    ppermute x1, waiting for transfers between devices, with_halo(): lax.ppermute(lax.slice_in_dim(block, 0, width, axis=dim), axis, backward)  7.92 us
    ppermute x1, starting transfers between devices, with_halo(): lax.ppermute(lax.slice_in_dim(block, block.shape[dim] - width, None, axis...  7.01 us
    convert_element_type x4, local copies, waits for them, and re-layouts, per_device(): dense = dense.astype(jnp.bfloat16)  2.55 us
    concatenate x1, other arithmetic, with_halo(): block = jnp.concatenate([low, block, high], axis=dim)  2.3 us
  transfers between devices with their start and end apart: 2, of which 1 were waited for; matrix products, arithmetic and copies ran while one was open for 4% of the time, Pallas kernels for 0%

profile of v4, /device:TPU:7, one launch (start us, length us, event | category | flops | bytes accessed | tf_op | source)
XLA Modules:
  0.0 104.4 jit_solution(4326999721683754398)
XLA Ops:
  0.0 0.0 copy-start
  0.0 1.4 %reshape.23.block_ref = bf16[16,512]{1,0:T(8,128)(2,1)} reshape(bf16[8,2,512]{2,1,0:T(2,128)(2,1)} %param.5) | data formatting | bytes 32768 | tf_op jit(solution)/shard_map/reshape | solution.py:253
  1.4 33.2 %shard_map.55 = bf16[32,16,512]{2,1,0:T(8,128)(2,1)} custom-call(bf16[16,512]{1,0:T(8,128)(2,1)} %reshape.23.block_ref), custom_call_target="tpu_custom_call" | custom-call | tf_op jit(solution)/shard_map/pallas_call | solution.py:116
  34.6 1.2 %reshape.24 = bf16[32,8,2,512]{3,2,1,0:T(2,128)(2,1)S(1)} reshape(bf16[32,16,512]{2,1,0:T(8,128)(2,1)} %shard_map.55) | data formatting | bytes 1048576 | tf_op jit(solution)/shard_map/reshape | solution.py:254
  35.8 0.1 copy.22
  35.9 0.0 copy-start.1
  35.9 7.0 %collective-permute-start = (bf16[2,256,512]{2,1,0:T(8,128)(2,1)S(1)}, bf16[2,256,512]{2,1,0:T(8,128)(2,1)S(1)}, u32[]{:S(2)}, u32[]{:S(2)}) collective-permute-start(bf16[2,256,512]{2,1,0:T(8,128)(2,1)S(1)} %bitcast.26), channel_id=1, source_target_pairs={{0,32},{32,64},{64,96},{96,128},{128,160},{160,192},{192,224},{224... | collective-permute-start | bytes 1572872 | tf_op jit(solution)/shard_map/ppermute | solution.py:235
  42.9 1.9 %collective-permute-start.1 = (bf16[2,256,512]{2,1,0:T(8,128)(2,1)S(1)}, bf16[2,256,512]{2,1,0:T(8,128)(2,1)}, u32[]{:S(2)}, u32[]{:S(2)}) collective-permute-start(bf16[2,256,512]{2,1,0:T(8,128)(2,1)S(1)} %bitcast.27), channel_id=1, source_target_pairs={{32,0},{64,32},{96,64},{128,96},{160,128},{192,160},{224,192},{256... | collective-permute-start | bytes 1572872 | tf_op jit(solution)/shard_map/ppermute | solution.py:238
  44.9 0.8 fusion.8
  45.6 0.0 copy-done
  45.6 0.4 fusion
  46.1 1.0 copy.11
  47.1 0.7 convert_element_type.19
  47.8 0.8 copy.13.triple_ref
  48.6 0.0 copy-done.1
  48.6 0.6 reshape.22.offs_ref
  49.2 0.0 collective-permute-done
  49.2 7.9 %collective-permute-done.1 = bf16[2,256,512]{2,1,0:T(8,128)(2,1)} collective-permute-done((bf16[2,256,512]{2,1,0:T(8,128)(2,1)S(1)}, bf16[2,256,512]{2,1,0:T(8,128)(2,1)}, u32[]{:S(2)}, u32[]{:S(2)}) %collective-permute-start.1) | collective-permute-done | bytes 524320 | tf_op jit(solution)/shard_map/ppermute | solution.py:238
  57.2 2.3 %pad_maximum_fusion.panel_ref = bf16[2,256,1536]{2,1,0:T(8,128)(2,1)} fusion(bf16[2,256,512]{2,1,0:T(8,128)(2,1)} %collective-permute-done.1, bf16[2,256,512]{2,1,0:T(8,128)(2,1)S(1)} %bitcast.28, bf16[2,256,512]{2,1,0:T(8,128)(2,1)S(1)} %collective-permute-done), kind=kLoop, calls=%fused_computation | loop fusion | flops 4718592 | bytes 3145728 | tf_op jit(solution)/shard_map/concatenate | solution.py:239
  59.5 8.9 %shard_map.56 = f32[256,1024]{1,0:T(8,128)} custom-call(s32[24]{0:T(128)} %reshape.22.offs_ref, bf16[2,256,1536]{2,1,0:T(8,128)(2,1)} %pad_maximum_fusion.panel_ref, bf16[2,2,6,256,256]{4,3,2,1,0:T(8,128)(2,1)} %stiff_ref.1, bf16[2,256,256]{2,1,0:T(8,128)(2,1)} %copy.13.triple_ref), custom_call_target="tpu_custom_call" | custom-call | tf_op jit(solution)/shard_map/pallas_call | solution.py:214
  68.4 2.1 %bitcast_convert_fusion.part_ref = bf16[32,8,1024]{2,1,0:T(8,128)(2,1)} fusion(f32[256,1024]{1,0:T(8,128)} %shard_map.56), kind=kLoop, calls=%fused_computation.13 | loop fusion | flops 262144 | bytes 1572864 | tf_op jit(solution)/shard_map/convert_element_type | solution.py:167
  70.5 32.5 %shard_map.57 = f32[8,1024]{1,0:T(8,128)} custom-call(bf16[32,8,1024]{2,1,0:T(8,128)(2,1)} %bitcast_convert_fusion.part_ref, f32[32,8,1024]{2,1,0:T(8,128)} %bitcast.25), custom_call_target="tpu_custom_call" | custom-call | tf_op jit(solution)/shard_map/pallas_call | solution.py:168
  103.0 1.4 %copy.14 = f32[8,2,512]{2,1,0:T(2,128)} copy(f32[8,2,512]{2,0,1:T(8,128)} %bitcast.31) | data formatting | bytes 65536 | tf_op jit(solution)/shard_map/reshape | solution.py:267
  (2 shorter events, 0.0 us)
Async XLA Ops:
  0.0 45.6 %copy-start = (bf16[2,24,32,32]{3,2,1,0:T(8,128)(2,1)S(1)}, bf16[2,24,32,32]{3,2,1,0:T(8,128)(2,1)}, u32[]{:S(2)}) copy-start(bf16[2,24,32,32]{3,2,1,0:T(8,128)(2,1)} %param.8) | copy-start | bytes 294916
  35.9 12.7 %copy-start.1 = (s32[2,2,6]{2,1,0:T(2,128)S(1)}, s32[2,2,6]{2,1,0:T(2,128)}, u32[]{:S(2)}) copy-start(s32[2,2,6]{2,1,0:T(2,128)} %param.7) | copy-start | bytes 292
  35.9 13.3 %collective-permute-start = (bf16[2,256,512]{2,1,0:T(8,128)(2,1)S(1)}, bf16[2,256,512]{2,1,0:T(8,128)(2,1)S(1)}, u32[]{:S(2)}, u32[]{:S(2)}) collective-permute-start(bf16[2,256,512]{2,1,0:T(8,128)(2,1)S(1)} %bitcast.26), channel_id=1, source_target_pairs={{0,32},{32,64},{64,96},{96,128},{128,160},{160,192},{192,224},{224... | collective-permute-start | bytes 1572872 | tf_op jit(solution)/shard_map/ppermute | solution.py:235
  42.9 14.2 %collective-permute-start.1 = (bf16[2,256,512]{2,1,0:T(8,128)(2,1)S(1)}, bf16[2,256,512]{2,1,0:T(8,128)(2,1)}, u32[]{:S(2)}, u32[]{:S(2)}) collective-permute-start(bf16[2,256,512]{2,1,0:T(8,128)(2,1)S(1)} %bitcast.27), channel_id=1, source_target_pairs={{32,0},{64,32},{96,64},{128,96},{160,128},{192,160},{224,192},{256... | collective-permute-start | bytes 1572872 | tf_op jit(solution)/shard_map/ppermute | solution.py:238

commit v5 on v4

--- a/solution.py
+++ b/solution.py
@@ -129,51 +129,103 @@
     )(block)
 
 
-def scatter_kernel(part_ref, own_ref, out_ref, slots, send_sems, recv_sems):
-    count = part_ref.shape[0]
-    me, row = greet_peers(count)
-
-    def outgoing(step):
-        peer = lax.rem(me + step, count)
-        return pltpu.make_async_remote_copy(
-            part_ref.at[peer], slots.at[me], send_sems.at[step], recv_sems.at[me],
-            device_id=(row, peer), device_id_type=MESH_ID,
-        )
-
-    def incoming(step):
-        source = lax.rem(me + count - step, count)
-        return pltpu.make_async_remote_copy(
-            part_ref.at[source], slots.at[source], send_sems.at[step], recv_sems.at[source],
-            device_id=(row, source), device_id_type=MESH_ID,
-        )
-
-    def start(step, carry):
-        outgoing(step).start()
-        return carry
-
-    lax.fori_loop(1, count, start, 0)
-
-    def finish(step, total):
-        outgoing(step).wait_send()
-        incoming(step).wait_recv()
-        source = lax.rem(me + count - step, count)
-        return total + slots[source].astype(jnp.float32)
-
-    out_ref[...] = lax.fori_loop(1, count, finish, own_ref[me])
+def scatter_kernel(part_ref, own_ref, out_ref, near_slots, class_sum, far_slots,
+                   send_near, recv_near, send_far, recv_far):
+    classes, chunk = part_ref.shape[0], part_ref.shape[1]
+    me = lax.axis_index("term")
+    row = lax.axis_index("space")
+    stride, lane = me // classes, me % classes
+    barrier = pltpu.get_barrier_semaphore()
+
+    def far_peer(step):
+        return lax.rem(stride + step, chunk) * classes + lane
+
+    def near_peer(step):
+        return stride * classes + lax.rem(lane + step, classes)
+
+    def greet_far(step, carry):
+        pl.semaphore_signal(barrier, 1, device_id=(row, far_peer(step)), device_id_type=MESH_ID)
+        return carry
+
+    def greet_near(step, carry):
+        pl.semaphore_signal(barrier, 1, device_id=(row, near_peer(step)), device_id_type=MESH_ID)
+        return carry
+
+    lax.fori_loop(1, chunk, greet_far, 0)
+    lax.fori_loop(1, classes, greet_near, 0)
+    pl.semaphore_wait(barrier, chunk + classes - 2)
+
+    def near_out(step):
+        target = lax.rem(lane + step, classes)
+        return pltpu.make_async_remote_copy(
+            part_ref.at[target], near_slots.at[lane], send_near.at[step], recv_near.at[lane],
+            device_id=(row, near_peer(step)), device_id_type=MESH_ID,
+        )
+
+    def near_in(step):
+        source = lax.rem(lane + classes - step, classes)
+        return pltpu.make_async_remote_copy(
+            part_ref.at[source], near_slots.at[source], send_near.at[step], recv_near.at[source],
+            device_id=(row, stride * classes + source), device_id_type=MESH_ID,
+        )
+
+    def near_start(step, carry):
+        near_out(step).start()
+        return carry
+
+    def near_finish(step, total):
+        near_out(step).wait_send()
+        near_in(step).wait_recv()
+        source = lax.rem(lane + classes - step, classes)
+        return total + near_slots[source].astype(jnp.float32)
+
+    lax.fori_loop(1, classes, near_start, 0)
+    class_sum[...] = lax.fori_loop(1, classes, near_finish, own_ref[lane])
+
+    def far_out(step):
+        target = lax.rem(stride + step, chunk)
+        return pltpu.make_async_remote_copy(
+            class_sum.at[target], far_slots.at[stride], send_far.at[step], recv_far.at[stride],
+            device_id=(row, far_peer(step)), device_id_type=MESH_ID,
+        )
+
+    def far_in(step):
+        source = lax.rem(stride + chunk - step, chunk)
+        return pltpu.make_async_remote_copy(
+            class_sum.at[source], far_slots.at[source], send_far.at[step], recv_far.at[source],
+            device_id=(row, source * classes + lane), device_id_type=MESH_ID,
+        )
+
+    def far_start(step, carry):
+        far_out(step).start()
+        return carry
+
+    def far_finish(step, total):
+        far_out(step).wait_send()
+        far_in(step).wait_recv()
+        source = lax.rem(stride + chunk - step, chunk)
+        return total + far_slots[source]
+
+    lax.fori_loop(1, chunk, far_start, 0)
+    out_ref[...] = lax.fori_loop(1, chunk, far_finish, class_sum[stride])
 
 
 def scatter_term(parts):
-    count = parts.shape[0]
+    classes, chunk = parts.shape[0], parts.shape[1]
     sent = parts.astype(jnp.bfloat16)
     return pl.pallas_call(
         scatter_kernel,
-        out_shape=jax.ShapeDtypeStruct(parts.shape[1:], parts.dtype),
+        out_shape=jax.ShapeDtypeStruct(parts.shape[2:], parts.dtype),
         in_specs=[pl.BlockSpec(memory_space=pltpu.VMEM)] * 2,
         out_specs=pl.BlockSpec(memory_space=pltpu.VMEM),
         scratch_shapes=[
             pltpu.VMEM(sent.shape, sent.dtype),
-            pltpu.SemaphoreType.DMA((count,)),
-            pltpu.SemaphoreType.DMA((count,)),
+            pltpu.VMEM(parts.shape[1:], parts.dtype),
+            pltpu.VMEM(parts.shape[1:], parts.dtype),
+            pltpu.SemaphoreType.DMA((classes,)),
+            pltpu.SemaphoreType.DMA((classes,)),
+            pltpu.SemaphoreType.DMA((chunk,)),
+            pltpu.SemaphoreType.DMA((chunk,)),
         ],
         compiler_params=pltpu.CompilerParams(collective_id=1, has_side_effects=True),
     )(sent, parts)
@@ -259,11 +311,13 @@
     row_hot = (triple_pattern[:, :, 0:1] == levels).astype(jnp.float32)
     col_hot = (triple_pattern[:, :, 1:2] == levels).astype(jnp.float32)
     dense = jnp.einsum("kna,knb,knxy->kaxby", row_hot, col_hot, triple_blocks.astype(jnp.float32))
-    dense = dense.reshape(term_count, total_rows, groups // CLASSES, CLASSES, local_rows)
-    dense = dense.transpose(0, 1, 3, 2, 4).reshape(term_count, total_rows, total_rows)
+    order = (groups // CLASSES, CLASSES, local_rows)
+    dense = dense.reshape((term_count,) + order + order).transpose(0, 2, 1, 3, 5, 4, 6)
+    dense = dense.reshape(term_count, total_rows, total_rows)
     dense = dense.astype(jnp.bfloat16)
     partial = image_contract(stiff_offsets, extended, stiff_blocks, dense)
-    summed = scatter_term(partial.reshape(groups, local_rows, load_count * cell_count))
+    parts = partial.reshape(CLASSES, groups // CLASSES, local_rows, load_count * cell_count)
+    summed = scatter_term(parts)
     return summed.reshape(local_rows, load_count, cell_count)
 
 

time: 105 us -> 119 us (1.13)
  the two profiles are of different devices: /device:TPU:7 before, /device:TPU:56 now
where the time goes in v5:
time: 119 us; the launch traced here: 118 us
  Pallas kernels  79.7 us (67%)
  local copies, waits for them, and re-layouts  25.4 us (21%)
  starting transfers between devices  9.18 us (8%)
  other arithmetic  3.35 us (3%)
    pallas_call x1, Pallas kernels, scatter_term(): pl.pallas_call(scatter_kernel, out_shape=jax.ShapeDtypeStruct(parts.shape...  36.3 us
    pallas_call x1, Pallas kernels, gather_term(): pl.pallas_call(gather_kernel, out_shape=jax.ShapeDtypeStruct((count,) + b...  34.5 us
    convert_element_type x3, local copies, waits for them, and re-layouts, per_device(): dense = dense.astype(jnp.bfloat16)  19.9 us
    pallas_call x1, Pallas kernels, image_contract(): pl.pallas_call(image_kernel, out_shape=jax.ShapeDtypeStruct((rows, loads...  8.95 us
    ppermute x1, starting transfers between devices, with_halo(): lax.ppermute(lax.slice_in_dim(block, 0, width, axis=dim), axis, backward)  7.26 us
  transfers between devices with their start and end apart: 2, of which 0 were waited for; matrix products, arithmetic and copies ran while one was open for 18% of the time, Pallas kernels for 0%

profile of v5, /device:TPU:56, one launch (start us, length us, event | category | flops | bytes accessed | tf_op | source)
XLA Modules:
  0.0 118.1 jit_solution(9611762658415141567)
XLA Ops:
  0.0 0.0 copy-start
  0.0 1.4 %reshape.23.block_ref = bf16[16,512]{1,0:T(8,128)(2,1)} reshape(bf16[8,2,512]{2,1,0:T(2,128)(2,1)} %param.5) | data formatting | bytes 32768 | tf_op jit(solution)/shard_map/reshape | solution.py:305
  1.4 34.5 %shard_map.55 = bf16[32,16,512]{2,1,0:T(8,128)(2,1)} custom-call(bf16[16,512]{1,0:T(8,128)(2,1)} %reshape.23.block_ref), custom_call_target="tpu_custom_call" | custom-call | tf_op jit(solution)/shard_map/pallas_call | solution.py:116
  35.8 1.2 %reshape.24 = bf16[32,8,2,512]{3,2,1,0:T(2,128)(2,1)S(1)} reshape(bf16[32,16,512]{2,1,0:T(8,128)(2,1)} %shard_map.55) | data formatting | bytes 1048576 | tf_op jit(solution)/shard_map/reshape | solution.py:306
  37.1 0.1 copy.19
  37.2 1.9 %collective-permute-start = (bf16[2,256,512]{2,1,0:T(8,128)(2,1)S(1)}, bf16[2,256,512]{2,1,0:T(8,128)(2,1)S(1)}, u32[]{:S(2)}, u32[]{:S(2)}) collective-permute-start(bf16[2,256,512]{2,1,0:T(8,128)(2,1)S(1)} %bitcast.30), channel_id=1, source_target_pairs={{0,32},{32,64},{64,96},{96,128},{128,160},{160,192},{192,224},{224... | collective-permute-start | bytes 1572872 | tf_op jit(solution)/shard_map/ppermute | solution.py:287
  39.1 7.3 %collective-permute-start.1 = (bf16[2,256,512]{2,1,0:T(8,128)(2,1)S(1)}, bf16[2,256,512]{2,1,0:T(8,128)(2,1)S(1)}, u32[]{:S(2)}, u32[]{:S(2)}) collective-permute-start(bf16[2,256,512]{2,1,0:T(8,128)(2,1)S(1)} %bitcast.31), channel_id=1, source_target_pairs={{32,0},{64,32},{96,64},{128,96},{160,128},{192,160},{224,192},{256... | collective-permute-start | bytes 1572872 | tf_op jit(solution)/shard_map/ppermute | solution.py:290
  46.3 0.8 fusion.8
  47.1 0.0 copy-done
  47.1 0.4 fusion
  47.5 3.3 %convert_element_type.19 = bf16[2,8,4,8,8,4,8]{6,5,1,3,2,4,0:T(4,128)(2,1)} reshape(bf16[2,8,32,8,32]{4,1,2,3,0:T(8,128)(2,1)S(1)} %fusion) | data formatting | bytes 524288 | tf_op jit(solution)/shard_map/convert_element_type | solution.py:317
  50.8 9.1 %copy.18 = bf16[2,8,4,8,8,4,8]{6,4,5,3,1,2,0:T(8,128)(2,1)} copy(bf16[2,8,4,8,8,4,8]{6,5,1,3,2,4,0:T(4,128)(2,1)} %convert_element_type.19) | data formatting | bytes 524288 | tf_op jit(solution)/shard_map/convert_element_type | solution.py:317
  59.9 0.0 copy-start.1
  59.9 7.5 %convert_element_type.21.triple_ref = bf16[2,256,256]{2,1,0:T(8,128)(2,1)} reshape(bf16[2,4,8,8,4,8,8]{6,5,4,3,2,1,0:T(8,128)(2,1)} %bitcast.27) | data formatting | bytes 524288 | tf_op jit(solution)/shard_map/convert_element_type | solution.py:317
  67.5 0.0 copy-done.1
  67.5 0.6 reshape.22.offs_ref
  68.1 0.0 collective-permute-done
  68.1 0.0 collective-permute-done.1
  68.1 1.3 %pad_maximum_fusion.panel_ref = bf16[2,256,1536]{2,1,0:T(8,128)(2,1)} fusion(bf16[2,256,512]{2,1,0:T(8,128)(2,1)S(1)} %collective-permute-done.1, bf16[2,256,512]{2,1,0:T(8,128)(2,1)S(1)} %bitcast.32, bf16[2,256,512]{2,1,0:T(8,128)(2,1)S(1)} %collective-permute-done), kind=kLoop, calls=%fused_computation.1 | loop fusion | flops 4718592 | bytes 3145728 | tf_op jit(solution)/shard_map/concatenate | solution.py:291
  69.3 8.9 %shard_map.56 = f32[256,1024]{1,0:T(8,128)} custom-call(s32[24]{0:T(128)} %reshape.22.offs_ref, bf16[2,256,1536]{2,1,0:T(8,128)(2,1)} %pad_maximum_fusion.panel_ref, bf16[2,2,6,256,256]{4,3,2,1,0:T(8,128)(2,1)} %stiff_ref.1, bf16[2,256,256]{2,1,0:T(8,128)(2,1)} %convert_element_type.21.triple_ref), custom_call_target="tpu_custom_call" | custom-call | tf_op jit(solution)/shard_map/pallas_call | solution.py:266
  78.3 2.1 %convert_element_type.22.part_ref = bf16[4,8,8,1024]{3,2,1,0:T(8,128)(2,1)} convert(f32[4,8,8,1024]{3,2,1,0:T(8,128)} %bitcast.28) | non-fusion elementwise | flops 262144 | bytes 1572864 | tf_op jit(solution)/shard_map/convert_element_type | solution.py:215
  80.4 36.3 %shard_map.57 = f32[8,1024]{1,0:T(8,128)} custom-call(bf16[4,8,8,1024]{3,2,1,0:T(8,128)(2,1)} %convert_element_type.22.part_ref, f32[4,8,8,1024]{3,2,1,0:T(8,128)} %bitcast.29), custom_call_target="tpu_custom_call" | custom-call | tf_op jit(solution)/shard_map/pallas_call | solution.py:216
  116.7 1.4 %copy.9 = f32[8,2,512]{2,1,0:T(2,128)} copy(f32[8,2,512]{2,0,1:T(8,128)} %bitcast.33) | data formatting | bytes 65536 | tf_op jit(solution)/shard_map/reshape | solution.py:321
  (1 shorter events, 0.0 us)
Async XLA Ops:
  0.0 47.1 %copy-start = (bf16[2,24,32,32]{3,2,1,0:T(8,128)(2,1)S(1)}, bf16[2,24,32,32]{3,2,1,0:T(8,128)(2,1)}, u32[]{:S(2)}) copy-start(bf16[2,24,32,32]{3,2,1,0:T(8,128)(2,1)} %param.8) | copy-start | bytes 294916
  37.2 30.9 %collective-permute-start = (bf16[2,256,512]{2,1,0:T(8,128)(2,1)S(1)}, bf16[2,256,512]{2,1,0:T(8,128)(2,1)S(1)}, u32[]{:S(2)}, u32[]{:S(2)}) collective-permute-start(bf16[2,256,512]{2,1,0:T(8,128)(2,1)S(1)} %bitcast.30), channel_id=1, source_target_pairs={{0,32},{32,64},{64,96},{96,128},{128,160},{160,192},{192,224},{224... | collective-permute-start | bytes 1572872 | tf_op jit(solution)/shard_map/ppermute | solution.py:287
  39.1 29.0 %collective-permute-start.1 = (bf16[2,256,512]{2,1,0:T(8,128)(2,1)S(1)}, bf16[2,256,512]{2,1,0:T(8,128)(2,1)S(1)}, u32[]{:S(2)}, u32[]{:S(2)}) collective-permute-start(bf16[2,256,512]{2,1,0:T(8,128)(2,1)S(1)} %bitcast.31), channel_id=1, source_target_pairs={{32,0},{64,32},{96,64},{128,96},{160,128},{192,160},{224,192},{256... | collective-permute-start | bytes 1572872 | tf_op jit(solution)/shard_map/ppermute | solution.py:290
  59.9 7.5 %copy-start.1 = (s32[2,2,6]{2,1,0:T(2,128)S(1)}, s32[2,2,6]{2,1,0:T(2,128)}, u32[]{:S(2)}) copy-start(s32[2,2,6]{2,1,0:T(2,128)} %param.7) | copy-start | bytes 292

commit v6 on v5

--- a/solution.py
+++ b/solution.py
@@ -131,7 +131,7 @@
 
 def scatter_kernel(part_ref, own_ref, out_ref, near_slots, class_sum, far_slots,
                    send_near, recv_near, send_far, recv_far):
-    classes, chunk = part_ref.shape[0], part_ref.shape[1]
+    chunk, classes = part_ref.shape[0], part_ref.shape[1]
     me = lax.axis_index("term")
     row = lax.axis_index("space")
     stride, lane = me // classes, me % classes
@@ -158,14 +158,14 @@
     def near_out(step):
         target = lax.rem(lane + step, classes)
         return pltpu.make_async_remote_copy(
-            part_ref.at[target], near_slots.at[lane], send_near.at[step], recv_near.at[lane],
+            part_ref.at[:, target], near_slots.at[lane], send_near.at[step], recv_near.at[lane],
             device_id=(row, near_peer(step)), device_id_type=MESH_ID,
         )
 
     def near_in(step):
         source = lax.rem(lane + classes - step, classes)
         return pltpu.make_async_remote_copy(
-            part_ref.at[source], near_slots.at[source], send_near.at[step], recv_near.at[source],
+            part_ref.at[:, source], near_slots.at[source], send_near.at[step], recv_near.at[source],
             device_id=(row, stride * classes + source), device_id_type=MESH_ID,
         )
 
@@ -180,7 +180,7 @@
         return total + near_slots[source].astype(jnp.float32)
 
     lax.fori_loop(1, classes, near_start, 0)
-    class_sum[...] = lax.fori_loop(1, classes, near_finish, own_ref[lane])
+    class_sum[...] = lax.fori_loop(1, classes, near_finish, own_ref[:, lane])
 
     def far_out(step):
         target = lax.rem(stride + step, chunk)
@@ -211,7 +211,7 @@
 
 
 def scatter_term(parts):
-    classes, chunk = parts.shape[0], parts.shape[1]
+    chunk, classes = parts.shape[0], parts.shape[1]
     sent = parts.astype(jnp.bfloat16)
     return pl.pallas_call(
         scatter_kernel,
@@ -219,9 +219,9 @@
         in_specs=[pl.BlockSpec(memory_space=pltpu.VMEM)] * 2,
         out_specs=pl.BlockSpec(memory_space=pltpu.VMEM),
         scratch_shapes=[
-            pltpu.VMEM(sent.shape, sent.dtype),
-            pltpu.VMEM(parts.shape[1:], parts.dtype),
-            pltpu.VMEM(parts.shape[1:], parts.dtype),
+            pltpu.VMEM((classes, chunk) + parts.shape[2:], sent.dtype),
+            pltpu.VMEM((chunk,) + parts.shape[2:], parts.dtype),
+            pltpu.VMEM((chunk,) + parts.shape[2:], parts.dtype),
             pltpu.SemaphoreType.DMA((classes,)),
             pltpu.SemaphoreType.DMA((classes,)),
             pltpu.SemaphoreType.DMA((chunk,)),
@@ -311,12 +311,11 @@
     row_hot = (triple_pattern[:, :, 0:1] == levels).astype(jnp.float32)
     col_hot = (triple_pattern[:, :, 1:2] == levels).astype(jnp.float32)
     dense = jnp.einsum("kna,knb,knxy->kaxby", row_hot, col_hot, triple_blocks.astype(jnp.float32))
-    order = (groups // CLASSES, CLASSES, local_rows)
-    dense = dense.reshape((term_count,) + order + order).transpose(0, 2, 1, 3, 5, 4, 6)
-    dense = dense.reshape(term_count, total_rows, total_rows)
+    dense = dense.reshape(term_count, total_rows, groups // CLASSES, CLASSES, local_rows)
+    dense = dense.transpose(0, 1, 3, 2, 4).reshape(term_count, total_rows, total_rows)
     dense = dense.astype(jnp.bfloat16)
     partial = image_contract(stiff_offsets, extended, stiff_blocks, dense)
-    parts = partial.reshape(CLASSES, groups // CLASSES, local_rows, load_count * cell_count)
+    parts = partial.reshape(groups // CLASSES, CLASSES, local_rows, load_count * cell_count)
     summed = scatter_term(parts)
     return summed.reshape(local_rows, load_count, cell_count)
 

time: 119 us -> 106 us (0.89)
  the two profiles are of different devices: /device:TPU:56 before, /device:TPU:48 now
where the time goes in v6:
time: 106 us; the launch traced here: 105 us
  Pallas kernels  80.9 us (76%)
  starting transfers between devices  9.18 us (9%)
  local copies, waits for them, and re-layouts  8 us (8%)
  other arithmetic  4.39 us (4%)
  waiting for transfers between devices  2.3 us (2%)
    pallas_call x1, Pallas kernels, scatter_term(): pl.pallas_call(scatter_kernel, out_shape=jax.ShapeDtypeStruct(parts.shape...  36.8 us
    pallas_call x1, Pallas kernels, gather_term(): pl.pallas_call(gather_kernel, out_shape=jax.ShapeDtypeStruct((count,) + b...  35.2 us
    pallas_call x1, Pallas kernels, image_contract(): pl.pallas_call(image_kernel, out_shape=jax.ShapeDtypeStruct((rows, loads...  8.94 us
    ppermute x1, starting transfers between devices, with_halo(): lax.ppermute(lax.slice_in_dim(block, 0, width, axis=dim), axis, backward)  7.26 us
    convert_element_type x4, local copies, waits for them, and re-layouts, per_device(): dense = dense.astype(jnp.bfloat16)  2.55 us
    concatenate x1, other arithmetic, with_halo(): block = jnp.concatenate([low, block, high], axis=dim)  2.3 us
  transfers between devices with their start and end apart: 2, of which 2 were waited for; matrix products, arithmetic and copies ran while one was open for 4% of the time, Pallas kernels for 0%

profile of v6, /device:TPU:48, one launch (start us, length us, event | category | flops | bytes accessed | tf_op | source)
XLA Modules:
  0.0 105.3 jit_solution(7044419562267026252)
XLA Ops:
  0.0 0.0 copy-start
  0.0 1.4 %reshape.23.block_ref = bf16[16,512]{1,0:T(8,128)(2,1)} reshape(bf16[8,2,512]{2,1,0:T(2,128)(2,1)} %param.5) | data formatting | bytes 32768 | tf_op jit(solution)/shard_map/reshape | solution.py:305
  1.4 35.2 %shard_map.55 = bf16[32,16,512]{2,1,0:T(8,128)(2,1)} custom-call(bf16[16,512]{1,0:T(8,128)(2,1)} %reshape.23.block_ref), custom_call_target="tpu_custom_call" | custom-call | tf_op jit(solution)/shard_map/pallas_call | solution.py:116
  36.6 1.2 %reshape.24 = bf16[32,8,2,512]{3,2,1,0:T(2,128)(2,1)S(1)} reshape(bf16[32,16,512]{2,1,0:T(8,128)(2,1)} %shard_map.55) | data formatting | bytes 1048576 | tf_op jit(solution)/shard_map/reshape | solution.py:306
  37.8 0.1 copy.22
  37.9 0.0 copy-start.1
  37.9 1.9 %collective-permute-start = (bf16[2,256,512]{2,1,0:T(8,128)(2,1)S(1)}, bf16[2,256,512]{2,1,0:T(8,128)(2,1)S(1)}, u32[]{:S(2)}, u32[]{:S(2)}) collective-permute-start(bf16[2,256,512]{2,1,0:T(8,128)(2,1)S(1)} %bitcast.26), channel_id=1, source_target_pairs={{0,32},{32,64},{64,96},{96,128},{128,160},{160,192},{192,224},{224... | collective-permute-start | bytes 1572872 | tf_op jit(solution)/shard_map/ppermute | solution.py:287
  39.9 7.3 %collective-permute-start.1 = (bf16[2,256,512]{2,1,0:T(8,128)(2,1)S(1)}, bf16[2,256,512]{2,1,0:T(8,128)(2,1)}, u32[]{:S(2)}, u32[]{:S(2)}) collective-permute-start(bf16[2,256,512]{2,1,0:T(8,128)(2,1)S(1)} %bitcast.27), channel_id=1, source_target_pairs={{32,0},{64,32},{96,64},{128,96},{160,128},{192,160},{224,192},{256... | collective-permute-start | bytes 1572872 | tf_op jit(solution)/shard_map/ppermute | solution.py:290
  47.1 0.8 fusion.8
  47.9 0.0 copy-done
  47.9 0.4 fusion
  48.3 1.0 copy.11
  49.3 0.7 convert_element_type.19
  50.0 0.8 copy.13.triple_ref
  50.9 0.0 copy-done.1
  50.9 0.6 reshape.22.offs_ref
  51.5 0.5 collective-permute-done
  52.0 1.8 %collective-permute-done.1 = bf16[2,256,512]{2,1,0:T(8,128)(2,1)} collective-permute-done((bf16[2,256,512]{2,1,0:T(8,128)(2,1)S(1)}, bf16[2,256,512]{2,1,0:T(8,128)(2,1)}, u32[]{:S(2)}, u32[]{:S(2)}) %collective-permute-start.1) | collective-permute-done | bytes 524320 | tf_op jit(solution)/shard_map/ppermute | solution.py:290
  53.8 2.3 %pad_maximum_fusion.panel_ref = bf16[2,256,1536]{2,1,0:T(8,128)(2,1)} fusion(bf16[2,256,512]{2,1,0:T(8,128)(2,1)} %collective-permute-done.1, bf16[2,256,512]{2,1,0:T(8,128)(2,1)S(1)} %bitcast.28, bf16[2,256,512]{2,1,0:T(8,128)(2,1)S(1)} %collective-permute-done), kind=kLoop, calls=%fused_computation | loop fusion | flops 4718592 | bytes 3145728 | tf_op jit(solution)/shard_map/concatenate | solution.py:291
  56.1 8.9 %shard_map.56 = f32[256,1024]{1,0:T(8,128)} custom-call(s32[24]{0:T(128)} %reshape.22.offs_ref, bf16[2,256,1536]{2,1,0:T(8,128)(2,1)} %pad_maximum_fusion.panel_ref, bf16[2,2,6,256,256]{4,3,2,1,0:T(8,128)(2,1)} %stiff_ref.1, bf16[2,256,256]{2,1,0:T(8,128)(2,1)} %copy.13.triple_ref), custom_call_target="tpu_custom_call" | custom-call | tf_op jit(solution)/shard_map/pallas_call | solution.py:266
  65.0 2.1 %convert_element_type.22.part_ref = bf16[8,4,8,1024]{3,2,1,0:T(8,128)(2,1)} convert(f32[8,4,8,1024]{3,2,1,0:T(8,128)} %bitcast.24) | non-fusion elementwise | flops 262144 | bytes 1572864 | tf_op jit(solution)/shard_map/convert_element_type | solution.py:215
  67.1 36.8 %shard_map.57 = f32[8,1024]{1,0:T(8,128)} custom-call(bf16[8,4,8,1024]{3,2,1,0:T(8,128)(2,1)} %convert_element_type.22.part_ref, f32[8,4,8,1024]{3,2,1,0:T(8,128)} %bitcast.25), custom_call_target="tpu_custom_call" | custom-call | tf_op jit(solution)/shard_map/pallas_call | solution.py:216
  103.9 1.4 %copy.14 = f32[8,2,512]{2,1,0:T(2,128)} copy(f32[8,2,512]{2,0,1:T(8,128)} %bitcast.31) | data formatting | bytes 65536 | tf_op jit(solution)/shard_map/reshape | solution.py:320
  (2 shorter events, 0.0 us)
Async XLA Ops:
  0.0 47.9 %copy-start = (bf16[2,24,32,32]{3,2,1,0:T(8,128)(2,1)S(1)}, bf16[2,24,32,32]{3,2,1,0:T(8,128)(2,1)}, u32[]{:S(2)}) copy-start(bf16[2,24,32,32]{3,2,1,0:T(8,128)(2,1)} %param.8) | copy-start | bytes 294916
  37.9 13.0 %copy-start.1 = (s32[2,2,6]{2,1,0:T(2,128)S(1)}, s32[2,2,6]{2,1,0:T(2,128)}, u32[]{:S(2)}) copy-start(s32[2,2,6]{2,1,0:T(2,128)} %param.7) | copy-start | bytes 292
  37.9 14.1 %collective-permute-start = (bf16[2,256,512]{2,1,0:T(8,128)(2,1)S(1)}, bf16[2,256,512]{2,1,0:T(8,128)(2,1)S(1)}, u32[]{:S(2)}, u32[]{:S(2)}) collective-permute-start(bf16[2,256,512]{2,1,0:T(8,128)(2,1)S(1)} %bitcast.26), channel_id=1, source_target_pairs={{0,32},{32,64},{64,96},{96,128},{128,160},{160,192},{192,224},{224... | collective-permute-start | bytes 1572872 | tf_op jit(solution)/shard_map/ppermute | solution.py:287
  39.9 13.9 %collective-permute-start.1 = (bf16[2,256,512]{2,1,0:T(8,128)(2,1)S(1)}, bf16[2,256,512]{2,1,0:T(8,128)(2,1)}, u32[]{:S(2)}, u32[]{:S(2)}) collective-permute-start(bf16[2,256,512]{2,1,0:T(8,128)(2,1)S(1)} %bitcast.27), channel_id=1, source_target_pairs={{32,0},{64,32},{96,64},{128,96},{160,128},{192,160},{224,192},{256... | collective-permute-start | bytes 1572872 | tf_op jit(solution)/shard_map/ppermute | solution.py:290

commit v7 on v6

--- a/solution.py
+++ b/solution.py
@@ -6,21 +6,6 @@
 from jax.sharding import PartitionSpec as P
 
 MESH_ID = pl.DeviceIdType.MESH
-
-
-def greet_peers(count):
-    me = lax.axis_index("term")
-    row = lax.axis_index("space")
-    barrier = pltpu.get_barrier_semaphore()
-
-    def greet(step, carry):
-        peer = lax.rem(me + step, count)
-        pl.semaphore_signal(barrier, 1, device_id=(row, peer), device_id_type=MESH_ID)
-        return carry
-
-    lax.fori_loop(1, count, greet, 0)
-    pl.semaphore_wait(barrier, count - 1)
-    return me, row
 
 
 CLASSES = 4
@@ -129,13 +114,10 @@
     )(block)
 
 
-def scatter_kernel(part_ref, own_ref, out_ref, near_slots, class_sum, far_slots,
-                   send_near, recv_near, send_far, recv_far):
-    chunk, classes = part_ref.shape[0], part_ref.shape[1]
+def scatter_peers(chunk, classes):
     me = lax.axis_index("term")
     row = lax.axis_index("space")
     stride, lane = me // classes, me % classes
-    barrier = pltpu.get_barrier_semaphore()
 
     def far_peer(step):
         return lax.rem(stride + step, chunk) * classes + lane
@@ -143,6 +125,13 @@
     def near_peer(step):
         return stride * classes + lax.rem(lane + step, classes)
 
+    return row, stride, lane, far_peer, near_peer
+
+
+def scatter_greet(chunk, classes):
+    row, stride, lane, far_peer, near_peer = scatter_peers(chunk, classes)
+    barrier = pltpu.get_barrier_semaphore()
+
     def greet_far(step, carry):
         pl.semaphore_signal(barrier, 1, device_id=(row, far_peer(step)), device_id_type=MESH_ID)
         return carry
@@ -153,7 +142,13 @@
 
     lax.fori_loop(1, chunk, greet_far, 0)
     lax.fori_loop(1, classes, greet_near, 0)
-    pl.semaphore_wait(barrier, chunk + classes - 2)
+
+
+def scatter_stages(part_ref, own_ref, out_ref, near_slots, class_sum, far_slots,
+                   send_near, recv_near, send_far, recv_far):
+    chunk, classes = part_ref.shape[0], part_ref.shape[1]
+    row, stride, lane, far_peer, near_peer = scatter_peers(chunk, classes)
+    pl.semaphore_wait(pltpu.get_barrier_semaphore(), chunk + classes - 2)
 
     def near_out(step):
         target = lax.rem(lane + step, classes)
@@ -210,72 +205,76 @@
     out_ref[...] = lax.fori_loop(1, chunk, far_finish, class_sum[stride])
 
 
-def scatter_term(parts):
-    chunk, classes = parts.shape[0], parts.shape[1]
-    sent = parts.astype(jnp.bfloat16)
-    return pl.pallas_call(
-        scatter_kernel,
-        out_shape=jax.ShapeDtypeStruct(parts.shape[2:], parts.dtype),
-        in_specs=[pl.BlockSpec(memory_space=pltpu.VMEM)] * 2,
-        out_specs=pl.BlockSpec(memory_space=pltpu.VMEM),
-        scratch_shapes=[
-            pltpu.VMEM((classes, chunk) + parts.shape[2:], sent.dtype),
-            pltpu.VMEM((chunk,) + parts.shape[2:], parts.dtype),
-            pltpu.VMEM((chunk,) + parts.shape[2:], parts.dtype),
-            pltpu.SemaphoreType.DMA((classes,)),
-            pltpu.SemaphoreType.DMA((classes,)),
-            pltpu.SemaphoreType.DMA((chunk,)),
-            pltpu.SemaphoreType.DMA((chunk,)),
-        ],
-        compiler_params=pltpu.CompilerParams(collective_id=1, has_side_effects=True),
-    )(sent, parts)
-
-
-def image_kernel(offs_ref, panel_ref, stiff_ref, triple_ref, out_ref):
+def image_kernel(offs_ref, panel_ref, stiff_ref, triple_ref, out_ref, total_ref, sent_ref,
+                 near_slots, class_sum, far_slots, send_near, recv_near, send_far, recv_far):
     term = pl.program_id(0)
     block = pl.program_id(1)
     block_rows = pl.num_programs(1)
     band = stiff_ref.shape[2]
     width = stiff_ref.shape[-1]
-    loads, rows, span = panel_ref.shape
-    rim = (span // width - block_rows) // 2
+    chunk, classes, local_rows, columns = total_ref.shape
+    rows = panel_ref.shape[1]
+    loads = columns // (block_rows * width)
+    rim = (panel_ref.shape[0] // loads - block_rows) // 2
 
     @pl.when((term == 0) & (block == 0))
     def _():
-        out_ref[...] = jnp.zeros_like(out_ref)
+        scatter_greet(chunk, classes)
+        total_ref[...] = jnp.zeros_like(total_ref)
 
     for load in range(loads):
         total = jnp.zeros((rows, width), jnp.float32)
         for slot in range(band):
             place = block + rim + offs_ref[(term * block_rows + block) * band + slot]
-            start = pl.multiple_of(place * width, width)
             total += lax.dot_general(
-                panel_ref[load, :, pl.ds(start, width)], stiff_ref[0, 0, slot],
+                panel_ref[place * loads + load], stiff_ref[0, 0, slot],
                 (((1,), (1,)), ((), ())), preferred_element_type=jnp.float32,
             )
         image = total.astype(jnp.bfloat16)
         column = pl.multiple_of((load * block_rows + block) * width, width)
-        out_ref[:, pl.ds(column, width)] += jnp.dot(
-            triple_ref[0], image, preferred_element_type=jnp.float32
-        )
-
-
-def image_contract(offsets, panel, stiff_blocks, dense):
+        product = jnp.dot(triple_ref[0], image, preferred_element_type=jnp.float32)
+        total_ref[:, :, :, pl.ds(column, width)] += product.reshape(chunk, classes, local_rows, width)
+
+    @pl.when((term == pl.num_programs(0) - 1) & (block == block_rows - 1))
+    def _():
+        sent_ref[...] = total_ref[...].astype(sent_ref.dtype)
+        scatter_stages(sent_ref, total_ref, out_ref, near_slots, class_sum, far_slots,
+                       send_near, recv_near, send_far, recv_far)
+
+
+def image_scatter(offsets, panel, stiff_blocks, dense, local_rows):
     term_count, block_rows, band, width, _ = stiff_blocks.shape
-    loads, rows, span = panel.shape
+    places, rows, _ = panel.shape
+    loads = places // (block_rows + 4)
+    columns = loads * block_rows * width
+    classes = CLASSES
+    chunk = rows // (classes * local_rows)
+    shape = (chunk, classes, local_rows, columns)
     return pl.pallas_call(
         image_kernel,
-        out_shape=jax.ShapeDtypeStruct((rows, loads * block_rows * width), jnp.float32),
+        out_shape=jax.ShapeDtypeStruct((local_rows, columns), jnp.float32),
         grid_spec=pltpu.PrefetchScalarGridSpec(
             num_scalar_prefetch=1,
             grid=(term_count, block_rows),
             in_specs=[
-                pl.BlockSpec((loads, rows, span), lambda k, b, offs: (0, 0, 0)),
+                pl.BlockSpec((places, rows, width), lambda k, b, offs: (0, 0, 0)),
                 pl.BlockSpec((1, 1, band, width, width), lambda k, b, offs: (k, b, 0, 0, 0)),
                 pl.BlockSpec((1, rows, rows), lambda k, b, offs: (k, 0, 0)),
             ],
-            out_specs=pl.BlockSpec((rows, loads * block_rows * width), lambda k, b, offs: (0, 0)),
+            out_specs=pl.BlockSpec((local_rows, columns), lambda k, b, offs: (0, 0)),
+            scratch_shapes=[
+                pltpu.VMEM(shape, jnp.float32),
+                pltpu.VMEM(shape, jnp.bfloat16),
+                pltpu.VMEM((classes, chunk, local_rows, columns), jnp.bfloat16),
+                pltpu.VMEM((chunk, local_rows, columns), jnp.float32),
+                pltpu.VMEM((chunk, local_rows, columns), jnp.float32),
+                pltpu.SemaphoreType.DMA((classes,)),
+                pltpu.SemaphoreType.DMA((classes,)),
+                pltpu.SemaphoreType.DMA((chunk,)),
+                pltpu.SemaphoreType.DMA((chunk,)),
+            ],
         ),
+        compiler_params=pltpu.CompilerParams(collective_id=1, has_side_effects=True),
     )(offsets.reshape(-1), panel, stiff_blocks, dense)
 
 
@@ -303,9 +302,10 @@
     total_rows = local_rows * groups
     rim_cells = 2 * block_width
     gathered = gather_term(chaos_field.reshape(local_rows * load_count, cell_count))
-    panel = gathered.reshape(groups, local_rows, load_count, cell_count).transpose(2, 0, 1, 3)
-    panel = panel.reshape(load_count, total_rows, cell_count)
-    extended = with_halo(panel, (("space", 2),), rim_cells)
+    panel = gathered.reshape(groups, local_rows, load_count, block_rows, block_width)
+    panel = panel.transpose(3, 2, 0, 1, 4).reshape(block_rows, load_count, total_rows, block_width)
+    extended = with_halo(panel, (("space", 0),), rim_cells // block_width)
+    extended = extended.reshape(-1, total_rows, block_width)
     block_size = triple_blocks.shape[2]
     levels = jnp.arange(total_rows // block_size, dtype=jnp.int32)
     row_hot = (triple_pattern[:, :, 0:1] == levels).astype(jnp.float32)
@@ -314,9 +314,7 @@
     dense = dense.reshape(term_count, total_rows, groups // CLASSES, CLASSES, local_rows)
     dense = dense.transpose(0, 1, 3, 2, 4).reshape(term_count, total_rows, total_rows)
     dense = dense.astype(jnp.bfloat16)
-    partial = image_contract(stiff_offsets, extended, stiff_blocks, dense)
-    parts = partial.reshape(groups // CLASSES, CLASSES, local_rows, load_count * cell_count)
-    summed = scatter_term(parts)
+    summed = image_scatter(stiff_offsets, extended, stiff_blocks, dense, local_rows)
     return summed.reshape(local_rows, load_count, cell_count)
 
 

time: 106 us -> 95.5 us (0.901)
  the two profiles are of different devices: /device:TPU:48 before, /device:TPU:111 now
where the time goes in v7:
time: 95.5 us; the launch traced here: 95.1 us
  Pallas kernels  70 us (73%)
  waiting for transfers between devices  8.64 us (9%)
  local copies, waits for them, and re-layouts  7.19 us (8%)
  starting transfers between devices  6.33 us (7%)
  other arithmetic  2.37 us (2%)
    pallas_call x1, Pallas kernels, image_scatter(): pl.pallas_call(image_kernel, out_shape=jax.ShapeDtypeStruct((local_rows,...  36.7 us
    pallas_call x1, Pallas kernels, gather_term(): pl.pallas_call(gather_kernel, out_shape=jax.ShapeDtypeStruct((count,) + b...  33.4 us
    ppermute x1, waiting for transfers between devices, with_halo(): lax.ppermute(lax.slice_in_dim(block, 0, width, axis=dim), axis, backward)  8.12 us
    ppermute x1, starting transfers between devices, with_halo(): lax.ppermute(lax.slice_in_dim(block, block.shape[dim] - width, None, axis...  4.41 us
    convert_element_type x4, local copies, waits for them, and re-layouts, per_device(): dense = dense.astype(jnp.bfloat16)  2.54 us
    concatenate x1, other arithmetic, with_halo(): block = jnp.concatenate([low, block, high], axis=dim)  2.37 us
    ppermute x1, starting transfers between devices, with_halo(): lax.ppermute(lax.slice_in_dim(block, 0, width, axis=dim), axis, backward)  1.92 us
  transfers between devices with their start and end apart: 2, of which 2 were waited for; matrix products, arithmetic and copies ran while one was open for 4% of the time, Pallas kernels for 0%

profile of v7, /device:TPU:111, one launch (start us, length us, event | category | flops | bytes accessed | tf_op | source)
XLA Modules:
  0.0 95.1 jit_solution(12511299301459140938)
XLA Ops:
  0.0 0.0 copy-start
  0.0 0.0 copy-start.2
  0.0 1.4 %reshape.23.block_ref = bf16[16,512]{1,0:T(8,128)(2,1)} reshape(bf16[8,2,512]{2,1,0:T(2,128)(2,1)} %param.5) | data formatting | bytes 32768 | tf_op jit(solution)/shard_map/reshape | solution.py:304
  1.4 33.4 %shard_map.55 = bf16[32,16,512]{2,1,0:T(8,128)(2,1)} custom-call(bf16[16,512]{1,0:T(8,128)(2,1)} %reshape.23.block_ref), custom_call_target="tpu_custom_call" | custom-call | tf_op jit(solution)/shard_map/pallas_call | solution.py:101
  34.8 1.2 %reshape.24 = bf16[32,8,2,2,256]{4,3,2,1,0:T(2,128)(2,1)S(1)} reshape(bf16[32,16,512]{2,1,0:T(8,128)(2,1)} %shard_map.55) | data formatting | bytes 1048576 | tf_op jit(solution)/shard_map/reshape | solution.py:305
  36.0 0.1 copy.22
  36.0 4.4 %collective-permute-start = (bf16[2,2,256,256]{3,2,1,0:T(8,128)(2,1)S(1)}, bf16[2,2,256,256]{3,2,1,0:T(8,128)(2,1)S(1)}, u32[]{:S(2)}, u32[]{:S(2)}) collective-permute-start(bf16[2,2,256,256]{3,2,1,0:T(8,128)(2,1)S(1)} %bitcast.25), channel_id=1, source_target_pairs={{0,32},{32,64},{64,96},{96,128},{128,160},{160,192},{192,224},{224... | collective-permute-start | bytes 1572872 | tf_op jit(solution)/shard_map/ppermute | solution.py:286
  40.5 1.9 %collective-permute-start.1 = (bf16[2,2,256,256]{3,2,1,0:T(8,128)(2,1)S(1)}, bf16[2,2,256,256]{3,2,1,0:T(8,128)(2,1)}, u32[]{:S(2)}, u32[]{:S(2)}) collective-permute-start(bf16[2,2,256,256]{3,2,1,0:T(8,128)(2,1)S(1)} %bitcast.26), channel_id=1, source_target_pairs={{32,0},{64,32},{96,64},{128,96},{160,128},{192,160},{224,192},{256... | collective-permute-start | bytes 1572872 | tf_op jit(solution)/shard_map/ppermute | solution.py:289
  42.4 0.0 copy-done.2
  42.4 0.0 copy-done
  42.4 0.4 fusion
  42.9 1.0 %copy.11 = bf16[2,8,32,8,32]{2,1,4,3,0:T(8,128)(2,1)S(1)} copy(bf16[2,8,32,8,32]{4,1,2,3,0:T(8,128)(2,1)S(1)} %fusion) | data formatting | bytes 524288 | tf_op jit(solution)/shard_map/convert_element_type | solution.py:316
  43.9 0.0 copy-start.1
  43.9 0.7 convert_element_type.16
  44.6 0.8 copy.13.triple_ref
  45.4 0.0 copy-done.1
  45.4 0.6 reshape.22.offs_ref
  46.0 0.5 collective-permute-done
  46.6 8.1 %collective-permute-done.1 = bf16[2,2,256,256]{3,2,1,0:T(8,128)(2,1)} collective-permute-done((bf16[2,2,256,256]{3,2,1,0:T(8,128)(2,1)S(1)}, bf16[2,2,256,256]{3,2,1,0:T(8,128)(2,1)}, u32[]{:S(2)}, u32[]{:S(2)}) %collective-permute-start.1) | collective-permute-done | bytes 524320 | tf_op jit(solution)/shard_map/ppermute | solution.py:289
  54.7 2.4 %pad_maximum_fusion = bf16[6,2,256,256]{3,2,1,0:T(8,128)(2,1)} fusion(bf16[2,2,256,256]{3,2,1,0:T(8,128)(2,1)} %collective-permute-done.1, bf16[2,2,256,256]{3,2,1,0:T(8,128)(2,1)S(1)} %bitcast.27, bf16[2,2,256,256]{3,2,1,0:T(8,128)(2,1)S(1)} %collective-permute-done), kind=kLoop, calls=%fused_computation | loop fusion | flops 1572864 | bytes 3145728 | tf_op jit(solution)/shard_map/concatenate | solution.py:290
  57.0 36.7 %shard_map.56 = f32[8,1024]{1,0:T(8,128)} custom-call(s32[24]{0:T(128)} %reshape.22.offs_ref, bf16[12,256,256]{2,1,0:T(8,128)(2,1)} %bitcast.23, bf16[2,2,6,256,256]{4,3,2,1,0:T(8,128)(2,1)} %stiff_ref.1, bf16[2,256,256]{2,1,0:T(8,128)(2,1)} %copy.13.triple_ref), custom_call_target="tpu_custom_call" | custom-call | tf_op jit(solution)/shard_map/pallas_call | solution.py:253
  93.7 1.4 %copy.14 = f32[8,2,512]{2,1,0:T(2,128)} copy(f32[8,2,512]{2,0,1:T(8,128)} %bitcast.30) | data formatting | bytes 65536 | tf_op jit(solution)/shard_map/reshape | solution.py:318
  (3 shorter events, 0.0 us)
Async XLA Ops:
  0.0 42.4 %copy-start = (bf16[2,24,32,32]{3,2,1,0:T(8,128)(2,1)S(1)}, bf16[2,24,32,32]{3,2,1,0:T(8,128)(2,1)}, u32[]{:S(2)}) copy-start(bf16[2,24,32,32]{3,2,1,0:T(8,128)(2,1)} %param.8) | copy-start | bytes 294916
  0.0 42.4 %copy-start.2 = (s32[2,24,2]{1,2,0:T(2,128)S(1)}, s32[2,24,2]{1,2,0:T(2,128)}, u32[]{:S(2)}) copy-start(s32[2,24,2]{1,2,0:T(2,128)} %param.9) | copy-start | bytes 1156
  36.0 10.5 %collective-permute-start = (bf16[2,2,256,256]{3,2,1,0:T(8,128)(2,1)S(1)}, bf16[2,2,256,256]{3,2,1,0:T(8,128)(2,1)S(1)}, u32[]{:S(2)}, u32[]{:S(2)}) collective-permute-start(bf16[2,2,256,256]{3,2,1,0:T(8,128)(2,1)S(1)} %bitcast.25), channel_id=1, source_target_pairs={{0,32},{32,64},{64,96},{96,128},{128,160},{160,192},{192,224},{224... | collective-permute-start | bytes 1572872 | tf_op jit(solution)/shard_map/ppermute | solution.py:286
  40.5 14.2 %collective-permute-start.1 = (bf16[2,2,256,256]{3,2,1,0:T(8,128)(2,1)S(1)}, bf16[2,2,256,256]{3,2,1,0:T(8,128)(2,1)}, u32[]{:S(2)}, u32[]{:S(2)}) collective-permute-start(bf16[2,2,256,256]{3,2,1,0:T(8,128)(2,1)S(1)} %bitcast.26), channel_id=1, source_target_pairs={{32,0},{64,32},{96,64},{128,96},{160,128},{192,160},{224,192},{256... | collective-permute-start | bytes 1572872 | tf_op jit(solution)/shard_map/ppermute | solution.py:289
  43.9 1.6 %copy-start.1 = (s32[2,2,6]{2,1,0:T(2,128)S(1)}, s32[2,2,6]{2,1,0:T(2,128)}, u32[]{:S(2)}) copy-start(s32[2,2,6]{2,1,0:T(2,128)} %param.7) | copy-start | bytes 292

commit v8 on v7

--- a/solution.py
+++ b/solution.py
@@ -213,26 +213,28 @@
     band = stiff_ref.shape[2]
     width = stiff_ref.shape[-1]
     chunk, classes, local_rows, columns = total_ref.shape
-    rows = panel_ref.shape[1]
-    loads = columns // (block_rows * width)
-    rim = (panel_ref.shape[0] // loads - block_rows) // 2
+    rows = triple_ref.shape[1]
+    loads = panel_ref.shape[1] // rows
+    rim = (panel_ref.shape[0] - block_rows) // 2
 
     @pl.when((term == 0) & (block == 0))
     def _():
         scatter_greet(chunk, classes)
         total_ref[...] = jnp.zeros_like(total_ref)
 
+    total = jnp.zeros((loads * rows, width), jnp.float32)
+    for slot in range(band):
+        place = block + rim + offs_ref[(term * block_rows + block) * band + slot]
+        total += lax.dot_general(
+            panel_ref[place], stiff_ref[0, 0, slot],
+            (((1,), (1,)), ((), ())), preferred_element_type=jnp.float32,
+        )
+    image = total.astype(jnp.bfloat16)
     for load in range(loads):
-        total = jnp.zeros((rows, width), jnp.float32)
-        for slot in range(band):
-            place = block + rim + offs_ref[(term * block_rows + block) * band + slot]
-            total += lax.dot_general(
-                panel_ref[place * loads + load], stiff_ref[0, 0, slot],
-                (((1,), (1,)), ((), ())), preferred_element_type=jnp.float32,
-            )
-        image = total.astype(jnp.bfloat16)
         column = pl.multiple_of((load * block_rows + block) * width, width)
-        product = jnp.dot(triple_ref[0], image, preferred_element_type=jnp.float32)
+        product = jnp.dot(
+            triple_ref[0], image[load * rows:(load + 1) * rows], preferred_element_type=jnp.float32
+        )
         total_ref[:, :, :, pl.ds(column, width)] += product.reshape(chunk, classes, local_rows, width)
 
     @pl.when((term == pl.num_programs(0) - 1) & (block == block_rows - 1))
@@ -244,9 +246,9 @@
 
 def image_scatter(offsets, panel, stiff_blocks, dense, local_rows):
     term_count, block_rows, band, width, _ = stiff_blocks.shape
-    places, rows, _ = panel.shape
-    loads = places // (block_rows + 4)
-    columns = loads * block_rows * width
+    places, stacked, _ = panel.shape
+    rows = dense.shape[1]
+    columns = stacked // rows * block_rows * width
     classes = CLASSES
     chunk = rows // (classes * local_rows)
     shape = (chunk, classes, local_rows, columns)
@@ -257,7 +259,7 @@
             num_scalar_prefetch=1,
             grid=(term_count, block_rows),
             in_specs=[
-                pl.BlockSpec((places, rows, width), lambda k, b, offs: (0, 0, 0)),
+                pl.BlockSpec((places, stacked, width), lambda k, b, offs: (0, 0, 0)),
                 pl.BlockSpec((1, 1, band, width, width), lambda k, b, offs: (k, b, 0, 0, 0)),
                 pl.BlockSpec((1, rows, rows), lambda k, b, offs: (k, 0, 0)),
             ],
@@ -305,7 +307,7 @@
     panel = gathered.reshape(groups, local_rows, load_count, block_rows, block_width)
     panel = panel.transpose(3, 2, 0, 1, 4).reshape(block_rows, load_count, total_rows, block_width)
     extended = with_halo(panel, (("space", 0),), rim_cells // block_width)
-    extended = extended.reshape(-1, total_rows, block_width)
+    extended = extended.reshape(block_rows + 4, load_count * total_rows, block_width)
     block_size = triple_blocks.shape[2]
     levels = jnp.arange(total_rows // block_size, dtype=jnp.int32)
     row_hot = (triple_pattern[:, :, 0:1] == levels).astype(jnp.float32)

time: 95.5 us -> 95.1 us (level)
  the two profiles are of different devices: /device:TPU:111 before, /device:TPU:48 now
where the time goes in v8:
time: 95.1 us; the launch traced here: 94.6 us
  Pallas kernels  72.3 us (76%)
  starting transfers between devices  9.18 us (10%)
  local copies, waits for them, and re-layouts  7.19 us (8%)
  waiting for transfers between devices  3.03 us (3%)
  other arithmetic  2.37 us (2%)
    pallas_call x1, Pallas kernels, image_scatter(): pl.pallas_call(image_kernel, out_shape=jax.ShapeDtypeStruct((local_rows,...  37.1 us
    pallas_call x1, Pallas kernels, gather_term(): pl.pallas_call(gather_kernel, out_shape=jax.ShapeDtypeStruct((count,) + b...  35.2 us
    ppermute x1, starting transfers between devices, with_halo(): lax.ppermute(lax.slice_in_dim(block, 0, width, axis=dim), axis, backward)  7.26 us
    convert_element_type x4, local copies, waits for them, and re-layouts, per_device(): dense = dense.astype(jnp.bfloat16)  2.54 us
    concatenate x1, other arithmetic, with_halo(): block = jnp.concatenate([low, block, high], axis=dim)  2.36 us
    ppermute x1, starting transfers between devices, with_halo(): lax.ppermute(lax.slice_in_dim(block, block.shape[dim] - width, None, axis...  1.92 us
  transfers between devices with their start and end apart: 2, of which 2 were waited for; matrix products, arithmetic and copies ran while one was open for 4% of the time, Pallas kernels for 0%

profile of v8, /device:TPU:48, one launch (start us, length us, event | category | flops | bytes accessed | tf_op | source)
XLA Modules:
  0.0 94.6 jit_solution(6510704318640863562)
XLA Ops:
  0.0 0.0 copy-start
  0.0 0.0 copy-start.2
  0.0 1.4 %reshape.25.block_ref = bf16[16,512]{1,0:T(8,128)(2,1)} reshape(bf16[8,2,512]{2,1,0:T(2,128)(2,1)} %param.5) | data formatting | bytes 32768 | tf_op jit(solution)/shard_map/reshape | solution.py:306
  1.4 35.2 %shard_map.55 = bf16[32,16,512]{2,1,0:T(8,128)(2,1)} custom-call(bf16[16,512]{1,0:T(8,128)(2,1)} %reshape.25.block_ref), custom_call_target="tpu_custom_call" | custom-call | tf_op jit(solution)/shard_map/pallas_call | solution.py:101
  36.6 1.2 %reshape.26 = bf16[32,8,2,2,256]{4,3,2,1,0:T(2,128)(2,1)S(1)} reshape(bf16[32,16,512]{2,1,0:T(8,128)(2,1)} %shard_map.55) | data formatting | bytes 1048576 | tf_op jit(solution)/shard_map/reshape | solution.py:307
  37.8 0.1 copy.23
  37.9 1.9 %collective-permute-start = (bf16[2,2,256,256]{3,2,1,0:T(8,128)(2,1)S(1)}, bf16[2,2,256,256]{3,2,1,0:T(8,128)(2,1)S(1)}, u32[]{:S(2)}, u32[]{:S(2)}) collective-permute-start(bf16[2,2,256,256]{3,2,1,0:T(8,128)(2,1)S(1)} %bitcast.26), channel_id=1, source_target_pairs={{0,32},{32,64},{64,96},{96,128},{128,160},{160,192},{192,224},{224... | collective-permute-start | bytes 1572872 | tf_op jit(solution)/shard_map/ppermute | solution.py:288
  39.8 7.3 %collective-permute-start.1 = (bf16[2,2,256,256]{3,2,1,0:T(8,128)(2,1)S(1)}, bf16[2,2,256,256]{3,2,1,0:T(8,128)(2,1)}, u32[]{:S(2)}, u32[]{:S(2)}) collective-permute-start(bf16[2,2,256,256]{3,2,1,0:T(8,128)(2,1)S(1)} %bitcast.27), channel_id=1, source_target_pairs={{32,0},{64,32},{96,64},{128,96},{160,128},{192,160},{224,192},{256... | collective-permute-start | bytes 1572872 | tf_op jit(solution)/shard_map/ppermute | solution.py:291
  47.1 0.0 copy-done.2
  47.1 0.0 copy-done
  47.1 0.4 fusion
  47.5 1.0 %copy.11 = bf16[2,8,32,8,32]{2,1,4,3,0:T(8,128)(2,1)S(1)} copy(bf16[2,8,32,8,32]{4,1,2,3,0:T(8,128)(2,1)S(1)} %fusion) | data formatting | bytes 524288 | tf_op jit(solution)/shard_map/convert_element_type | solution.py:318
  48.5 0.0 copy-start.1
  48.5 0.7 convert_element_type.16
  49.3 0.8 copy.13.triple_ref
  50.1 0.0 copy-done.1
  50.1 0.6 reshape.24.offs_ref
  50.7 1.3 %collective-permute-done = bf16[2,2,256,256]{3,2,1,0:T(8,128)(2,1)S(1)} collective-permute-done((bf16[2,2,256,256]{3,2,1,0:T(8,128)(2,1)S(1)}, bf16[2,2,256,256]{3,2,1,0:T(8,128)(2,1)S(1)}, u32[]{:S(2)}, u32[]{:S(2)}) %collective-permute-start) | collective-permute-done | bytes 524320 | tf_op jit(solution)/shard_map/ppermute | solution.py:288
  52.0 1.8 %collective-permute-done.1 = bf16[2,2,256,256]{3,2,1,0:T(8,128)(2,1)} collective-permute-done((bf16[2,2,256,256]{3,2,1,0:T(8,128)(2,1)S(1)}, bf16[2,2,256,256]{3,2,1,0:T(8,128)(2,1)}, u32[]{:S(2)}, u32[]{:S(2)}) %collective-permute-start.1) | collective-permute-done | bytes 524320 | tf_op jit(solution)/shard_map/ppermute | solution.py:291
  53.7 2.4 %pad_maximum_fusion.panel_ref = bf16[6,512,256]{2,1,0:T(8,128)(2,1)} fusion(bf16[2,512,256]{2,1,0:T(8,128)(2,1)} %bitcast.5, bf16[2,512,256]{2,1,0:T(8,128)(2,1)S(1)} %bitcast.28, bf16[2,512,256]{2,1,0:T(8,128)(2,1)S(1)} %bitcast.31), kind=kLoop, calls=%fused_computation | loop fusion | flops 1572864 | bytes 3145728 | tf_op jit(solution)/shard_map/concatenate | solution.py:292
  56.1 37.1 %shard_map.56 = f32[8,1024]{1,0:T(8,128)} custom-call(s32[24]{0:T(128)} %reshape.24.offs_ref, bf16[6,512,256]{2,1,0:T(8,128)(2,1)} %pad_maximum_fusion.panel_ref, bf16[2,2,6,256,256]{4,3,2,1,0:T(8,128)(2,1)} %stiff_ref.1, bf16[2,256,256]{2,1,0:T(8,128)(2,1)} %copy.13.triple_ref), custom_call_target="tpu_custom_call" | custom-call | tf_op jit(solution)/shard_map/pallas_call | solution.py:255
  93.2 1.4 %copy.14 = f32[8,2,512]{2,1,0:T(2,128)} copy(f32[8,2,512]{2,0,1:T(8,128)} %bitcast.32) | data formatting | bytes 65536 | tf_op jit(solution)/shard_map/reshape | solution.py:320
  (3 shorter events, 0.0 us)
Async XLA Ops:
  0.0 47.1 %copy-start = (bf16[2,24,32,32]{3,2,1,0:T(8,128)(2,1)S(1)}, bf16[2,24,32,32]{3,2,1,0:T(8,128)(2,1)}, u32[]{:S(2)}) copy-start(bf16[2,24,32,32]{3,2,1,0:T(8,128)(2,1)} %param.8) | copy-start | bytes 294916
  0.0 47.1 %copy-start.2 = (s32[2,24,2]{1,2,0:T(2,128)S(1)}, s32[2,24,2]{1,2,0:T(2,128)}, u32[]{:S(2)}) copy-start(s32[2,24,2]{1,2,0:T(2,128)} %param.9) | copy-start | bytes 1156
  37.9 14.1 %collective-permute-start = (bf16[2,2,256,256]{3,2,1,0:T(8,128)(2,1)S(1)}, bf16[2,2,256,256]{3,2,1,0:T(8,128)(2,1)S(1)}, u32[]{:S(2)}, u32[]{:S(2)}) collective-permute-start(bf16[2,2,256,256]{3,2,1,0:T(8,128)(2,1)S(1)} %bitcast.26), channel_id=1, source_target_pairs={{0,32},{32,64},{64,96},{96,128},{128,160},{160,192},{192,224},{224... | collective-permute-start | bytes 1572872 | tf_op jit(solution)/shard_map/ppermute | solution.py:288
  39.8 13.9 %collective-permute-start.1 = (bf16[2,2,256,256]{3,2,1,0:T(8,128)(2,1)S(1)}, bf16[2,2,256,256]{3,2,1,0:T(8,128)(2,1)}, u32[]{:S(2)}, u32[]{:S(2)}) collective-permute-start(bf16[2,2,256,256]{3,2,1,0:T(8,128)(2,1)S(1)} %bitcast.27), channel_id=1, source_target_pairs={{32,0},{64,32},{96,64},{128,96},{160,128},{192,160},{224,192},{256... | collective-permute-start | bytes 1572872 | tf_op jit(solution)/shard_map/ppermute | solution.py:291
  48.5 1.6 %copy-start.1 = (s32[2,2,6]{2,1,0:T(2,128)S(1)}, s32[2,2,6]{2,1,0:T(2,128)}, u32[]{:S(2)}) copy-start(s32[2,2,6]{2,1,0:T(2,128)} %param.7) | copy-start | bytes 292

commit v9 on v8

--- a/solution.py
+++ b/solution.py
@@ -9,21 +9,14 @@
 
 
 CLASSES = 4
+PAIR = 2
 
 
 def gather_kernel(block_ref, out_ref, local_sem, send_near, recv_near, send_far, recv_far):
     count = out_ref.shape[0]
     chunk = count // CLASSES
-    me = lax.axis_index("term")
-    row = lax.axis_index("space")
-    stride, lane = me // CLASSES, me % CLASSES
+    row, stride, lane, far_peer, near_peer = scatter_peers(chunk, CLASSES)
     barrier = pltpu.get_barrier_semaphore()
-
-    def far_peer(step):
-        return lax.rem(stride + step, chunk) * CLASSES + lane
-
-    def near_peer(step):
-        return stride * CLASSES + lax.rem(lane + step, CLASSES)
 
     def greet_far(step, carry):
         pl.semaphore_signal(barrier, 1, device_id=(row, far_peer(step)), device_id_type=MESH_ID)
@@ -51,7 +44,7 @@
         source = lax.rem(stride + chunk - step, chunk)
         return pltpu.make_async_remote_copy(
             block_ref, out_ref.at[lane * chunk + source], send_far.at[step], recv_far.at[source],
-            device_id=(row, source * CLASSES + lane), device_id_type=MESH_ID,
+            device_id=(row, term_device(lane, source, chunk)), device_id_type=MESH_ID,
         )
 
     def far_start(step, carry):
@@ -80,7 +73,7 @@
         theirs = out_ref.at[pl.ds(source * chunk, chunk)]
         return pltpu.make_async_remote_copy(
             theirs, theirs, send_near.at[step], recv_near.at[source],
-            device_id=(row, stride * CLASSES + source), device_id_type=MESH_ID,
+            device_id=(row, term_device(source, stride, chunk)), device_id_type=MESH_ID,
         )
 
     def near_start(step, carry):
@@ -114,16 +107,22 @@
     )(block)
 
 
+def term_device(lane, stride, chunk):
+    return (lane // PAIR) * (chunk * PAIR) + stride * PAIR + lane % PAIR
+
+
 def scatter_peers(chunk, classes):
     me = lax.axis_index("term")
     row = lax.axis_index("space")
-    stride, lane = me // classes, me % classes
+    ring = chunk * PAIR
+    stride = lax.rem(me, ring) // PAIR
+    lane = (me // ring) * PAIR + lax.rem(me, PAIR)
 
     def far_peer(step):
-        return lax.rem(stride + step, chunk) * classes + lane
+        return term_device(lane, lax.rem(stride + step, chunk), chunk)
 
     def near_peer(step):
-        return stride * classes + lax.rem(lane + step, classes)
+        return term_device(lax.rem(lane + step, classes), stride, chunk)
 
     return row, stride, lane, far_peer, near_peer
 
@@ -146,22 +145,24 @@
 
 def scatter_stages(part_ref, own_ref, out_ref, near_slots, class_sum, far_slots,
                    send_near, recv_near, send_far, recv_far):
-    chunk, classes = part_ref.shape[0], part_ref.shape[1]
+    chunk, classes = part_ref.shape[1], part_ref.shape[0] * part_ref.shape[2]
     row, stride, lane, far_peer, near_peer = scatter_peers(chunk, classes)
     pl.semaphore_wait(pltpu.get_barrier_semaphore(), chunk + classes - 2)
 
     def near_out(step):
         target = lax.rem(lane + step, classes)
         return pltpu.make_async_remote_copy(
-            part_ref.at[:, target], near_slots.at[lane], send_near.at[step], recv_near.at[lane],
+            part_ref.at[target // PAIR, :, target % PAIR], near_slots.at[lane], send_near.at[step],
+            recv_near.at[lane],
             device_id=(row, near_peer(step)), device_id_type=MESH_ID,
         )
 
     def near_in(step):
         source = lax.rem(lane + classes - step, classes)
         return pltpu.make_async_remote_copy(
-            part_ref.at[:, source], near_slots.at[source], send_near.at[step], recv_near.at[source],
-            device_id=(row, stride * classes + source), device_id_type=MESH_ID,
+            part_ref.at[source // PAIR, :, source % PAIR], near_slots.at[source], send_near.at[step],
+            recv_near.at[source],
+            device_id=(row, term_device(source, stride, chunk)), device_id_type=MESH_ID,
         )
 
     def near_start(step, carry):
@@ -175,7 +176,7 @@
         return total + near_slots[source].astype(jnp.float32)
 
     lax.fori_loop(1, classes, near_start, 0)
-    class_sum[...] = lax.fori_loop(1, classes, near_finish, own_ref[:, lane])
+    class_sum[...] = lax.fori_loop(1, classes, near_finish, own_ref[lane // PAIR, :, lane % PAIR])
 
     def far_out(step):
         target = lax.rem(stride + step, chunk)
@@ -188,7 +189,7 @@
         source = lax.rem(stride + chunk - step, chunk)
         return pltpu.make_async_remote_copy(
             class_sum.at[source], far_slots.at[source], send_far.at[step], recv_far.at[source],
-            device_id=(row, source * classes + lane), device_id_type=MESH_ID,
+            device_id=(row, term_device(lane, source, chunk)), device_id_type=MESH_ID,
         )
 
     def far_start(step, carry):
@@ -212,7 +213,8 @@
     block_rows = pl.num_programs(1)
     band = stiff_ref.shape[2]
     width = stiff_ref.shape[-1]
-    chunk, classes, local_rows, columns = total_ref.shape
+    sides, chunk, _, local_rows, columns = total_ref.shape
+    classes = sides * PAIR
     rows = triple_ref.shape[1]
     loads = panel_ref.shape[1] // rows
     rim = (panel_ref.shape[0] - block_rows) // 2
@@ -235,7 +237,9 @@
         product = jnp.dot(
             triple_ref[0], image[load * rows:(load + 1) * rows], preferred_element_type=jnp.float32
         )
-        total_ref[:, :, :, pl.ds(column, width)] += product.reshape(chunk, classes, local_rows, width)
+        total_ref[:, :, :, :, pl.ds(column, width)] += product.reshape(
+            sides, chunk, PAIR, local_rows, width
+        )
 
     @pl.when((term == pl.num_programs(0) - 1) & (block == block_rows - 1))
     def _():
@@ -251,7 +255,7 @@
     columns = stacked // rows * block_rows * width
     classes = CLASSES
     chunk = rows // (classes * local_rows)
-    shape = (chunk, classes, local_rows, columns)
+    shape = (classes // PAIR, chunk, PAIR, local_rows, columns)
     return pl.pallas_call(
         image_kernel,
         out_shape=jax.ShapeDtypeStruct((local_rows, columns), jnp.float32),
@@ -313,8 +317,8 @@
     row_hot = (triple_pattern[:, :, 0:1] == levels).astype(jnp.float32)
     col_hot = (triple_pattern[:, :, 1:2] == levels).astype(jnp.float32)
     dense = jnp.einsum("kna,knb,knxy->kaxby", row_hot, col_hot, triple_blocks.astype(jnp.float32))
-    dense = dense.reshape(term_count, total_rows, groups // CLASSES, CLASSES, local_rows)
-    dense = dense.transpose(0, 1, 3, 2, 4).reshape(term_count, total_rows, total_rows)
+    dense = dense.reshape(term_count, total_rows, CLASSES // PAIR, groups // CLASSES, PAIR, local_rows)
+    dense = dense.transpose(0, 1, 2, 4, 3, 5).reshape(term_count, total_rows, total_rows)
     dense = dense.astype(jnp.bfloat16)
     summed = image_scatter(stiff_offsets, extended, stiff_blocks, dense, local_rows)
     return summed.reshape(local_rows, load_count, cell_count)

time: 95.1 us -> 86.6 us (0.911)
  the two profiles are of different devices: /device:TPU:48 before, /device:TPU:7 now
where the time goes in v9:
time: 86.6 us; the launch traced here: 85.8 us
  Pallas kernels  57.7 us (67%)
  starting transfers between devices  9.3 us (11%)
  waiting for transfers between devices  8.64 us (10%)
  local copies, waits for them, and re-layouts  7.19 us (8%)
  other arithmetic  2.37 us (3%)
    pallas_call x1, Pallas kernels, image_scatter(): pl.pallas_call(image_kernel, out_shape=jax.ShapeDtypeStruct((local_rows,...  29.7 us
    pallas_call x1, Pallas kernels, gather_term(): pl.pallas_call(gather_kernel, out_shape=jax.ShapeDtypeStruct((count,) + b...  28.1 us
    ppermute x1, waiting for transfers between devices, with_halo(): lax.ppermute(lax.slice_in_dim(block, 0, width, axis=dim), axis, backward)  8.12 us
    ppermute x1, starting transfers between devices, with_halo(): lax.ppermute(lax.slice_in_dim(block, block.shape[dim] - width, None, axis...  7.38 us
    convert_element_type x4, local copies, waits for them, and re-layouts, per_device(): dense = dense.astype(jnp.bfloat16)  2.54 us
    concatenate x1, other arithmetic, with_halo(): block = jnp.concatenate([low, block, high], axis=dim)  2.37 us
    ppermute x1, starting transfers between devices, with_halo(): lax.ppermute(lax.slice_in_dim(block, 0, width, axis=dim), axis, backward)  1.92 us
  transfers between devices with their start and end apart: 2, of which 2 were waited for; matrix products, arithmetic and copies ran while one was open for 4% of the time, Pallas kernels for 0%

profile of v9, /device:TPU:7, one launch (start us, length us, event | category | flops | bytes accessed | tf_op | source)
XLA Modules:
  0.0 85.8 jit_solution(2063178206570449649)
XLA Ops:
  0.0 0.0 copy-start
  0.0 0.0 copy-start.2
  0.0 1.4 %reshape.25.block_ref = bf16[16,512]{1,0:T(8,128)(2,1)} reshape(bf16[8,2,512]{2,1,0:T(2,128)(2,1)} %param.5) | data formatting | bytes 32768 | tf_op jit(solution)/shard_map/reshape | solution.py:310
  1.4 28.1 %shard_map.55 = bf16[32,16,512]{2,1,0:T(8,128)(2,1)} custom-call(bf16[16,512]{1,0:T(8,128)(2,1)} %reshape.25.block_ref), custom_call_target="tpu_custom_call" | custom-call | tf_op jit(solution)/shard_map/pallas_call | solution.py:94
  29.5 1.2 %reshape.26 = bf16[32,8,2,2,256]{4,3,2,1,0:T(2,128)(2,1)S(1)} reshape(bf16[32,16,512]{2,1,0:T(8,128)(2,1)} %shard_map.55) | data formatting | bytes 1048576 | tf_op jit(solution)/shard_map/reshape | solution.py:311
  30.7 0.1 copy.23
  30.7 7.4 %collective-permute-start = (bf16[2,2,256,256]{3,2,1,0:T(8,128)(2,1)S(1)}, bf16[2,2,256,256]{3,2,1,0:T(8,128)(2,1)S(1)}, u32[]{:S(2)}, u32[]{:S(2)}) collective-permute-start(bf16[2,2,256,256]{3,2,1,0:T(8,128)(2,1)S(1)} %bitcast.26), channel_id=1, source_target_pairs={{0,32},{32,64},{64,96},{96,128},{128,160},{160,192},{192,224},{224... | collective-permute-start | bytes 1572872 | tf_op jit(solution)/shard_map/ppermute | solution.py:292
  38.1 1.9 %collective-permute-start.1 = (bf16[2,2,256,256]{3,2,1,0:T(8,128)(2,1)S(1)}, bf16[2,2,256,256]{3,2,1,0:T(8,128)(2,1)}, u32[]{:S(2)}, u32[]{:S(2)}) collective-permute-start(bf16[2,2,256,256]{3,2,1,0:T(8,128)(2,1)S(1)} %bitcast.27), channel_id=1, source_target_pairs={{32,0},{64,32},{96,64},{128,96},{160,128},{192,160},{224,192},{256... | collective-permute-start | bytes 1572872 | tf_op jit(solution)/shard_map/ppermute | solution.py:295
  40.0 0.0 copy-done.2
  40.1 0.0 copy-done
  40.1 0.4 fusion
  40.5 1.0 %copy.11 = bf16[2,8,32,8,32]{2,1,4,3,0:T(8,128)(2,1)S(1)} copy(bf16[2,8,32,8,32]{4,1,2,3,0:T(8,128)(2,1)S(1)} %fusion) | data formatting | bytes 524288 | tf_op jit(solution)/shard_map/convert_element_type | solution.py:322
  41.5 0.0 copy-start.1
  41.5 0.7 convert_element_type.16
  42.3 0.8 copy.13.triple_ref
  43.1 0.0 copy-done.1
  43.1 0.6 reshape.24.offs_ref
  43.7 0.5 collective-permute-done
  44.2 8.1 %collective-permute-done.1 = bf16[2,2,256,256]{3,2,1,0:T(8,128)(2,1)} collective-permute-done((bf16[2,2,256,256]{3,2,1,0:T(8,128)(2,1)S(1)}, bf16[2,2,256,256]{3,2,1,0:T(8,128)(2,1)}, u32[]{:S(2)}, u32[]{:S(2)}) %collective-permute-start.1) | collective-permute-done | bytes 524320 | tf_op jit(solution)/shard_map/ppermute | solution.py:295
  52.3 2.4 %pad_maximum_fusion.panel_ref = bf16[6,512,256]{2,1,0:T(8,128)(2,1)} fusion(bf16[2,512,256]{2,1,0:T(8,128)(2,1)} %bitcast.5, bf16[2,512,256]{2,1,0:T(8,128)(2,1)S(1)} %bitcast.28, bf16[2,512,256]{2,1,0:T(8,128)(2,1)S(1)} %bitcast.31), kind=kLoop, calls=%fused_computation | loop fusion | flops 1572864 | bytes 3145728 | tf_op jit(solution)/shard_map/concatenate | solution.py:296
  54.7 29.7 %shard_map.56 = f32[8,1024]{1,0:T(8,128)} custom-call(s32[24]{0:T(128)} %reshape.24.offs_ref, bf16[6,512,256]{2,1,0:T(8,128)(2,1)} %pad_maximum_fusion.panel_ref, bf16[2,2,6,256,256]{4,3,2,1,0:T(8,128)(2,1)} %stiff_ref.1, bf16[2,256,256]{2,1,0:T(8,128)(2,1)} %copy.13.triple_ref), custom_call_target="tpu_custom_call" | custom-call | tf_op jit(solution)/shard_map/pallas_call | solution.py:259
  84.4 1.4 %copy.14 = f32[8,2,512]{2,1,0:T(2,128)} copy(f32[8,2,512]{2,0,1:T(8,128)} %bitcast.32) | data formatting | bytes 65536 | tf_op jit(solution)/shard_map/reshape | solution.py:324
  (3 shorter events, 0.0 us)
Async XLA Ops:
  0.0 40.1 %copy-start = (bf16[2,24,32,32]{3,2,1,0:T(8,128)(2,1)S(1)}, bf16[2,24,32,32]{3,2,1,0:T(8,128)(2,1)}, u32[]{:S(2)}) copy-start(bf16[2,24,32,32]{3,2,1,0:T(8,128)(2,1)} %param.8) | copy-start | bytes 294916
  0.0 40.0 %copy-start.2 = (s32[2,24,2]{1,2,0:T(2,128)S(1)}, s32[2,24,2]{1,2,0:T(2,128)}, u32[]{:S(2)}) copy-start(s32[2,24,2]{1,2,0:T(2,128)} %param.9) | copy-start | bytes 1156
  30.7 13.5 %collective-permute-start = (bf16[2,2,256,256]{3,2,1,0:T(8,128)(2,1)S(1)}, bf16[2,2,256,256]{3,2,1,0:T(8,128)(2,1)S(1)}, u32[]{:S(2)}, u32[]{:S(2)}) collective-permute-start(bf16[2,2,256,256]{3,2,1,0:T(8,128)(2,1)S(1)} %bitcast.26), channel_id=1, source_target_pairs={{0,32},{32,64},{64,96},{96,128},{128,160},{160,192},{192,224},{224... | collective-permute-start | bytes 1572872 | tf_op jit(solution)/shard_map/ppermute | solution.py:292
  38.1 14.2 %collective-permute-start.1 = (bf16[2,2,256,256]{3,2,1,0:T(8,128)(2,1)S(1)}, bf16[2,2,256,256]{3,2,1,0:T(8,128)(2,1)}, u32[]{:S(2)}, u32[]{:S(2)}) collective-permute-start(bf16[2,2,256,256]{3,2,1,0:T(8,128)(2,1)S(1)} %bitcast.27), channel_id=1, source_target_pairs={{32,0},{64,32},{96,64},{128,96},{160,128},{192,160},{224,192},{256... | collective-permute-start | bytes 1572872 | tf_op jit(solution)/shard_map/ppermute | solution.py:295
  41.5 1.6 %copy-start.1 = (s32[2,2,6]{2,1,0:T(2,128)S(1)}, s32[2,2,6]{2,1,0:T(2,128)}, u32[]{:S(2)}) copy-start(s32[2,2,6]{2,1,0:T(2,128)} %param.7) | copy-start | bytes 292

commit v10 on v9

--- a/solution.py
+++ b/solution.py
@@ -143,81 +143,21 @@
     lax.fori_loop(1, classes, greet_near, 0)
 
 
-def scatter_stages(part_ref, own_ref, out_ref, near_slots, class_sum, far_slots,
-                   send_near, recv_near, send_far, recv_far):
-    chunk, classes = part_ref.shape[1], part_ref.shape[0] * part_ref.shape[2]
-    row, stride, lane, far_peer, near_peer = scatter_peers(chunk, classes)
-    pl.semaphore_wait(pltpu.get_barrier_semaphore(), chunk + classes - 2)
-
-    def near_out(step):
-        target = lax.rem(lane + step, classes)
-        return pltpu.make_async_remote_copy(
-            part_ref.at[target // PAIR, :, target % PAIR], near_slots.at[lane], send_near.at[step],
-            recv_near.at[lane],
-            device_id=(row, near_peer(step)), device_id_type=MESH_ID,
-        )
-
-    def near_in(step):
-        source = lax.rem(lane + classes - step, classes)
-        return pltpu.make_async_remote_copy(
-            part_ref.at[source // PAIR, :, source % PAIR], near_slots.at[source], send_near.at[step],
-            recv_near.at[source],
-            device_id=(row, term_device(source, stride, chunk)), device_id_type=MESH_ID,
-        )
-
-    def near_start(step, carry):
-        near_out(step).start()
-        return carry
-
-    def near_finish(step, total):
-        near_out(step).wait_send()
-        near_in(step).wait_recv()
-        source = lax.rem(lane + classes - step, classes)
-        return total + near_slots[source].astype(jnp.float32)
-
-    lax.fori_loop(1, classes, near_start, 0)
-    class_sum[...] = lax.fori_loop(1, classes, near_finish, own_ref[lane // PAIR, :, lane % PAIR])
-
-    def far_out(step):
-        target = lax.rem(stride + step, chunk)
-        return pltpu.make_async_remote_copy(
-            class_sum.at[target], far_slots.at[stride], send_far.at[step], recv_far.at[stride],
-            device_id=(row, far_peer(step)), device_id_type=MESH_ID,
-        )
-
-    def far_in(step):
-        source = lax.rem(stride + chunk - step, chunk)
-        return pltpu.make_async_remote_copy(
-            class_sum.at[source], far_slots.at[source], send_far.at[step], recv_far.at[source],
-            device_id=(row, term_device(lane, source, chunk)), device_id_type=MESH_ID,
-        )
-
-    def far_start(step, carry):
-        far_out(step).start()
-        return carry
-
-    def far_finish(step, total):
-        far_out(step).wait_send()
-        far_in(step).wait_recv()
-        source = lax.rem(stride + chunk - step, chunk)
-        return total + far_slots[source]
-
-    lax.fori_loop(1, chunk, far_start, 0)
-    out_ref[...] = lax.fori_loop(1, chunk, far_finish, class_sum[stride])
-
-
 def image_kernel(offs_ref, panel_ref, stiff_ref, triple_ref, out_ref, total_ref, sent_ref,
                  near_slots, class_sum, far_slots, send_near, recv_near, send_far, recv_far):
-    term = pl.program_id(0)
-    block = pl.program_id(1)
-    block_rows = pl.num_programs(1)
+    block = pl.program_id(0)
+    term = pl.program_id(1)
     band = stiff_ref.shape[2]
     width = stiff_ref.shape[-1]
     sides, chunk, _, local_rows, columns = total_ref.shape
     classes = sides * PAIR
     rows = triple_ref.shape[1]
     loads = panel_ref.shape[1] // rows
+    block_rows = columns // (loads * width)
+    term_count = pl.num_programs(1)
     rim = (panel_ref.shape[0] - block_rows) // 2
+    half = loads * width
+    row, stride, lane, far_peer, near_peer = scatter_peers(chunk, classes)
 
     @pl.when((term == 0) & (block == 0))
     def _():
@@ -233,7 +173,7 @@
         )
     image = total.astype(jnp.bfloat16)
     for load in range(loads):
-        column = pl.multiple_of((load * block_rows + block) * width, width)
+        column = pl.multiple_of((block * loads + load) * width, width)
         product = jnp.dot(
             triple_ref[0], image[load * rows:(load + 1) * rows], preferred_element_type=jnp.float32
         )
@@ -241,11 +181,82 @@
             sides, chunk, PAIR, local_rows, width
         )
 
-    @pl.when((term == pl.num_programs(0) - 1) & (block == block_rows - 1))
+    def near_copy(step, part, inbound):
+        cols = pl.ds(pl.multiple_of(part * half, half), half)
+        if inbound:
+            source = lax.rem(lane + classes - step, classes)
+            return pltpu.make_async_remote_copy(
+                sent_ref.at[source // PAIR, :, source % PAIR, :, cols],
+                near_slots.at[source, :, :, cols], send_near.at[part, step], recv_near.at[part, source],
+                device_id=(row, term_device(source, stride, chunk)), device_id_type=MESH_ID,
+            )
+        target = lax.rem(lane + step, classes)
+        return pltpu.make_async_remote_copy(
+            sent_ref.at[target // PAIR, :, target % PAIR, :, cols],
+            near_slots.at[lane, :, :, cols], send_near.at[part, step], recv_near.at[part, lane],
+            device_id=(row, near_peer(step)), device_id_type=MESH_ID,
+        )
+
+    @pl.when(term == term_count - 1)
     def _():
-        sent_ref[...] = total_ref[...].astype(sent_ref.dtype)
-        scatter_stages(sent_ref, total_ref, out_ref, near_slots, class_sum, far_slots,
-                       send_near, recv_near, send_far, recv_far)
+        cols = pl.ds(pl.multiple_of(block * half, half), half)
+        sent_ref[:, :, :, :, cols] = total_ref[:, :, :, :, cols].astype(sent_ref.dtype)
+
+        @pl.when(block == 0)
+        def _():
+            pl.semaphore_wait(pltpu.get_barrier_semaphore(), chunk + classes - 2)
+
+        def near_start(step, carry):
+            near_copy(step, block, False).start()
+            return carry
+
+        lax.fori_loop(1, classes, near_start, 0)
+
+    @pl.when((term == term_count - 1) & (block == block_rows - 1))
+    def _():
+        for part in range(block_rows):
+            cols = pl.ds(part * half, half)
+
+            def near_finish(step, total):
+                near_copy(step, part, False).wait_send()
+                near_copy(step, part, True).wait_recv()
+                source = lax.rem(lane + classes - step, classes)
+                return total + near_slots[source, :, :, cols].astype(jnp.float32)
+
+            own = total_ref[lane // PAIR, :, lane % PAIR, :, cols]
+            class_sum[:, :, cols] = lax.fori_loop(1, classes, near_finish, own)
+
+        def far_out(step):
+            target = lax.rem(stride + step, chunk)
+            return pltpu.make_async_remote_copy(
+                class_sum.at[target], far_slots.at[stride], send_far.at[step], recv_far.at[stride],
+                device_id=(row, far_peer(step)), device_id_type=MESH_ID,
+            )
+
+        def far_in(step):
+            source = lax.rem(stride + chunk - step, chunk)
+            return pltpu.make_async_remote_copy(
+                class_sum.at[source], far_slots.at[source], send_far.at[step], recv_far.at[source],
+                device_id=(row, term_device(lane, source, chunk)), device_id_type=MESH_ID,
+            )
+
+        def far_start(step, carry):
+            far_out(step).start()
+            return carry
+
+        def far_finish(step, total):
+            far_out(step).wait_send()
+            far_in(step).wait_recv()
+            source = lax.rem(stride + chunk - step, chunk)
+            return total + far_slots[source]
+
+        lax.fori_loop(1, chunk, far_start, 0)
+        summed = lax.fori_loop(1, chunk, far_finish, class_sum[stride])
+        for part in range(block_rows):
+            for load in range(loads):
+                source = (part * loads + load) * width
+                target = (load * block_rows + part) * width
+                out_ref[:, target:target + width] = summed[:, source:source + width]
 
 
 def image_scatter(offsets, panel, stiff_blocks, dense, local_rows):
@@ -261,21 +272,21 @@
         out_shape=jax.ShapeDtypeStruct((local_rows, columns), jnp.float32),
         grid_spec=pltpu.PrefetchScalarGridSpec(
             num_scalar_prefetch=1,
-            grid=(term_count, block_rows),
+            grid=(block_rows, term_count),
             in_specs=[
-                pl.BlockSpec((places, stacked, width), lambda k, b, offs: (0, 0, 0)),
-                pl.BlockSpec((1, 1, band, width, width), lambda k, b, offs: (k, b, 0, 0, 0)),
-                pl.BlockSpec((1, rows, rows), lambda k, b, offs: (k, 0, 0)),
+                pl.BlockSpec((places, stacked, width), lambda b, k, offs: (0, 0, 0)),
+                pl.BlockSpec((1, 1, band, width, width), lambda b, k, offs: (k, b, 0, 0, 0)),
+                pl.BlockSpec((1, rows, rows), lambda b, k, offs: (k, 0, 0)),
             ],
-            out_specs=pl.BlockSpec((local_rows, columns), lambda k, b, offs: (0, 0)),
+            out_specs=pl.BlockSpec((local_rows, columns), lambda b, k, offs: (0, 0)),
             scratch_shapes=[
                 pltpu.VMEM(shape, jnp.float32),
                 pltpu.VMEM(shape, jnp.bfloat16),
                 pltpu.VMEM((classes, chunk, local_rows, columns), jnp.bfloat16),
                 pltpu.VMEM((chunk, local_rows, columns), jnp.float32),
                 pltpu.VMEM((chunk, local_rows, columns), jnp.float32),
-                pltpu.SemaphoreType.DMA((classes,)),
-                pltpu.SemaphoreType.DMA((classes,)),
+                pltpu.SemaphoreType.DMA((block_rows, classes)),
+                pltpu.SemaphoreType.DMA((block_rows, classes)),
                 pltpu.SemaphoreType.DMA((chunk,)),
                 pltpu.SemaphoreType.DMA((chunk,)),
             ],

time: 86.6 us -> 85.1 us (0.983)
  Pallas kernels: 57.7 us -> 56.6 us
    pallas_call x1, Pallas kernels: 29.7 us -> 28.6 us  [image_scatter(): pl.pallas_call(image_kernel, out_shape=jax.ShapeDtypeStruct((local_rows,...]
where the time goes in v10:
time: 85.1 us; the launch traced here: 84.7 us
  Pallas kernels  56.6 us (67%)
  starting transfers between devices  9.3 us (11%)
  waiting for transfers between devices  8.64 us (10%)
  local copies, waits for them, and re-layouts  7.19 us (8%)
  other arithmetic  2.37 us (3%)
    pallas_call x1, Pallas kernels, image_scatter(): pl.pallas_call(image_kernel, out_shape=jax.ShapeDtypeStruct((local_rows,...  28.6 us
    pallas_call x1, Pallas kernels, gather_term(): pl.pallas_call(gather_kernel, out_shape=jax.ShapeDtypeStruct((count,) + b...  28.1 us
    ppermute x1, waiting for transfers between devices, with_halo(): lax.ppermute(lax.slice_in_dim(block, 0, width, axis=dim), axis, backward)  8.12 us
    ppermute x1, starting transfers between devices, with_halo(): lax.ppermute(lax.slice_in_dim(block, block.shape[dim] - width, None, axis...  7.38 us
    convert_element_type x4, local copies, waits for them, and re-layouts, per_device(): dense = dense.astype(jnp.bfloat16)  2.54 us
    concatenate x1, other arithmetic, with_halo(): block = jnp.concatenate([low, block, high], axis=dim)  2.37 us
    ppermute x1, starting transfers between devices, with_halo(): lax.ppermute(lax.slice_in_dim(block, 0, width, axis=dim), axis, backward)  1.92 us
  transfers between devices with their start and end apart: 2, of which 2 were waited for; matrix products, arithmetic and copies ran while one was open for 4% of the time, Pallas kernels for 0%

profile of v10, /device:TPU:7, one launch (start us, length us, event | category | flops | bytes accessed | tf_op | source)
XLA Modules:
  0.0 84.7 jit_solution(17044298189821392164)
XLA Ops:
  0.0 0.0 copy-start
  0.0 0.0 copy-start.2
  0.0 1.4 %reshape.25.block_ref = bf16[16,512]{1,0:T(8,128)(2,1)} reshape(bf16[8,2,512]{2,1,0:T(2,128)(2,1)} %param.5) | data formatting | bytes 32768 | tf_op jit(solution)/shard_map/reshape | solution.py:321
  1.4 28.1 %shard_map.55 = bf16[32,16,512]{2,1,0:T(8,128)(2,1)} custom-call(bf16[16,512]{1,0:T(8,128)(2,1)} %reshape.25.block_ref), custom_call_target="tpu_custom_call" | custom-call | tf_op jit(solution)/shard_map/pallas_call | solution.py:94
  29.5 1.2 %reshape.26 = bf16[32,8,2,2,256]{4,3,2,1,0:T(2,128)(2,1)S(1)} reshape(bf16[32,16,512]{2,1,0:T(8,128)(2,1)} %shard_map.55) | data formatting | bytes 1048576 | tf_op jit(solution)/shard_map/reshape | solution.py:322
  30.7 0.1 copy.23
  30.7 7.4 %collective-permute-start = (bf16[2,2,256,256]{3,2,1,0:T(8,128)(2,1)S(1)}, bf16[2,2,256,256]{3,2,1,0:T(8,128)(2,1)S(1)}, u32[]{:S(2)}, u32[]{:S(2)}) collective-permute-start(bf16[2,2,256,256]{3,2,1,0:T(8,128)(2,1)S(1)} %bitcast.26), channel_id=1, source_target_pairs={{0,32},{32,64},{64,96},{96,128},{128,160},{160,192},{192,224},{224... | collective-permute-start | bytes 1572872 | tf_op jit(solution)/shard_map/ppermute | solution.py:303
  38.1 1.9 %collective-permute-start.1 = (bf16[2,2,256,256]{3,2,1,0:T(8,128)(2,1)S(1)}, bf16[2,2,256,256]{3,2,1,0:T(8,128)(2,1)}, u32[]{:S(2)}, u32[]{:S(2)}) collective-permute-start(bf16[2,2,256,256]{3,2,1,0:T(8,128)(2,1)S(1)} %bitcast.27), channel_id=1, source_target_pairs={{32,0},{64,32},{96,64},{128,96},{160,128},{192,160},{224,192},{256... | collective-permute-start | bytes 1572872 | tf_op jit(solution)/shard_map/ppermute | solution.py:306
  40.0 0.0 copy-done.2
  40.1 0.0 copy-done
  40.1 0.4 fusion
  40.5 1.0 %copy.11 = bf16[2,8,32,8,32]{2,1,4,3,0:T(8,128)(2,1)S(1)} copy(bf16[2,8,32,8,32]{4,1,2,3,0:T(8,128)(2,1)S(1)} %fusion) | data formatting | bytes 524288 | tf_op jit(solution)/shard_map/convert_element_type | solution.py:333
  41.5 0.0 copy-start.1
  41.5 0.7 convert_element_type.16
  42.3 0.8 copy.13.triple_ref
  43.1 0.0 copy-done.1
  43.1 0.6 reshape.24.offs_ref
  43.7 0.5 collective-permute-done
  44.2 8.1 %collective-permute-done.1 = bf16[2,2,256,256]{3,2,1,0:T(8,128)(2,1)} collective-permute-done((bf16[2,2,256,256]{3,2,1,0:T(8,128)(2,1)S(1)}, bf16[2,2,256,256]{3,2,1,0:T(8,128)(2,1)}, u32[]{:S(2)}, u32[]{:S(2)}) %collective-permute-start.1) | collective-permute-done | bytes 524320 | tf_op jit(solution)/shard_map/ppermute | solution.py:306
  52.3 2.4 %pad_maximum_fusion.panel_ref = bf16[6,512,256]{2,1,0:T(8,128)(2,1)} fusion(bf16[2,512,256]{2,1,0:T(8,128)(2,1)} %bitcast.5, bf16[2,512,256]{2,1,0:T(8,128)(2,1)S(1)} %bitcast.28, bf16[2,512,256]{2,1,0:T(8,128)(2,1)S(1)} %bitcast.31), kind=kLoop, calls=%fused_computation | loop fusion | flops 1572864 | bytes 3145728 | tf_op jit(solution)/shard_map/concatenate | solution.py:307
  54.7 28.6 %shard_map.56 = f32[8,1024]{1,0:T(8,128)} custom-call(s32[24]{0:T(128)} %reshape.24.offs_ref, bf16[6,512,256]{2,1,0:T(8,128)(2,1)} %pad_maximum_fusion.panel_ref, bf16[2,2,6,256,256]{4,3,2,1,0:T(8,128)(2,1)} %stiff_ref.1, bf16[2,256,256]{2,1,0:T(8,128)(2,1)} %copy.13.triple_ref), custom_call_target="tpu_custom_call" | custom-call | tf_op jit(solution)/shard_map/pallas_call | solution.py:270
  83.3 1.4 %copy.14 = f32[8,2,512]{2,1,0:T(2,128)} copy(f32[8,2,512]{2,0,1:T(8,128)} %bitcast.32) | data formatting | bytes 65536 | tf_op jit(solution)/shard_map/reshape | solution.py:335
  (3 shorter events, 0.0 us)
Async XLA Ops:
  0.0 40.1 %copy-start = (bf16[2,24,32,32]{3,2,1,0:T(8,128)(2,1)S(1)}, bf16[2,24,32,32]{3,2,1,0:T(8,128)(2,1)}, u32[]{:S(2)}) copy-start(bf16[2,24,32,32]{3,2,1,0:T(8,128)(2,1)} %param.8) | copy-start | bytes 294916
  0.0 40.0 %copy-start.2 = (s32[2,24,2]{1,2,0:T(2,128)S(1)}, s32[2,24,2]{1,2,0:T(2,128)}, u32[]{:S(2)}) copy-start(s32[2,24,2]{1,2,0:T(2,128)} %param.9) | copy-start | bytes 1156
  30.7 13.5 %collective-permute-start = (bf16[2,2,256,256]{3,2,1,0:T(8,128)(2,1)S(1)}, bf16[2,2,256,256]{3,2,1,0:T(8,128)(2,1)S(1)}, u32[]{:S(2)}, u32[]{:S(2)}) collective-permute-start(bf16[2,2,256,256]{3,2,1,0:T(8,128)(2,1)S(1)} %bitcast.26), channel_id=1, source_target_pairs={{0,32},{32,64},{64,96},{96,128},{128,160},{160,192},{192,224},{224... | collective-permute-start | bytes 1572872 | tf_op jit(solution)/shard_map/ppermute | solution.py:303
  38.1 14.2 %collective-permute-start.1 = (bf16[2,2,256,256]{3,2,1,0:T(8,128)(2,1)S(1)}, bf16[2,2,256,256]{3,2,1,0:T(8,128)(2,1)}, u32[]{:S(2)}, u32[]{:S(2)}) collective-permute-start(bf16[2,2,256,256]{3,2,1,0:T(8,128)(2,1)S(1)} %bitcast.27), channel_id=1, source_target_pairs={{32,0},{64,32},{96,64},{128,96},{160,128},{192,160},{224,192},{256... | collective-permute-start | bytes 1572872 | tf_op jit(solution)/shard_map/ppermute | solution.py:306
  41.5 1.6 %copy-start.1 = (s32[2,2,6]{2,1,0:T(2,128)S(1)}, s32[2,2,6]{2,1,0:T(2,128)}, u32[]{:S(2)}) copy-start(s32[2,2,6]{2,1,0:T(2,128)} %param.7) | copy-start | bytes 292

commit v11 on v10

--- a/solution.py
+++ b/solution.py
@@ -143,7 +143,7 @@
     lax.fori_loop(1, classes, greet_near, 0)
 
 
-def image_kernel(offs_ref, panel_ref, stiff_ref, triple_ref, out_ref, total_ref, sent_ref,
+def image_kernel(offs_ref, panel_ref, stiff_ref, triple_ref, out_ref, total_ref, far_src,
                  near_slots, class_sum, far_slots, send_near, recv_near, send_far, recv_far):
     block = pl.program_id(0)
     term = pl.program_id(1)
@@ -186,22 +186,19 @@
         if inbound:
             source = lax.rem(lane + classes - step, classes)
             return pltpu.make_async_remote_copy(
-                sent_ref.at[source // PAIR, :, source % PAIR, :, cols],
+                total_ref.at[source // PAIR, :, source % PAIR, :, cols],
                 near_slots.at[source, :, :, cols], send_near.at[part, step], recv_near.at[part, source],
                 device_id=(row, term_device(source, stride, chunk)), device_id_type=MESH_ID,
             )
         target = lax.rem(lane + step, classes)
         return pltpu.make_async_remote_copy(
-            sent_ref.at[target // PAIR, :, target % PAIR, :, cols],
+            total_ref.at[target // PAIR, :, target % PAIR, :, cols],
             near_slots.at[lane, :, :, cols], send_near.at[part, step], recv_near.at[part, lane],
             device_id=(row, near_peer(step)), device_id_type=MESH_ID,
         )
 
     @pl.when(term == term_count - 1)
     def _():
-        cols = pl.ds(pl.multiple_of(block * half, half), half)
-        sent_ref[:, :, :, :, cols] = total_ref[:, :, :, :, cols].astype(sent_ref.dtype)
-
         @pl.when(block == 0)
         def _():
             pl.semaphore_wait(pltpu.get_barrier_semaphore(), chunk + classes - 2)
@@ -221,22 +218,24 @@
                 near_copy(step, part, False).wait_send()
                 near_copy(step, part, True).wait_recv()
                 source = lax.rem(lane + classes - step, classes)
-                return total + near_slots[source, :, :, cols].astype(jnp.float32)
+                return total + near_slots[source, :, :, cols]
 
             own = total_ref[lane // PAIR, :, lane % PAIR, :, cols]
             class_sum[:, :, cols] = lax.fori_loop(1, classes, near_finish, own)
+
+        far_src[...] = class_sum[...].astype(far_src.dtype)
 
         def far_out(step):
             target = lax.rem(stride + step, chunk)
             return pltpu.make_async_remote_copy(
-                class_sum.at[target], far_slots.at[stride], send_far.at[step], recv_far.at[stride],
+                far_src.at[target], far_slots.at[stride], send_far.at[step], recv_far.at[stride],
                 device_id=(row, far_peer(step)), device_id_type=MESH_ID,
             )
 
         def far_in(step):
             source = lax.rem(stride + chunk - step, chunk)
             return pltpu.make_async_remote_copy(
-                class_sum.at[source], far_slots.at[source], send_far.at[step], recv_far.at[source],
+                far_src.at[source], far_slots.at[source], send_far.at[step], recv_far.at[source],
                 device_id=(row, term_device(lane, source, chunk)), device_id_type=MESH_ID,
             )
 
@@ -248,7 +247,7 @@
             far_out(step).wait_send()
             far_in(step).wait_recv()
             source = lax.rem(stride + chunk - step, chunk)
-            return total + far_slots[source]
+            return total + far_slots[source].astype(jnp.float32)
 
         lax.fori_loop(1, chunk, far_start, 0)
         summed = lax.fori_loop(1, chunk, far_finish, class_sum[stride])
@@ -281,10 +280,10 @@
             out_specs=pl.BlockSpec((local_rows, columns), lambda b, k, offs: (0, 0)),
             scratch_shapes=[
                 pltpu.VMEM(shape, jnp.float32),
-                pltpu.VMEM(shape, jnp.bfloat16),
-                pltpu.VMEM((classes, chunk, local_rows, columns), jnp.bfloat16),
+                pltpu.VMEM((chunk, local_rows, columns), jnp.bfloat16),
+                pltpu.VMEM((classes, chunk, local_rows, columns), jnp.float32),
                 pltpu.VMEM((chunk, local_rows, columns), jnp.float32),
-                pltpu.VMEM((chunk, local_rows, columns), jnp.float32),
+                pltpu.VMEM((chunk, local_rows, columns), jnp.bfloat16),
                 pltpu.SemaphoreType.DMA((block_rows, classes)),
                 pltpu.SemaphoreType.DMA((block_rows, classes)),
                 pltpu.SemaphoreType.DMA((chunk,)),

time: 85.1 us -> 83.7 us (0.984)
  Pallas kernels: 56.6 us -> 55.2 us
    pallas_call x1, Pallas kernels: 28.6 us -> 27.1 us  [image_scatter(): pl.pallas_call(image_kernel, out_shape=jax.ShapeDtypeStruct((local_rows,...]
where the time goes in v11:
time: 83.7 us; the launch traced here: 83.3 us
  Pallas kernels  55.2 us (66%)
  starting transfers between devices  9.3 us (11%)
  waiting for transfers between devices  8.64 us (10%)
  local copies, waits for them, and re-layouts  7.19 us (9%)
  other arithmetic  2.37 us (3%)
    pallas_call x1, Pallas kernels, gather_term(): pl.pallas_call(gather_kernel, out_shape=jax.ShapeDtypeStruct((count,) + b...  28.1 us
    pallas_call x1, Pallas kernels, image_scatter(): pl.pallas_call(image_kernel, out_shape=jax.ShapeDtypeStruct((local_rows,...  27.1 us
    ppermute x1, waiting for transfers between devices, with_halo(): lax.ppermute(lax.slice_in_dim(block, 0, width, axis=dim), axis, backward)  8.12 us
    ppermute x1, starting transfers between devices, with_halo(): lax.ppermute(lax.slice_in_dim(block, block.shape[dim] - width, None, axis...  7.38 us
    convert_element_type x4, local copies, waits for them, and re-layouts, per_device(): dense = dense.astype(jnp.bfloat16)  2.54 us
    concatenate x1, other arithmetic, with_halo(): block = jnp.concatenate([low, block, high], axis=dim)  2.37 us
    ppermute x1, starting transfers between devices, with_halo(): lax.ppermute(lax.slice_in_dim(block, 0, width, axis=dim), axis, backward)  1.92 us
  transfers between devices with their start and end apart: 2, of which 2 were waited for; matrix products, arithmetic and copies ran while one was open for 4% of the time, Pallas kernels for 0%

profile of v11, /device:TPU:7, one launch (start us, length us, event | category | flops | bytes accessed | tf_op | source)
XLA Modules:
  0.0 83.3 jit_solution(14483591131300570567)
XLA Ops:
  0.0 0.0 copy-start
  0.0 0.0 copy-start.2
  0.0 1.4 %reshape.25.block_ref = bf16[16,512]{1,0:T(8,128)(2,1)} reshape(bf16[8,2,512]{2,1,0:T(2,128)(2,1)} %param.5) | data formatting | bytes 32768 | tf_op jit(solution)/shard_map/reshape | solution.py:320
  1.4 28.1 %shard_map.55 = bf16[32,16,512]{2,1,0:T(8,128)(2,1)} custom-call(bf16[16,512]{1,0:T(8,128)(2,1)} %reshape.25.block_ref), custom_call_target="tpu_custom_call" | custom-call | tf_op jit(solution)/shard_map/pallas_call | solution.py:94
  29.5 1.2 %reshape.26 = bf16[32,8,2,2,256]{4,3,2,1,0:T(2,128)(2,1)S(1)} reshape(bf16[32,16,512]{2,1,0:T(8,128)(2,1)} %shard_map.55) | data formatting | bytes 1048576 | tf_op jit(solution)/shard_map/reshape | solution.py:321
  30.7 0.1 copy.23
  30.7 7.4 %collective-permute-start = (bf16[2,2,256,256]{3,2,1,0:T(8,128)(2,1)S(1)}, bf16[2,2,256,256]{3,2,1,0:T(8,128)(2,1)S(1)}, u32[]{:S(2)}, u32[]{:S(2)}) collective-permute-start(bf16[2,2,256,256]{3,2,1,0:T(8,128)(2,1)S(1)} %bitcast.26), channel_id=1, source_target_pairs={{0,32},{32,64},{64,96},{96,128},{128,160},{160,192},{192,224},{224... | collective-permute-start | bytes 1572872 | tf_op jit(solution)/shard_map/ppermute | solution.py:302
  38.1 1.9 %collective-permute-start.1 = (bf16[2,2,256,256]{3,2,1,0:T(8,128)(2,1)S(1)}, bf16[2,2,256,256]{3,2,1,0:T(8,128)(2,1)}, u32[]{:S(2)}, u32[]{:S(2)}) collective-permute-start(bf16[2,2,256,256]{3,2,1,0:T(8,128)(2,1)S(1)} %bitcast.27), channel_id=1, source_target_pairs={{32,0},{64,32},{96,64},{128,96},{160,128},{192,160},{224,192},{256... | collective-permute-start | bytes 1572872 | tf_op jit(solution)/shard_map/ppermute | solution.py:305
  40.0 0.0 copy-done.2
  40.1 0.0 copy-done
  40.1 0.4 fusion
  40.5 1.0 %copy.11 = bf16[2,8,32,8,32]{2,1,4,3,0:T(8,128)(2,1)S(1)} copy(bf16[2,8,32,8,32]{4,1,2,3,0:T(8,128)(2,1)S(1)} %fusion) | data formatting | bytes 524288 | tf_op jit(solution)/shard_map/convert_element_type | solution.py:332
  41.5 0.0 copy-start.1
  41.5 0.7 convert_element_type.16
  42.3 0.8 %copy.13.triple_ref = bf16[2,256,256]{2,1,0:T(8,128)(2,1)} copy(bf16[2,256,256]{1,2,0:T(8,128)(2,1)S(1)} %bitcast.30) | data formatting | bytes 524288 | tf_op jit(solution)/shard_map/convert_element_type | solution.py:332
  43.1 0.0 copy-done.1
  43.1 0.6 reshape.24.offs_ref
  43.7 0.5 collective-permute-done
  44.2 8.1 %collective-permute-done.1 = bf16[2,2,256,256]{3,2,1,0:T(8,128)(2,1)} collective-permute-done((bf16[2,2,256,256]{3,2,1,0:T(8,128)(2,1)S(1)}, bf16[2,2,256,256]{3,2,1,0:T(8,128)(2,1)}, u32[]{:S(2)}, u32[]{:S(2)}) %collective-permute-start.1) | collective-permute-done | bytes 524320 | tf_op jit(solution)/shard_map/ppermute | solution.py:305
  52.3 2.4 %pad_maximum_fusion.panel_ref = bf16[6,512,256]{2,1,0:T(8,128)(2,1)} fusion(bf16[2,512,256]{2,1,0:T(8,128)(2,1)} %bitcast.5, bf16[2,512,256]{2,1,0:T(8,128)(2,1)S(1)} %bitcast.28, bf16[2,512,256]{2,1,0:T(8,128)(2,1)S(1)} %bitcast.31), kind=kLoop, calls=%fused_computation | loop fusion | flops 1572864 | bytes 3145728 | tf_op jit(solution)/shard_map/concatenate | solution.py:306
  54.7 27.1 %shard_map.56 = f32[8,1024]{1,0:T(8,128)} custom-call(s32[24]{0:T(128)} %reshape.24.offs_ref, bf16[6,512,256]{2,1,0:T(8,128)(2,1)} %pad_maximum_fusion.panel_ref, bf16[2,2,6,256,256]{4,3,2,1,0:T(8,128)(2,1)} %stiff_ref.1, bf16[2,256,256]{2,1,0:T(8,128)(2,1)} %copy.13.triple_ref), custom_call_target="tpu_custom_call" | custom-call | tf_op jit(solution)/shard_map/pallas_call | solution.py:269
  81.9 1.4 %copy.14 = f32[8,2,512]{2,1,0:T(2,128)} copy(f32[8,2,512]{2,0,1:T(8,128)} %bitcast.32) | data formatting | bytes 65536 | tf_op jit(solution)/shard_map/reshape | solution.py:334
  (3 shorter events, 0.0 us)
Async XLA Ops:
  0.0 40.1 %copy-start = (bf16[2,24,32,32]{3,2,1,0:T(8,128)(2,1)S(1)}, bf16[2,24,32,32]{3,2,1,0:T(8,128)(2,1)}, u32[]{:S(2)}) copy-start(bf16[2,24,32,32]{3,2,1,0:T(8,128)(2,1)} %param.8) | copy-start | bytes 294916
  0.0 40.0 %copy-start.2 = (s32[2,24,2]{1,2,0:T(2,128)S(1)}, s32[2,24,2]{1,2,0:T(2,128)}, u32[]{:S(2)}) copy-start(s32[2,24,2]{1,2,0:T(2,128)} %param.9) | copy-start | bytes 1156
  30.7 13.5 %collective-permute-start = (bf16[2,2,256,256]{3,2,1,0:T(8,128)(2,1)S(1)}, bf16[2,2,256,256]{3,2,1,0:T(8,128)(2,1)S(1)}, u32[]{:S(2)}, u32[]{:S(2)}) collective-permute-start(bf16[2,2,256,256]{3,2,1,0:T(8,128)(2,1)S(1)} %bitcast.26), channel_id=1, source_target_pairs={{0,32},{32,64},{64,96},{96,128},{128,160},{160,192},{192,224},{224... | collective-permute-start | bytes 1572872 | tf_op jit(solution)/shard_map/ppermute | solution.py:302
  38.1 14.2 %collective-permute-start.1 = (bf16[2,2,256,256]{3,2,1,0:T(8,128)(2,1)S(1)}, bf16[2,2,256,256]{3,2,1,0:T(8,128)(2,1)}, u32[]{:S(2)}, u32[]{:S(2)}) collective-permute-start(bf16[2,2,256,256]{3,2,1,0:T(8,128)(2,1)S(1)} %bitcast.27), channel_id=1, source_target_pairs={{32,0},{64,32},{96,64},{128,96},{160,128},{192,160},{224,192},{256... | collective-permute-start | bytes 1572872 | tf_op jit(solution)/shard_map/ppermute | solution.py:305
  41.5 1.6 %copy-start.1 = (s32[2,2,6]{2,1,0:T(2,128)S(1)}, s32[2,2,6]{2,1,0:T(2,128)}, u32[]{:S(2)}) copy-start(s32[2,2,6]{2,1,0:T(2,128)} %param.7) | copy-start | bytes 292

commit v12 on v11

--- a/solution.py
+++ b/solution.py
@@ -47,6 +47,25 @@
             device_id=(row, term_device(lane, source, chunk)), device_id_type=MESH_ID,
         )
 
+    def near_out(held, step):
+        slot = out_ref.at[lane * chunk + held]
+        return pltpu.make_async_remote_copy(
+            slot, slot, send_near.at[held, step], recv_near.at[held, lane],
+            device_id=(row, near_peer(step)), device_id_type=MESH_ID,
+        )
+
+    def near_in(held, step):
+        source = lax.rem(lane + CLASSES - step, CLASSES)
+        slot = out_ref.at[source * chunk + held]
+        return pltpu.make_async_remote_copy(
+            slot, slot, send_near.at[held, step], recv_near.at[held, source],
+            device_id=(row, term_device(source, stride, chunk)), device_id_type=MESH_ID,
+        )
+
+    def forward(held):
+        for step in range(1, CLASSES):
+            near_out(held, step).start()
+
     def far_start(step, carry):
         far_out(step).start()
         return carry
@@ -54,39 +73,21 @@
     def far_finish(step, carry):
         far_out(step).wait_send()
         far_in(step).wait_recv()
+        forward(lax.rem(stride + chunk - step, chunk))
         return carry
 
     lax.fori_loop(1, chunk, far_start, 0)
     local.wait()
+    forward(stride)
     lax.fori_loop(1, chunk, far_finish, 0)
 
-    own = out_ref.at[pl.ds(lane * chunk, chunk)]
-
-    def near_out(step):
-        return pltpu.make_async_remote_copy(
-            own, own, send_near.at[step], recv_near.at[lane],
-            device_id=(row, near_peer(step)), device_id_type=MESH_ID,
-        )
-
-    def near_in(step):
-        source = lax.rem(lane + CLASSES - step, CLASSES)
-        theirs = out_ref.at[pl.ds(source * chunk, chunk)]
-        return pltpu.make_async_remote_copy(
-            theirs, theirs, send_near.at[step], recv_near.at[source],
-            device_id=(row, term_device(source, stride, chunk)), device_id_type=MESH_ID,
-        )
-
-    def near_start(step, carry):
-        near_out(step).start()
-        return carry
-
-    def near_finish(step, carry):
-        near_out(step).wait_send()
-        near_in(step).wait_recv()
-        return carry
-
-    lax.fori_loop(1, CLASSES, near_start, 0)
-    lax.fori_loop(1, CLASSES, near_finish, 0)
+    def near_finish(held, carry):
+        for step in range(1, CLASSES):
+            near_out(held, step).wait_send()
+            near_in(held, step).wait_recv()
+        return carry
+
+    lax.fori_loop(0, chunk, near_finish, 0)
 
 
 def gather_term(block):
@@ -98,8 +99,8 @@
         out_specs=pl.BlockSpec(memory_space=pltpu.VMEM),
         scratch_shapes=[
             pltpu.SemaphoreType.DMA(()),
-            pltpu.SemaphoreType.DMA((CLASSES,)),
-            pltpu.SemaphoreType.DMA((CLASSES,)),
+            pltpu.SemaphoreType.DMA((count // CLASSES, CLASSES)),
+            pltpu.SemaphoreType.DMA((count // CLASSES, CLASSES)),
             pltpu.SemaphoreType.DMA((count // CLASSES,)),
             pltpu.SemaphoreType.DMA((count // CLASSES,)),
         ],

time: 83.7 us -> 83.9 us (level); the launches traced: 83.3 us -> 82.4 us
  starting transfers between devices: 9.3 us -> 7.66 us
    ppermute x1, starting transfers between devices: 7.38 us -> 5.74 us  [with_halo(): lax.ppermute(lax.slice_in_dim(block, block.shape[dim] - width, None, axis...]
    pallas_call x1, Pallas kernels: 28.1 us -> 29.6 us  [gather_term(): pl.pallas_call(gather_kernel, out_shape=jax.ShapeDtypeStruct((count,) + b...]
where the time goes in v12:
time: 83.9 us; the launch traced here: 82.4 us
  Pallas kernels  55.9 us (67%)
  waiting for transfers between devices  8.64 us (10%)
  starting transfers between devices  7.66 us (9%)
  local copies, waits for them, and re-layouts  7.19 us (9%)
  other arithmetic  2.37 us (3%)
    pallas_call x1, Pallas kernels, gather_term(): pl.pallas_call(gather_kernel, out_shape=jax.ShapeDtypeStruct((count,) + b...  29.6 us
    pallas_call x1, Pallas kernels, image_scatter(): pl.pallas_call(image_kernel, out_shape=jax.ShapeDtypeStruct((local_rows,...  26.4 us
    ppermute x1, waiting for transfers between devices, with_halo(): lax.ppermute(lax.slice_in_dim(block, 0, width, axis=dim), axis, backward)  8.12 us
    ppermute x1, starting transfers between devices, with_halo(): lax.ppermute(lax.slice_in_dim(block, block.shape[dim] - width, None, axis...  5.74 us
    convert_element_type x4, local copies, waits for them, and re-layouts, per_device(): dense = dense.astype(jnp.bfloat16)  2.54 us
    concatenate x1, other arithmetic, with_halo(): block = jnp.concatenate([low, block, high], axis=dim)  2.37 us
    ppermute x1, starting transfers between devices, with_halo(): lax.ppermute(lax.slice_in_dim(block, 0, width, axis=dim), axis, backward)  1.92 us
  transfers between devices with their start and end apart: 2, of which 2 were waited for; matrix products, arithmetic and copies ran while one was open for 4% of the time, Pallas kernels for 0%

profile of v12, /device:TPU:7, one launch (start us, length us, event | category | flops | bytes accessed | tf_op | source)
XLA Modules:
  0.0 82.4 jit_solution(11853106869837599282)
XLA Ops:
  0.0 0.0 copy-start
  0.0 0.0 copy-start.2
  0.0 1.4 %reshape.25.block_ref = bf16[16,512]{1,0:T(8,128)(2,1)} reshape(bf16[8,2,512]{2,1,0:T(2,128)(2,1)} %param.5) | data formatting | bytes 32768 | tf_op jit(solution)/shard_map/reshape | solution.py:321
  1.4 29.6 %shard_map.55 = bf16[32,16,512]{2,1,0:T(8,128)(2,1)} custom-call(bf16[16,512]{1,0:T(8,128)(2,1)} %reshape.25.block_ref), custom_call_target="tpu_custom_call" | custom-call | tf_op jit(solution)/shard_map/pallas_call | solution.py:95
  31.0 1.2 %reshape.26 = bf16[32,8,2,2,256]{4,3,2,1,0:T(2,128)(2,1)S(1)} reshape(bf16[32,16,512]{2,1,0:T(8,128)(2,1)} %shard_map.55) | data formatting | bytes 1048576 | tf_op jit(solution)/shard_map/reshape | solution.py:322
  32.2 0.1 copy.23
  32.2 5.7 %collective-permute-start = (bf16[2,2,256,256]{3,2,1,0:T(8,128)(2,1)S(1)}, bf16[2,2,256,256]{3,2,1,0:T(8,128)(2,1)S(1)}, u32[]{:S(2)}, u32[]{:S(2)}) collective-permute-start(bf16[2,2,256,256]{3,2,1,0:T(8,128)(2,1)S(1)} %bitcast.26), channel_id=1, source_target_pairs={{0,32},{32,64},{64,96},{96,128},{128,160},{160,192},{192,224},{224... | collective-permute-start | bytes 1572872 | tf_op jit(solution)/shard_map/ppermute | solution.py:303
  38.0 1.9 %collective-permute-start.1 = (bf16[2,2,256,256]{3,2,1,0:T(8,128)(2,1)S(1)}, bf16[2,2,256,256]{3,2,1,0:T(8,128)(2,1)}, u32[]{:S(2)}, u32[]{:S(2)}) collective-permute-start(bf16[2,2,256,256]{3,2,1,0:T(8,128)(2,1)S(1)} %bitcast.27), channel_id=1, source_target_pairs={{32,0},{64,32},{96,64},{128,96},{160,128},{192,160},{224,192},{256... | collective-permute-start | bytes 1572872 | tf_op jit(solution)/shard_map/ppermute | solution.py:306
  39.9 0.0 copy-done.2
  40.0 0.0 copy-done
  40.0 0.4 fusion
  40.4 1.0 %copy.11 = bf16[2,8,32,8,32]{2,1,4,3,0:T(8,128)(2,1)S(1)} copy(bf16[2,8,32,8,32]{4,1,2,3,0:T(8,128)(2,1)S(1)} %fusion) | data formatting | bytes 524288 | tf_op jit(solution)/shard_map/convert_element_type | solution.py:333
  41.4 0.0 copy-start.1
  41.4 0.7 convert_element_type.16
  42.1 0.8 %copy.13.triple_ref = bf16[2,256,256]{2,1,0:T(8,128)(2,1)} copy(bf16[2,256,256]{1,2,0:T(8,128)(2,1)S(1)} %bitcast.30) | data formatting | bytes 524288 | tf_op jit(solution)/shard_map/convert_element_type | solution.py:333
  43.0 0.0 copy-done.1
  43.0 0.6 reshape.24.offs_ref
  43.6 0.5 collective-permute-done
  44.1 8.1 %collective-permute-done.1 = bf16[2,2,256,256]{3,2,1,0:T(8,128)(2,1)} collective-permute-done((bf16[2,2,256,256]{3,2,1,0:T(8,128)(2,1)S(1)}, bf16[2,2,256,256]{3,2,1,0:T(8,128)(2,1)}, u32[]{:S(2)}, u32[]{:S(2)}) %collective-permute-start.1) | collective-permute-done | bytes 524320 | tf_op jit(solution)/shard_map/ppermute | solution.py:306
  52.2 2.4 %pad_maximum_fusion.panel_ref = bf16[6,512,256]{2,1,0:T(8,128)(2,1)} fusion(bf16[2,512,256]{2,1,0:T(8,128)(2,1)} %bitcast.5, bf16[2,512,256]{2,1,0:T(8,128)(2,1)S(1)} %bitcast.28, bf16[2,512,256]{2,1,0:T(8,128)(2,1)S(1)} %bitcast.31), kind=kLoop, calls=%fused_computation | loop fusion | flops 1572864 | bytes 3145728 | tf_op jit(solution)/shard_map/concatenate | solution.py:307
  54.6 26.4 %shard_map.56 = f32[8,1024]{1,0:T(8,128)} custom-call(s32[24]{0:T(128)} %reshape.24.offs_ref, bf16[6,512,256]{2,1,0:T(8,128)(2,1)} %pad_maximum_fusion.panel_ref, bf16[2,2,6,256,256]{4,3,2,1,0:T(8,128)(2,1)} %stiff_ref.1, bf16[2,256,256]{2,1,0:T(8,128)(2,1)} %copy.13.triple_ref), custom_call_target="tpu_custom_call" | custom-call | tf_op jit(solution)/shard_map/pallas_call | solution.py:270
  81.0 1.4 %copy.14 = f32[8,2,512]{2,1,0:T(2,128)} copy(f32[8,2,512]{2,0,1:T(8,128)} %bitcast.32) | data formatting | bytes 65536 | tf_op jit(solution)/shard_map/reshape | solution.py:335
  (3 shorter events, 0.0 us)
Async XLA Ops:
  0.0 40.0 %copy-start = (bf16[2,24,32,32]{3,2,1,0:T(8,128)(2,1)S(1)}, bf16[2,24,32,32]{3,2,1,0:T(8,128)(2,1)}, u32[]{:S(2)}) copy-start(bf16[2,24,32,32]{3,2,1,0:T(8,128)(2,1)} %param.8) | copy-start | bytes 294916
  0.0 39.9 %copy-start.2 = (s32[2,24,2]{1,2,0:T(2,128)S(1)}, s32[2,24,2]{1,2,0:T(2,128)}, u32[]{:S(2)}) copy-start(s32[2,24,2]{1,2,0:T(2,128)} %param.9) | copy-start | bytes 1156
  32.2 11.8 %collective-permute-start = (bf16[2,2,256,256]{3,2,1,0:T(8,128)(2,1)S(1)}, bf16[2,2,256,256]{3,2,1,0:T(8,128)(2,1)S(1)}, u32[]{:S(2)}, u32[]{:S(2)}) collective-permute-start(bf16[2,2,256,256]{3,2,1,0:T(8,128)(2,1)S(1)} %bitcast.26), channel_id=1, source_target_pairs={{0,32},{32,64},{64,96},{96,128},{128,160},{160,192},{192,224},{224... | collective-permute-start | bytes 1572872 | tf_op jit(solution)/shard_map/ppermute | solution.py:303
  38.0 14.2 %collective-permute-start.1 = (bf16[2,2,256,256]{3,2,1,0:T(8,128)(2,1)S(1)}, bf16[2,2,256,256]{3,2,1,0:T(8,128)(2,1)}, u32[]{:S(2)}, u32[]{:S(2)}) collective-permute-start(bf16[2,2,256,256]{3,2,1,0:T(8,128)(2,1)S(1)} %bitcast.27), channel_id=1, source_target_pairs={{32,0},{64,32},{96,64},{128,96},{160,128},{192,160},{224,192},{256... | collective-permute-start | bytes 1572872 | tf_op jit(solution)/shard_map/ppermute | solution.py:306
  41.4 1.6 %copy-start.1 = (s32[2,2,6]{2,1,0:T(2,128)S(1)}, s32[2,2,6]{2,1,0:T(2,128)}, u32[]{:S(2)}) copy-start(s32[2,2,6]{2,1,0:T(2,128)} %param.7) | copy-start | bytes 292

commit v13 on v11

--- a/solution.py
+++ b/solution.py
@@ -254,8 +254,7 @@
         for part in range(block_rows):
             for load in range(loads):
                 source = (part * loads + load) * width
-                target = (load * block_rows + part) * width
-                out_ref[:, target:target + width] = summed[:, source:source + width]
+                out_ref[:, load, part * width:(part + 1) * width] = summed[:, source:source + width]
 
 
 def image_scatter(offsets, panel, stiff_blocks, dense, local_rows):
@@ -268,7 +267,7 @@
     shape = (classes // PAIR, chunk, PAIR, local_rows, columns)
     return pl.pallas_call(
         image_kernel,
-        out_shape=jax.ShapeDtypeStruct((local_rows, columns), jnp.float32),
+        out_shape=jax.ShapeDtypeStruct((local_rows, columns // (block_rows * width), block_rows * width), jnp.float32),
         grid_spec=pltpu.PrefetchScalarGridSpec(
             num_scalar_prefetch=1,
             grid=(block_rows, term_count),
@@ -277,7 +276,9 @@
                 pl.BlockSpec((1, 1, band, width, width), lambda b, k, offs: (k, b, 0, 0, 0)),
                 pl.BlockSpec((1, rows, rows), lambda b, k, offs: (k, 0, 0)),
             ],
-            out_specs=pl.BlockSpec((local_rows, columns), lambda b, k, offs: (0, 0)),
+            out_specs=pl.BlockSpec(
+                (local_rows, columns // (block_rows * width), block_rows * width), lambda b, k, offs: (0, 0, 0)
+            ),
             scratch_shapes=[
                 pltpu.VMEM(shape, jnp.float32),
                 pltpu.VMEM((chunk, local_rows, columns), jnp.bfloat16),

time: 83.7 us -> 83.7 us (level)
    reshape x1 -> x0, local copies, waits for them, and re-layouts: 1.4 us -> none  [per_device(): return summed.reshape(local_rows, load_count, cell_count)]
    unnamed x6 -> x7, local copies, waits for them, and re-layouts: 0.01 us -> 1.39 us
where the time goes in v13:
time: 83.7 us; the launch traced here: 83.2 us
  Pallas kernels  55.2 us (66%)
  starting transfers between devices  9.3 us (11%)
  waiting for transfers between devices  8.64 us (10%)
  local copies, waits for them, and re-layouts  7.16 us (9%)
  other arithmetic  2.37 us (3%)
    pallas_call x1, Pallas kernels, gather_term(): pl.pallas_call(gather_kernel, out_shape=jax.ShapeDtypeStruct((count,) + b...  28.1 us
    pallas_call x1, Pallas kernels, image_scatter(): pl.pallas_call(image_kernel, out_shape=jax.ShapeDtypeStruct((local_rows,...  27.2 us
    ppermute x1, waiting for transfers between devices, with_halo(): lax.ppermute(lax.slice_in_dim(block, 0, width, axis=dim), axis, backward)  8.12 us
    ppermute x1, starting transfers between devices, with_halo(): lax.ppermute(lax.slice_in_dim(block, block.shape[dim] - width, None, axis...  7.38 us
    convert_element_type x4, local copies, waits for them, and re-layouts, per_device(): dense = dense.astype(jnp.bfloat16)  2.54 us
    concatenate x1, other arithmetic, with_halo(): block = jnp.concatenate([low, block, high], axis=dim)  2.37 us
    ppermute x1, starting transfers between devices, with_halo(): lax.ppermute(lax.slice_in_dim(block, 0, width, axis=dim), axis, backward)  1.92 us
  transfers between devices with their start and end apart: 2, of which 2 were waited for; matrix products, arithmetic and copies ran while one was open for 4% of the time, Pallas kernels for 0%

profile of v13, /device:TPU:7, one launch (start us, length us, event | category | flops | bytes accessed | tf_op | source)
XLA Modules:
  0.0 83.2 jit_solution(5221255887312010283)
XLA Ops:
  0.0 0.0 copy-start
  0.0 0.0 copy-start.2
  0.0 1.4 %reshape.22.block_ref = bf16[16,512]{1,0:T(8,128)(2,1)} reshape(bf16[8,2,512]{2,1,0:T(2,128)(2,1)} %param.5) | data formatting | bytes 32768 | tf_op jit(solution)/shard_map/reshape | solution.py:321
  1.4 28.1 %shard_map.55 = bf16[32,16,512]{2,1,0:T(8,128)(2,1)} custom-call(bf16[16,512]{1,0:T(8,128)(2,1)} %reshape.22.block_ref), custom_call_target="tpu_custom_call" | custom-call | tf_op jit(solution)/shard_map/pallas_call | solution.py:94
  29.5 1.2 %reshape.23 = bf16[32,8,2,2,256]{4,3,2,1,0:T(2,128)(2,1)S(1)} reshape(bf16[32,16,512]{2,1,0:T(8,128)(2,1)} %shard_map.55) | data formatting | bytes 1048576 | tf_op jit(solution)/shard_map/reshape | solution.py:322
  30.7 0.1 copy.21
  30.7 7.4 %collective-permute-start = (bf16[2,2,256,256]{3,2,1,0:T(8,128)(2,1)S(1)}, bf16[2,2,256,256]{3,2,1,0:T(8,128)(2,1)S(1)}, u32[]{:S(2)}, u32[]{:S(2)}) collective-permute-start(bf16[2,2,256,256]{3,2,1,0:T(8,128)(2,1)S(1)} %bitcast.25), channel_id=1, source_target_pairs={{0,32},{32,64},{64,96},{96,128},{128,160},{160,192},{192,224},{224... | collective-permute-start | bytes 1572872 | tf_op jit(solution)/shard_map/ppermute | solution.py:303
  38.1 1.9 %collective-permute-start.1 = (bf16[2,2,256,256]{3,2,1,0:T(8,128)(2,1)S(1)}, bf16[2,2,256,256]{3,2,1,0:T(8,128)(2,1)}, u32[]{:S(2)}, u32[]{:S(2)}) collective-permute-start(bf16[2,2,256,256]{3,2,1,0:T(8,128)(2,1)S(1)} %bitcast.26), channel_id=1, source_target_pairs={{32,0},{64,32},{96,64},{128,96},{160,128},{192,160},{224,192},{256... | collective-permute-start | bytes 1572872 | tf_op jit(solution)/shard_map/ppermute | solution.py:306
  40.0 0.0 copy-done.2
  40.1 0.0 copy-done
  40.1 0.4 fusion
  40.5 1.0 %copy.10 = bf16[2,8,32,8,32]{2,1,4,3,0:T(8,128)(2,1)S(1)} copy(bf16[2,8,32,8,32]{4,1,2,3,0:T(8,128)(2,1)S(1)} %fusion) | data formatting | bytes 524288 | tf_op jit(solution)/shard_map/convert_element_type | solution.py:333
  41.5 0.0 copy-start.1
  41.5 0.7 convert_element_type.16
  42.3 0.8 %copy.12.triple_ref = bf16[2,256,256]{2,1,0:T(8,128)(2,1)} copy(bf16[2,256,256]{1,2,0:T(8,128)(2,1)S(1)} %bitcast.29) | data formatting | bytes 524288 | tf_op jit(solution)/shard_map/convert_element_type | solution.py:333
  43.1 0.0 copy-done.1
  43.1 0.6 reshape.21.offs_ref
  43.7 0.5 collective-permute-done
  44.2 8.1 %collective-permute-done.1 = bf16[2,2,256,256]{3,2,1,0:T(8,128)(2,1)} collective-permute-done((bf16[2,2,256,256]{3,2,1,0:T(8,128)(2,1)S(1)}, bf16[2,2,256,256]{3,2,1,0:T(8,128)(2,1)}, u32[]{:S(2)}, u32[]{:S(2)}) %collective-permute-start.1) | collective-permute-done | bytes 524320 | tf_op jit(solution)/shard_map/ppermute | solution.py:306
  52.3 2.4 %pad_maximum_fusion.panel_ref = bf16[6,512,256]{2,1,0:T(8,128)(2,1)} fusion(bf16[2,512,256]{2,1,0:T(8,128)(2,1)} %bitcast.5, bf16[2,512,256]{2,1,0:T(8,128)(2,1)S(1)} %bitcast.27, bf16[2,512,256]{2,1,0:T(8,128)(2,1)S(1)} %bitcast.30), kind=kLoop, calls=%fused_computation | loop fusion | flops 1572864 | bytes 3145728 | tf_op jit(solution)/shard_map/concatenate | solution.py:307
  54.7 27.2 %shard_map.56 = f32[8,2,512]{2,1,0:T(2,128)} custom-call(s32[24]{0:T(128)} %reshape.21.offs_ref, bf16[6,512,256]{2,1,0:T(8,128)(2,1)} %pad_maximum_fusion.panel_ref, bf16[2,2,6,256,256]{4,3,2,1,0:T(8,128)(2,1)} %stiff_ref.1, bf16[2,256,256]{2,1,0:T(8,128)(2,1)} %copy.12.triple_ref), custom_call_target="tpu_custom_call" | custom-call | tf_op jit(solution)/shard_map/pallas_call | solution.py:268
  81.9 1.4 %copy.23 = f32[8,2,512]{2,1,0:T(2,128)} copy(f32[8,2,512]{2,1,0:T(2,128)} %shard_map.56) | data formatting | bytes 65536
  (3 shorter events, 0.0 us)
Async XLA Ops:
  0.0 40.1 %copy-start = (bf16[2,24,32,32]{3,2,1,0:T(8,128)(2,1)S(1)}, bf16[2,24,32,32]{3,2,1,0:T(8,128)(2,1)}, u32[]{:S(2)}) copy-start(bf16[2,24,32,32]{3,2,1,0:T(8,128)(2,1)} %param.8) | copy-start | bytes 294916
  0.0 40.0 %copy-start.2 = (s32[2,24,2]{1,2,0:T(2,128)S(1)}, s32[2,24,2]{1,2,0:T(2,128)}, u32[]{:S(2)}) copy-start(s32[2,24,2]{1,2,0:T(2,128)} %param.9) | copy-start | bytes 1156
  30.7 13.5 %collective-permute-start = (bf16[2,2,256,256]{3,2,1,0:T(8,128)(2,1)S(1)}, bf16[2,2,256,256]{3,2,1,0:T(8,128)(2,1)S(1)}, u32[]{:S(2)}, u32[]{:S(2)}) collective-permute-start(bf16[2,2,256,256]{3,2,1,0:T(8,128)(2,1)S(1)} %bitcast.25), channel_id=1, source_target_pairs={{0,32},{32,64},{64,96},{96,128},{128,160},{160,192},{192,224},{224... | collective-permute-start | bytes 1572872 | tf_op jit(solution)/shard_map/ppermute | solution.py:303
  38.1 14.2 %collective-permute-start.1 = (bf16[2,2,256,256]{3,2,1,0:T(8,128)(2,1)S(1)}, bf16[2,2,256,256]{3,2,1,0:T(8,128)(2,1)}, u32[]{:S(2)}, u32[]{:S(2)}) collective-permute-start(bf16[2,2,256,256]{3,2,1,0:T(8,128)(2,1)S(1)} %bitcast.26), channel_id=1, source_target_pairs={{32,0},{64,32},{96,64},{128,96},{160,128},{192,160},{224,192},{256... | collective-permute-start | bytes 1572872 | tf_op jit(solution)/shard_map/ppermute | solution.py:306
  41.5 1.6 %copy-start.1 = (s32[2,2,6]{2,1,0:T(2,128)S(1)}, s32[2,2,6]{2,1,0:T(2,128)}, u32[]{:S(2)}) copy-start(s32[2,2,6]{2,1,0:T(2,128)} %param.7) | copy-start | bytes 292

commit v14 on v11

--- a/solution.py
+++ b/solution.py
@@ -211,6 +211,22 @@
 
     @pl.when((term == term_count - 1) & (block == block_rows - 1))
     def _():
+        def far_copy(step, part, inbound):
+            cols = pl.ds(part * half, half)
+            if inbound:
+                source = lax.rem(stride + chunk - step, chunk)
+                return pltpu.make_async_remote_copy(
+                    far_src.at[source, :, cols], far_slots.at[source, :, cols],
+                    send_far.at[part, step], recv_far.at[part, source],
+                    device_id=(row, term_device(lane, source, chunk)), device_id_type=MESH_ID,
+                )
+            target = lax.rem(stride + step, chunk)
+            return pltpu.make_async_remote_copy(
+                far_src.at[target, :, cols], far_slots.at[stride, :, cols],
+                send_far.at[part, step], recv_far.at[part, stride],
+                device_id=(row, far_peer(step)), device_id_type=MESH_ID,
+            )
+
         for part in range(block_rows):
             cols = pl.ds(part * half, half)
 
@@ -221,41 +237,29 @@
                 return total + near_slots[source, :, :, cols]
 
             own = total_ref[lane // PAIR, :, lane % PAIR, :, cols]
-            class_sum[:, :, cols] = lax.fori_loop(1, classes, near_finish, own)
-
-        far_src[...] = class_sum[...].astype(far_src.dtype)
-
-        def far_out(step):
-            target = lax.rem(stride + step, chunk)
-            return pltpu.make_async_remote_copy(
-                far_src.at[target], far_slots.at[stride], send_far.at[step], recv_far.at[stride],
-                device_id=(row, far_peer(step)), device_id_type=MESH_ID,
-            )
-
-        def far_in(step):
-            source = lax.rem(stride + chunk - step, chunk)
-            return pltpu.make_async_remote_copy(
-                far_src.at[source], far_slots.at[source], send_far.at[step], recv_far.at[source],
-                device_id=(row, term_device(lane, source, chunk)), device_id_type=MESH_ID,
-            )
-
-        def far_start(step, carry):
-            far_out(step).start()
-            return carry
-
-        def far_finish(step, total):
-            far_out(step).wait_send()
-            far_in(step).wait_recv()
-            source = lax.rem(stride + chunk - step, chunk)
-            return total + far_slots[source].astype(jnp.float32)
-
-        lax.fori_loop(1, chunk, far_start, 0)
-        summed = lax.fori_loop(1, chunk, far_finish, class_sum[stride])
+            part_sum = lax.fori_loop(1, classes, near_finish, own)
+            class_sum[:, :, cols] = part_sum
+            far_src[:, :, cols] = part_sum.astype(far_src.dtype)
+
+            def far_start(step, carry):
+                far_copy(step, part, False).start()
+                return carry
+
+            lax.fori_loop(1, chunk, far_start, 0)
+
         for part in range(block_rows):
+            cols = pl.ds(part * half, half)
+
+            def far_finish(step, total):
+                far_copy(step, part, False).wait_send()
+                far_copy(step, part, True).wait_recv()
+                source = lax.rem(stride + chunk - step, chunk)
+                return total + far_slots[source, :, cols].astype(jnp.float32)
+
+            summed = lax.fori_loop(1, chunk, far_finish, class_sum[stride, :, cols])
             for load in range(loads):
-                source = (part * loads + load) * width
                 target = (load * block_rows + part) * width
-                out_ref[:, target:target + width] = summed[:, source:source + width]
+                out_ref[:, target:target + width] = summed[:, load * width:(load + 1) * width]
 
 
 def image_scatter(offsets, panel, stiff_blocks, dense, local_rows):
@@ -286,8 +290,8 @@
                 pltpu.VMEM((chunk, local_rows, columns), jnp.bfloat16),
                 pltpu.SemaphoreType.DMA((block_rows, classes)),
                 pltpu.SemaphoreType.DMA((block_rows, classes)),
-                pltpu.SemaphoreType.DMA((chunk,)),
-                pltpu.SemaphoreType.DMA((chunk,)),
+                pltpu.SemaphoreType.DMA((block_rows, chunk)),
+                pltpu.SemaphoreType.DMA((block_rows, chunk)),
             ],
         ),
         compiler_params=pltpu.CompilerParams(collective_id=1, has_side_effects=True),

time: 83.7 us -> 83.7 us (level); the launches traced: 83.3 us -> 82.3 us
  Pallas kernels: 55.2 us -> 54.3 us
    pallas_call x1, Pallas kernels: 27.1 us -> 26.2 us  [image_scatter(): pl.pallas_call(image_kernel, out_shape=jax.ShapeDtypeStruct((local_rows,...]
where the time goes in v14:
time: 83.7 us; the launch traced here: 82.3 us
  Pallas kernels  54.3 us (65%)
  starting transfers between devices  9.3 us (11%)
  waiting for transfers between devices  8.64 us (10%)
  local copies, waits for them, and re-layouts  7.19 us (9%)
  other arithmetic  2.37 us (3%)
    pallas_call x1, Pallas kernels, gather_term(): pl.pallas_call(gather_kernel, out_shape=jax.ShapeDtypeStruct((count,) + b...  28.1 us
    pallas_call x1, Pallas kernels, image_scatter(): pl.pallas_call(image_kernel, out_shape=jax.ShapeDtypeStruct((local_rows,...  26.2 us
    ppermute x1, waiting for transfers between devices, with_halo(): lax.ppermute(lax.slice_in_dim(block, 0, width, axis=dim), axis, backward)  8.12 us
    ppermute x1, starting transfers between devices, with_halo(): lax.ppermute(lax.slice_in_dim(block, block.shape[dim] - width, None, axis...  7.38 us
    convert_element_type x4, local copies, waits for them, and re-layouts, per_device(): dense = dense.astype(jnp.bfloat16)  2.54 us
    concatenate x1, other arithmetic, with_halo(): block = jnp.concatenate([low, block, high], axis=dim)  2.37 us
    ppermute x1, starting transfers between devices, with_halo(): lax.ppermute(lax.slice_in_dim(block, 0, width, axis=dim), axis, backward)  1.92 us
  transfers between devices with their start and end apart: 2, of which 2 were waited for; matrix products, arithmetic and copies ran while one was open for 4% of the time, Pallas kernels for 0%

profile of v14, /device:TPU:7, one launch (start us, length us, event | category | flops | bytes accessed | tf_op | source)
XLA Modules:
  0.0 82.3 jit_solution(6925025758468746870)
XLA Ops:
  0.0 0.0 copy-start
  0.0 0.0 copy-start.2
  0.0 1.4 %reshape.25.block_ref = bf16[16,512]{1,0:T(8,128)(2,1)} reshape(bf16[8,2,512]{2,1,0:T(2,128)(2,1)} %param.5) | data formatting | bytes 32768 | tf_op jit(solution)/shard_map/reshape | solution.py:324
  1.4 28.1 %shard_map.55 = bf16[32,16,512]{2,1,0:T(8,128)(2,1)} custom-call(bf16[16,512]{1,0:T(8,128)(2,1)} %reshape.25.block_ref), custom_call_target="tpu_custom_call" | custom-call | tf_op jit(solution)/shard_map/pallas_call | solution.py:94
  29.5 1.2 %reshape.26 = bf16[32,8,2,2,256]{4,3,2,1,0:T(2,128)(2,1)S(1)} reshape(bf16[32,16,512]{2,1,0:T(8,128)(2,1)} %shard_map.55) | data formatting | bytes 1048576 | tf_op jit(solution)/shard_map/reshape | solution.py:325
  30.7 0.1 copy.23
  30.7 7.4 %collective-permute-start = (bf16[2,2,256,256]{3,2,1,0:T(8,128)(2,1)S(1)}, bf16[2,2,256,256]{3,2,1,0:T(8,128)(2,1)S(1)}, u32[]{:S(2)}, u32[]{:S(2)}) collective-permute-start(bf16[2,2,256,256]{3,2,1,0:T(8,128)(2,1)S(1)} %bitcast.26), channel_id=1, source_target_pairs={{0,32},{32,64},{64,96},{96,128},{128,160},{160,192},{192,224},{224... | collective-permute-start | bytes 1572872 | tf_op jit(solution)/shard_map/ppermute | solution.py:306
  38.1 1.9 %collective-permute-start.1 = (bf16[2,2,256,256]{3,2,1,0:T(8,128)(2,1)S(1)}, bf16[2,2,256,256]{3,2,1,0:T(8,128)(2,1)}, u32[]{:S(2)}, u32[]{:S(2)}) collective-permute-start(bf16[2,2,256,256]{3,2,1,0:T(8,128)(2,1)S(1)} %bitcast.27), channel_id=1, source_target_pairs={{32,0},{64,32},{96,64},{128,96},{160,128},{192,160},{224,192},{256... | collective-permute-start | bytes 1572872 | tf_op jit(solution)/shard_map/ppermute | solution.py:309
  40.0 0.0 copy-done.2
  40.1 0.0 copy-done
  40.1 0.4 fusion
  40.5 1.0 %copy.11 = bf16[2,8,32,8,32]{2,1,4,3,0:T(8,128)(2,1)S(1)} copy(bf16[2,8,32,8,32]{4,1,2,3,0:T(8,128)(2,1)S(1)} %fusion) | data formatting | bytes 524288 | tf_op jit(solution)/shard_map/convert_element_type | solution.py:336
  41.5 0.0 copy-start.1
  41.5 0.7 convert_element_type.16
  42.3 0.8 %copy.13.triple_ref = bf16[2,256,256]{2,1,0:T(8,128)(2,1)} copy(bf16[2,256,256]{1,2,0:T(8,128)(2,1)S(1)} %bitcast.30) | data formatting | bytes 524288 | tf_op jit(solution)/shard_map/convert_element_type | solution.py:336
  43.1 0.0 copy-done.1
  43.1 0.6 reshape.24.offs_ref
  43.7 0.5 collective-permute-done
  44.2 8.1 %collective-permute-done.1 = bf16[2,2,256,256]{3,2,1,0:T(8,128)(2,1)} collective-permute-done((bf16[2,2,256,256]{3,2,1,0:T(8,128)(2,1)S(1)}, bf16[2,2,256,256]{3,2,1,0:T(8,128)(2,1)}, u32[]{:S(2)}, u32[]{:S(2)}) %collective-permute-start.1) | collective-permute-done | bytes 524320 | tf_op jit(solution)/shard_map/ppermute | solution.py:309
  52.3 2.4 %pad_maximum_fusion.panel_ref = bf16[6,512,256]{2,1,0:T(8,128)(2,1)} fusion(bf16[2,512,256]{2,1,0:T(8,128)(2,1)} %bitcast.5, bf16[2,512,256]{2,1,0:T(8,128)(2,1)S(1)} %bitcast.28, bf16[2,512,256]{2,1,0:T(8,128)(2,1)S(1)} %bitcast.31), kind=kLoop, calls=%fused_computation | loop fusion | flops 1572864 | bytes 3145728 | tf_op jit(solution)/shard_map/concatenate | solution.py:310
  54.7 26.2 %shard_map.56 = f32[8,1024]{1,0:T(8,128)} custom-call(s32[24]{0:T(128)} %reshape.24.offs_ref, bf16[6,512,256]{2,1,0:T(8,128)(2,1)} %pad_maximum_fusion.panel_ref, bf16[2,2,6,256,256]{4,3,2,1,0:T(8,128)(2,1)} %stiff_ref.1, bf16[2,256,256]{2,1,0:T(8,128)(2,1)} %copy.13.triple_ref), custom_call_target="tpu_custom_call" | custom-call | tf_op jit(solution)/shard_map/pallas_call | solution.py:273
  80.9 1.4 %copy.14 = f32[8,2,512]{2,1,0:T(2,128)} copy(f32[8,2,512]{2,0,1:T(8,128)} %bitcast.32) | data formatting | bytes 65536 | tf_op jit(solution)/shard_map/reshape | solution.py:338
  (3 shorter events, 0.0 us)
Async XLA Ops:
  0.0 40.1 %copy-start = (bf16[2,24,32,32]{3,2,1,0:T(8,128)(2,1)S(1)}, bf16[2,24,32,32]{3,2,1,0:T(8,128)(2,1)}, u32[]{:S(2)}) copy-start(bf16[2,24,32,32]{3,2,1,0:T(8,128)(2,1)} %param.8) | copy-start | bytes 294916
  0.0 40.0 %copy-start.2 = (s32[2,24,2]{1,2,0:T(2,128)S(1)}, s32[2,24,2]{1,2,0:T(2,128)}, u32[]{:S(2)}) copy-start(s32[2,24,2]{1,2,0:T(2,128)} %param.9) | copy-start | bytes 1156
  30.7 13.5 %collective-permute-start = (bf16[2,2,256,256]{3,2,1,0:T(8,128)(2,1)S(1)}, bf16[2,2,256,256]{3,2,1,0:T(8,128)(2,1)S(1)}, u32[]{:S(2)}, u32[]{:S(2)}) collective-permute-start(bf16[2,2,256,256]{3,2,1,0:T(8,128)(2,1)S(1)} %bitcast.26), channel_id=1, source_target_pairs={{0,32},{32,64},{64,96},{96,128},{128,160},{160,192},{192,224},{224... | collective-permute-start | bytes 1572872 | tf_op jit(solution)/shard_map/ppermute | solution.py:306
  38.1 14.2 %collective-permute-start.1 = (bf16[2,2,256,256]{3,2,1,0:T(8,128)(2,1)S(1)}, bf16[2,2,256,256]{3,2,1,0:T(8,128)(2,1)}, u32[]{:S(2)}, u32[]{:S(2)}) collective-permute-start(bf16[2,2,256,256]{3,2,1,0:T(8,128)(2,1)S(1)} %bitcast.27), channel_id=1, source_target_pairs={{32,0},{64,32},{96,64},{128,96},{160,128},{192,160},{224,192},{256... | collective-permute-start | bytes 1572872 | tf_op jit(solution)/shard_map/ppermute | solution.py:309
  41.5 1.6 %copy-start.1 = (s32[2,2,6]{2,1,0:T(2,128)S(1)}, s32[2,2,6]{2,1,0:T(2,128)}, u32[]{:S(2)}) copy-start(s32[2,2,6]{2,1,0:T(2,128)} %param.7) | copy-start | bytes 292

commit v15 on v11

--- a/solution.py
+++ b/solution.py
@@ -12,8 +12,11 @@
 PAIR = 2
 
 
-def gather_kernel(block_ref, out_ref, local_sem, send_near, recv_near, send_far, recv_far):
+def gather_kernel(block_ref, out_ref, flat_ref, local_sem, send_near, recv_near, send_far, recv_far):
     count = out_ref.shape[0]
+    rows, loads, cells = block_ref.shape
+    for load in range(loads):
+        flat_ref[load * rows:(load + 1) * rows, :] = block_ref[:, load, :]
     chunk = count // CLASSES
     row, stride, lane, far_peer, near_peer = scatter_peers(chunk, CLASSES)
     barrier = pltpu.get_barrier_semaphore()
@@ -31,19 +34,19 @@
     pl.semaphore_wait(barrier, chunk + CLASSES - 2)
 
     mine = lane * chunk + stride
-    local = pltpu.make_async_copy(block_ref, out_ref.at[mine], local_sem)
+    local = pltpu.make_async_copy(flat_ref, out_ref.at[mine], local_sem)
     local.start()
 
     def far_out(step):
         return pltpu.make_async_remote_copy(
-            block_ref, out_ref.at[mine], send_far.at[step], recv_far.at[stride],
+            flat_ref, out_ref.at[mine], send_far.at[step], recv_far.at[stride],
             device_id=(row, far_peer(step)), device_id_type=MESH_ID,
         )
 
     def far_in(step):
         source = lax.rem(stride + chunk - step, chunk)
         return pltpu.make_async_remote_copy(
-            block_ref, out_ref.at[lane * chunk + source], send_far.at[step], recv_far.at[source],
+            flat_ref, out_ref.at[lane * chunk + source], send_far.at[step], recv_far.at[source],
             device_id=(row, term_device(lane, source, chunk)), device_id_type=MESH_ID,
         )
 
@@ -93,10 +96,11 @@
     count = lax.axis_size("term")
     return pl.pallas_call(
         gather_kernel,
-        out_shape=jax.ShapeDtypeStruct((count,) + block.shape, block.dtype),
+        out_shape=jax.ShapeDtypeStruct((count, block.shape[0] * block.shape[1], block.shape[2]), block.dtype),
         in_specs=[pl.BlockSpec(memory_space=pltpu.VMEM)],
         out_specs=pl.BlockSpec(memory_space=pltpu.VMEM),
         scratch_shapes=[
+            pltpu.VMEM((block.shape[0] * block.shape[1], block.shape[2]), block.dtype),
             pltpu.SemaphoreType.DMA(()),
             pltpu.SemaphoreType.DMA((CLASSES,)),
             pltpu.SemaphoreType.DMA((CLASSES,)),
@@ -317,9 +321,9 @@
     groups = lax.axis_size("term")
     total_rows = local_rows * groups
     rim_cells = 2 * block_width
-    gathered = gather_term(chaos_field.reshape(local_rows * load_count, cell_count))
-    panel = gathered.reshape(groups, local_rows, load_count, block_rows, block_width)
-    panel = panel.transpose(3, 2, 0, 1, 4).reshape(block_rows, load_count, total_rows, block_width)
+    gathered = gather_term(chaos_field)
+    panel = gathered.reshape(groups, load_count, local_rows, block_rows, block_width)
+    panel = panel.transpose(3, 1, 0, 2, 4).reshape(block_rows, load_count, total_rows, block_width)
     extended = with_halo(panel, (("space", 0),), rim_cells // block_width)
     extended = extended.reshape(block_rows + 4, load_count * total_rows, block_width)
     block_size = triple_blocks.shape[2]

time: 83.7 us -> 82.6 us (0.987)
  local copies, waits for them, and re-layouts: 7.19 us -> 5.63 us
    reshape x3 -> x1, local copies, waits for them, and re-layouts: 2.63 us -> 1.08 us  [per_device(): gathered.reshape(groups, load_count, local_rows, block_rows, block_width)]
where the time goes in v15:
time: 82.6 us; the launch traced here: 82.2 us
  Pallas kernels  55.9 us (68%)
  starting transfers between devices  9.13 us (11%)
  waiting for transfers between devices  8.64 us (10%)
  local copies, waits for them, and re-layouts  5.63 us (7%)
  other arithmetic  2.37 us (3%)
    pallas_call x1, Pallas kernels, gather_term(): pl.pallas_call(gather_kernel, out_shape=jax.ShapeDtypeStruct((count, bloc...  28.7 us
    pallas_call x1, Pallas kernels, image_scatter(): pl.pallas_call(image_kernel, out_shape=jax.ShapeDtypeStruct((local_rows,...  27.2 us
    ppermute x1, waiting for transfers between devices, with_halo(): lax.ppermute(lax.slice_in_dim(block, 0, width, axis=dim), axis, backward)  8.12 us
    ppermute x1, starting transfers between devices, with_halo(): lax.ppermute(lax.slice_in_dim(block, block.shape[dim] - width, None, axis...  7.21 us
    convert_element_type x4, local copies, waits for them, and re-layouts, per_device(): dense = dense.astype(jnp.bfloat16)  2.54 us
    concatenate x1, other arithmetic, with_halo(): block = jnp.concatenate([low, block, high], axis=dim)  2.37 us
    ppermute x1, starting transfers between devices, with_halo(): lax.ppermute(lax.slice_in_dim(block, 0, width, axis=dim), axis, backward)  1.92 us
  transfers between devices with their start and end apart: 2, of which 2 were waited for; matrix products, arithmetic and copies ran while one was open for 4% of the time, Pallas kernels for 0%

profile of v15, /device:TPU:7, one launch (start us, length us, event | category | flops | bytes accessed | tf_op | source)
XLA Modules:
  0.0 82.2 jit_solution(13063481798866625018)
XLA Ops:
  0.0 0.0 copy-start
  0.0 0.0 copy-start.2
  0.0 28.7 %shard_map.55 = bf16[32,16,512]{2,1,0:T(8,128)(2,1)} custom-call(bf16[8,2,512]{2,1,0:T(2,128)(2,1)} %block_ref.1), custom_call_target="tpu_custom_call" | custom-call | tf_op jit(solution)/shard_map/pallas_call | solution.py:97
  28.7 1.1 %copy.23 = bf16[32,2,8,2,256]{4,2,0,1,3:T(8,128)(2,1)S(1)} copy(bf16[32,2,8,2,256]{4,2,3,1,0:T(8,128)(2,1)} %bitcast.27) | data formatting | bytes 1048576 | tf_op jit(solution)/shard_map/reshape | solution.py:325
  29.8 7.2 %collective-permute-start = (bf16[2,2,256,256]{3,2,1,0:T(8,128)(2,1)S(1)}, bf16[2,2,256,256]{3,2,1,0:T(8,128)(2,1)S(1)}, u32[]{:S(2)}, u32[]{:S(2)}) collective-permute-start(bf16[2,2,256,256]{3,2,1,0:T(8,128)(2,1)S(1)} %bitcast.28), channel_id=1, source_target_pairs={{0,32},{32,64},{64,96},{96,128},{128,160},{160,192},{192,224},{224... | collective-permute-start | bytes 1572872 | tf_op jit(solution)/shard_map/ppermute | solution.py:306
  37.0 1.9 %collective-permute-start.1 = (bf16[2,2,256,256]{3,2,1,0:T(8,128)(2,1)S(1)}, bf16[2,2,256,256]{3,2,1,0:T(8,128)(2,1)}, u32[]{:S(2)}, u32[]{:S(2)}) collective-permute-start(bf16[2,2,256,256]{3,2,1,0:T(8,128)(2,1)S(1)} %bitcast.29), channel_id=1, source_target_pairs={{32,0},{64,32},{96,64},{128,96},{160,128},{192,160},{224,192},{256... | collective-permute-start | bytes 1572872 | tf_op jit(solution)/shard_map/ppermute | solution.py:309
  38.9 0.0 copy-done.2
  39.0 0.0 copy-done
  39.0 0.4 fusion
  39.4 1.0 %copy.11 = bf16[2,8,32,8,32]{2,1,4,3,0:T(8,128)(2,1)S(1)} copy(bf16[2,8,32,8,32]{4,1,2,3,0:T(8,128)(2,1)S(1)} %fusion) | data formatting | bytes 524288 | tf_op jit(solution)/shard_map/convert_element_type | solution.py:336
  40.4 0.0 copy-start.1
  40.4 0.7 convert_element_type.16
  41.1 0.8 %copy.13.triple_ref = bf16[2,256,256]{2,1,0:T(8,128)(2,1)} copy(bf16[2,256,256]{1,2,0:T(8,128)(2,1)S(1)} %bitcast.32) | data formatting | bytes 524288 | tf_op jit(solution)/shard_map/convert_element_type | solution.py:336
  42.0 0.0 copy-done.1
  42.0 0.6 reshape.21.offs_ref
  42.6 0.5 collective-permute-done
  43.1 8.1 %collective-permute-done.1 = bf16[2,2,256,256]{3,2,1,0:T(8,128)(2,1)} collective-permute-done((bf16[2,2,256,256]{3,2,1,0:T(8,128)(2,1)S(1)}, bf16[2,2,256,256]{3,2,1,0:T(8,128)(2,1)}, u32[]{:S(2)}, u32[]{:S(2)}) %collective-permute-start.1) | collective-permute-done | bytes 524320 | tf_op jit(solution)/shard_map/ppermute | solution.py:309
  51.2 2.4 %pad_maximum_fusion.panel_ref = bf16[6,512,256]{2,1,0:T(8,128)(2,1)} fusion(bf16[2,512,256]{2,1,0:T(8,128)(2,1)} %bitcast.6, bf16[2,512,256]{2,1,0:T(8,128)(2,1)S(1)} %bitcast.30, bf16[2,512,256]{2,1,0:T(8,128)(2,1)S(1)} %bitcast.33), kind=kLoop, calls=%fused_computation | loop fusion | flops 1572864 | bytes 3145728 | tf_op jit(solution)/shard_map/concatenate | solution.py:310
  53.6 27.2 %shard_map.56 = f32[8,1024]{1,0:T(8,128)} custom-call(s32[24]{0:T(128)} %reshape.21.offs_ref, bf16[6,512,256]{2,1,0:T(8,128)(2,1)} %pad_maximum_fusion.panel_ref, bf16[2,2,6,256,256]{4,3,2,1,0:T(8,128)(2,1)} %stiff_ref.1, bf16[2,256,256]{2,1,0:T(8,128)(2,1)} %copy.13.triple_ref), custom_call_target="tpu_custom_call" | custom-call | tf_op jit(solution)/shard_map/pallas_call | solution.py:273
  80.8 1.4 %copy.14 = f32[8,2,512]{2,1,0:T(2,128)} copy(f32[8,2,512]{2,0,1:T(8,128)} %bitcast.34) | data formatting | bytes 65536 | tf_op jit(solution)/shard_map/reshape | solution.py:338
  (3 shorter events, 0.0 us)
Async XLA Ops:
  0.0 39.0 %copy-start = (bf16[2,24,32,32]{3,2,1,0:T(8,128)(2,1)S(1)}, bf16[2,24,32,32]{3,2,1,0:T(8,128)(2,1)}, u32[]{:S(2)}) copy-start(bf16[2,24,32,32]{3,2,1,0:T(8,128)(2,1)} %param.8) | copy-start | bytes 294916
  0.0 38.9 %copy-start.2 = (s32[2,24,2]{1,2,0:T(2,128)S(1)}, s32[2,24,2]{1,2,0:T(2,128)}, u32[]{:S(2)}) copy-start(s32[2,24,2]{1,2,0:T(2,128)} %param.9) | copy-start | bytes 1156
  29.8 13.3 %collective-permute-start = (bf16[2,2,256,256]{3,2,1,0:T(8,128)(2,1)S(1)}, bf16[2,2,256,256]{3,2,1,0:T(8,128)(2,1)S(1)}, u32[]{:S(2)}, u32[]{:S(2)}) collective-permute-start(bf16[2,2,256,256]{3,2,1,0:T(8,128)(2,1)S(1)} %bitcast.28), channel_id=1, source_target_pairs={{0,32},{32,64},{64,96},{96,128},{128,160},{160,192},{192,224},{224... | collective-permute-start | bytes 1572872 | tf_op jit(solution)/shard_map/ppermute | solution.py:306
  37.0 14.2 %collective-permute-start.1 = (bf16[2,2,256,256]{3,2,1,0:T(8,128)(2,1)S(1)}, bf16[2,2,256,256]{3,2,1,0:T(8,128)(2,1)}, u32[]{:S(2)}, u32[]{:S(2)}) collective-permute-start(bf16[2,2,256,256]{3,2,1,0:T(8,128)(2,1)S(1)} %bitcast.29), channel_id=1, source_target_pairs={{32,0},{64,32},{96,64},{128,96},{160,128},{192,160},{224,192},{256... | collective-permute-start | bytes 1572872 | tf_op jit(solution)/shard_map/ppermute | solution.py:309
  40.4 1.6 %copy-start.1 = (s32[2,2,6]{2,1,0:T(2,128)S(1)}, s32[2,2,6]{2,1,0:T(2,128)}, u32[]{:S(2)}) copy-start(s32[2,2,6]{2,1,0:T(2,128)} %param.7) | copy-start | bytes 292

commit v16 on v15

--- a/solution.py
+++ b/solution.py
@@ -12,7 +12,8 @@
 PAIR = 2
 
 
-def gather_kernel(block_ref, out_ref, flat_ref, local_sem, send_near, recv_near, send_far, recv_far):
+def gather_kernel(block_ref, panel_ref, out_ref, flat_ref, local_sem, send_near, recv_near, send_far,
+                  recv_far):
     count = out_ref.shape[0]
     rows, loads, cells = block_ref.shape
     for load in range(loads):
@@ -91,15 +92,26 @@
     lax.fori_loop(1, CLASSES, near_start, 0)
     lax.fori_loop(1, CLASSES, near_finish, 0)
 
-
-def gather_term(block):
+    width = panel_ref.shape[-1]
+    for slot in range(count):
+        for load in range(loads):
+            for block in range(panel_ref.shape[0]):
+                panel_ref[block, load, slot * rows:(slot + 1) * rows, :] = out_ref[
+                    slot, load * rows:(load + 1) * rows, block * width:(block + 1) * width
+                ]
+
+
+def gather_term(block, width):
     count = lax.axis_size("term")
     return pl.pallas_call(
         gather_kernel,
-        out_shape=jax.ShapeDtypeStruct((count, block.shape[0] * block.shape[1], block.shape[2]), block.dtype),
+        out_shape=jax.ShapeDtypeStruct(
+            (block.shape[2] // width, block.shape[1], count * block.shape[0], width), block.dtype
+        ),
         in_specs=[pl.BlockSpec(memory_space=pltpu.VMEM)],
         out_specs=pl.BlockSpec(memory_space=pltpu.VMEM),
         scratch_shapes=[
+            pltpu.VMEM((count, block.shape[0] * block.shape[1], block.shape[2]), block.dtype),
             pltpu.VMEM((block.shape[0] * block.shape[1], block.shape[2]), block.dtype),
             pltpu.SemaphoreType.DMA(()),
             pltpu.SemaphoreType.DMA((CLASSES,)),
@@ -321,9 +333,7 @@
     groups = lax.axis_size("term")
     total_rows = local_rows * groups
     rim_cells = 2 * block_width
-    gathered = gather_term(chaos_field)
-    panel = gathered.reshape(groups, load_count, local_rows, block_rows, block_width)
-    panel = panel.transpose(3, 1, 0, 2, 4).reshape(block_rows, load_count, total_rows, block_width)
+    panel = gather_term(chaos_field, block_width)
     extended = with_halo(panel, (("space", 0),), rim_cells // block_width)
     extended = extended.reshape(block_rows + 4, load_count * total_rows, block_width)
     block_size = triple_blocks.shape[2]

time: 82.6 us -> 80.6 us (0.976)
  other arithmetic: 2.37 us -> 1.33 us
    reshape x1 -> x0, local copies, waits for them, and re-layouts: 1.08 us -> none  [per_device(): gathered.reshape(groups, load_count, local_rows, block_rows, block_width)]
    concatenate x1, other arithmetic: 2.37 us -> 1.33 us  [with_halo(): block = jnp.concatenate([low, block, high], axis=dim)]
  transfers between devices with their start and end apart: 2 -> 2, of which waited for: 2 -> 2; matrix products, arithmetic and copies ran while one was open for 4% -> 5% of each run, Pallas kernels for 0% -> 0%
where the time goes in v16:
time: 80.6 us; the launch traced here: 80.3 us
  Pallas kernels  56 us (69%)
  starting transfers between devices  9.13 us (11%)
  waiting for transfers between devices  8.01 us (10%)
  local copies, waits for them, and re-layouts  5.3 us (7%)
  other arithmetic  1.33 us (2%)
    pallas_call x1, Pallas kernels, gather_term(): pl.pallas_call(gather_kernel, out_shape=jax.ShapeDtypeStruct((block.shape...  28.7 us
    pallas_call x1, Pallas kernels, image_scatter(): pl.pallas_call(image_kernel, out_shape=jax.ShapeDtypeStruct((local_rows,...  27.3 us
    ppermute x1, waiting for transfers between devices, with_halo(): lax.ppermute(lax.slice_in_dim(block, 0, width, axis=dim), axis, backward)  7.9 us
    ppermute x1, starting transfers between devices, with_halo(): lax.ppermute(lax.slice_in_dim(block, block.shape[dim] - width, None, axis...  7.21 us
    convert_element_type x4, local copies, waits for them, and re-layouts, per_device(): dense = dense.astype(jnp.bfloat16)  2.53 us
    ppermute x1, starting transfers between devices, with_halo(): lax.ppermute(lax.slice_in_dim(block, 0, width, axis=dim), axis, backward)  1.92 us
  transfers between devices with their start and end apart: 2, of which 2 were waited for; matrix products, arithmetic and copies ran while one was open for 5% of the time, Pallas kernels for 0%

profile of v16, /device:TPU:7, one launch (start us, length us, event | category | flops | bytes accessed | tf_op | source)
XLA Modules:
  0.0 80.3 jit_solution(9928183460767727430)
XLA Ops:
  0.0 0.0 copy-start
  0.0 28.7 %shard_map.55 = bf16[2,2,256,256]{3,2,1,0:T(8,128)(2,1)} custom-call(bf16[8,2,512]{2,1,0:T(2,128)(2,1)} %block_ref.1), custom_call_target="tpu_custom_call" | custom-call | tf_op jit(solution)/shard_map/pallas_call | solution.py:106
  28.7 7.2 %collective-permute-start = (bf16[2,2,256,256]{3,2,1,0:T(8,128)(2,1)}, bf16[2,2,256,256]{3,2,1,0:T(8,128)(2,1)S(1)}, u32[]{:S(2)}, u32[]{:S(2)}) collective-permute-start(bf16[2,2,256,256]{3,2,1,0:T(8,128)(2,1)} %shard_map.55), channel_id=1, source_target_pairs={{0,32},{32,64},{64,96},{96,128},{128,160},{160,192},{192,224},{224... | collective-permute-start | bytes 1572872 | tf_op jit(solution)/shard_map/ppermute | solution.py:318
  35.9 1.9 %collective-permute-start.1 = (bf16[2,2,256,256]{3,2,1,0:T(8,128)(2,1)}, bf16[2,2,256,256]{3,2,1,0:T(8,128)(2,1)S(1)}, u32[]{:S(2)}, u32[]{:S(2)}) collective-permute-start(bf16[2,2,256,256]{3,2,1,0:T(8,128)(2,1)} %shard_map.55), channel_id=1, source_target_pairs={{32,0},{64,32},{96,64},{128,96},{160,128},{192,160},{224,192},{256... | collective-permute-start | bytes 1572872 | tf_op jit(solution)/shard_map/ppermute | solution.py:321
  37.9 0.8 fusion.8
  38.6 0.0 copy-done
  38.6 0.4 fusion
  39.1 1.0 %copy.9 = bf16[2,8,32,8,32]{2,1,4,3,0:T(8,128)(2,1)S(1)} copy(bf16[2,8,32,8,32]{4,1,2,3,0:T(8,128)(2,1)S(1)} %fusion) | data formatting | bytes 524288 | tf_op jit(solution)/shard_map/convert_element_type | solution.py:346
  40.1 0.0 copy-start.2
  40.1 0.0 copy-start.1
  40.1 0.7 convert_element_type.16
  40.8 0.8 %copy.11.triple_ref = bf16[2,256,256]{2,1,0:T(8,128)(2,1)} copy(bf16[2,256,256]{1,2,0:T(8,128)(2,1)S(1)} %bitcast.21) | data formatting | bytes 524288 | tf_op jit(solution)/shard_map/convert_element_type | solution.py:346
  41.7 0.0 copy-done.2
  41.7 0.6 reshape.13.offs_ref
  42.2 0.1 collective-permute-done
  42.4 7.9 %collective-permute-done.1 = bf16[2,2,256,256]{3,2,1,0:T(8,128)(2,1)S(1)} collective-permute-done((bf16[2,2,256,256]{3,2,1,0:T(8,128)(2,1)}, bf16[2,2,256,256]{3,2,1,0:T(8,128)(2,1)S(1)}, u32[]{:S(2)}, u32[]{:S(2)}) %collective-permute-start.1) | collective-permute-done | bytes 524320 | tf_op jit(solution)/shard_map/ppermute | solution.py:321
  50.3 0.0 copy-done.1
  50.3 1.3 %pad_maximum_fusion = bf16[6,2,256,256]{3,2,1,0:T(8,128)(2,1)} fusion(bf16[2,2,256,256]{3,2,1,0:T(8,128)(2,1)S(1)} %collective-permute-done.1, bf16[2,2,256,256]{3,2,1,0:T(8,128)(2,1)S(1)} %copy-done.1, bf16[2,2,256,256]{3,2,1,0:T(8,128)(2,1)S(1)} %collective-permute-done), kind=kLoop, calls=%fused_computation | loop fusion | flops 1572864 | bytes 3145728 | tf_op jit(solution)/shard_map/concatenate | solution.py:322
  51.6 27.3 %shard_map.56 = f32[8,1024]{1,0:T(8,128)} custom-call(s32[24]{0:T(128)} %reshape.13.offs_ref, bf16[6,512,256]{2,1,0:T(8,128)(2,1)} %bitcast.19, bf16[2,2,6,256,256]{4,3,2,1,0:T(8,128)(2,1)} %stiff_ref.1, bf16[2,256,256]{2,1,0:T(8,128)(2,1)} %copy.11.triple_ref), custom_call_target="tpu_custom_call" | custom-call | tf_op jit(solution)/shard_map/pallas_call | solution.py:285
  78.9 1.4 %copy.12 = f32[8,2,512]{2,1,0:T(2,128)} copy(f32[8,2,512]{2,0,1:T(8,128)} %bitcast.22) | data formatting | bytes 65536 | tf_op jit(solution)/shard_map/reshape | solution.py:348
  (2 shorter events, 0.0 us)
Async XLA Ops:
  0.0 38.6 %copy-start = (bf16[2,24,32,32]{3,2,1,0:T(8,128)(2,1)S(1)}, bf16[2,24,32,32]{3,2,1,0:T(8,128)(2,1)}, u32[]{:S(2)}) copy-start(bf16[2,24,32,32]{3,2,1,0:T(8,128)(2,1)} %param.8) | copy-start | bytes 294916
  28.7 13.6 %collective-permute-start = (bf16[2,2,256,256]{3,2,1,0:T(8,128)(2,1)}, bf16[2,2,256,256]{3,2,1,0:T(8,128)(2,1)S(1)}, u32[]{:S(2)}, u32[]{:S(2)}) collective-permute-start(bf16[2,2,256,256]{3,2,1,0:T(8,128)(2,1)} %shard_map.55), channel_id=1, source_target_pairs={{0,32},{32,64},{64,96},{96,128},{128,160},{160,192},{192,224},{224... | collective-permute-start | bytes 1572872 | tf_op jit(solution)/shard_map/ppermute | solution.py:318
  35.9 14.3 %collective-permute-start.1 = (bf16[2,2,256,256]{3,2,1,0:T(8,128)(2,1)}, bf16[2,2,256,256]{3,2,1,0:T(8,128)(2,1)S(1)}, u32[]{:S(2)}, u32[]{:S(2)}) collective-permute-start(bf16[2,2,256,256]{3,2,1,0:T(8,128)(2,1)} %shard_map.55), channel_id=1, source_target_pairs={{32,0},{64,32},{96,64},{128,96},{160,128},{192,160},{224,192},{256... | collective-permute-start | bytes 1572872 | tf_op jit(solution)/shard_map/ppermute | solution.py:321
  40.1 1.6 %copy-start.2 = (s32[2,2,6]{2,1,0:T(2,128)S(1)}, s32[2,2,6]{2,1,0:T(2,128)}, u32[]{:S(2)}) copy-start(s32[2,2,6]{2,1,0:T(2,128)} %param.7) | copy-start | bytes 292
  40.1 10.2 %copy-start.1 = (bf16[2,2,256,256]{3,2,1,0:T(8,128)(2,1)S(1)}, bf16[2,2,256,256]{3,2,1,0:T(8,128)(2,1)}, u32[]{:S(2)}) copy-start(bf16[2,2,256,256]{3,2,1,0:T(8,128)(2,1)} %shard_map.55) | copy-start | bytes 1572868

commit v17 on v16

--- a/solution.py
+++ b/solution.py
@@ -13,8 +13,10 @@
 
 
 def gather_kernel(block_ref, panel_ref, out_ref, flat_ref, local_sem, send_near, recv_near, send_far,
-                  recv_far):
+                  recv_far, halo_send, halo_recv):
     count = out_ref.shape[0]
+    slabs = lax.axis_size("space")
+    rim = (panel_ref.shape[0] - block_ref.shape[2] // panel_ref.shape[-1]) // 2
     rows, loads, cells = block_ref.shape
     for load in range(loads):
         flat_ref[load * rows:(load + 1) * rows, :] = block_ref[:, load, :]
@@ -32,7 +34,21 @@
 
     lax.fori_loop(1, chunk, greet_far, 0)
     lax.fori_loop(1, CLASSES, greet_near, 0)
-    pl.semaphore_wait(barrier, chunk + CLASSES - 2)
+    me = lax.axis_index("term")
+    has_left = row > 0
+    has_right = row < slabs - 1
+
+    @pl.when(has_left)
+    def _():
+        pl.semaphore_signal(barrier, 1, device_id=(row - 1, me), device_id_type=MESH_ID)
+
+    @pl.when(has_right)
+    def _():
+        pl.semaphore_signal(barrier, 1, device_id=(row + 1, me), device_id_type=MESH_ID)
+
+    pl.semaphore_wait(
+        barrier, chunk + CLASSES - 2 + has_left.astype(jnp.int32) + has_right.astype(jnp.int32)
+    )
 
     mine = lane * chunk + stride
     local = pltpu.make_async_copy(flat_ref, out_ref.at[mine], local_sem)
@@ -93,12 +109,48 @@
     lax.fori_loop(1, CLASSES, near_finish, 0)
 
     width = panel_ref.shape[-1]
+    blocks = cells // width
     for slot in range(count):
         for load in range(loads):
-            for block in range(panel_ref.shape[0]):
-                panel_ref[block, load, slot * rows:(slot + 1) * rows, :] = out_ref[
+            for block in range(blocks):
+                panel_ref[rim + block, load, slot * rows:(slot + 1) * rows, :] = out_ref[
                     slot, load * rows:(load + 1) * rows, block * width:(block + 1) * width
                 ]
+    own = panel_ref.at[pl.ds(rim, blocks)]
+    to_left = pltpu.make_async_remote_copy(
+        own, panel_ref.at[pl.ds(rim + blocks, rim)], halo_send.at[0], halo_recv.at[0],
+        device_id=(row - 1, me), device_id_type=MESH_ID,
+    )
+    to_right = pltpu.make_async_remote_copy(
+        own, panel_ref.at[pl.ds(0, rim)], halo_send.at[1], halo_recv.at[1],
+        device_id=(row + 1, me), device_id_type=MESH_ID,
+    )
+
+    @pl.when(has_left)
+    def _():
+        to_left.start()
+
+    @pl.when(has_right)
+    def _():
+        to_right.start()
+
+    @pl.when(jnp.logical_not(has_left))
+    def _():
+        panel_ref[pl.ds(0, rim)] = jnp.zeros((rim,) + panel_ref.shape[1:], panel_ref.dtype)
+
+    @pl.when(jnp.logical_not(has_right))
+    def _():
+        panel_ref[pl.ds(rim + blocks, rim)] = jnp.zeros((rim,) + panel_ref.shape[1:], panel_ref.dtype)
+
+    @pl.when(has_left)
+    def _():
+        to_left.wait_send()
+        to_right.wait_recv()
+
+    @pl.when(has_right)
+    def _():
+        to_right.wait_send()
+        to_left.wait_recv()
 
 
 def gather_term(block, width):
@@ -106,7 +158,7 @@
     return pl.pallas_call(
         gather_kernel,
         out_shape=jax.ShapeDtypeStruct(
-            (block.shape[2] // width, block.shape[1], count * block.shape[0], width), block.dtype
+            (block.shape[2] // width + 4, block.shape[1], count * block.shape[0], width), block.dtype
         ),
         in_specs=[pl.BlockSpec(memory_space=pltpu.VMEM)],
         out_specs=pl.BlockSpec(memory_space=pltpu.VMEM),
@@ -118,6 +170,8 @@
             pltpu.SemaphoreType.DMA((CLASSES,)),
             pltpu.SemaphoreType.DMA((count // CLASSES,)),
             pltpu.SemaphoreType.DMA((count // CLASSES,)),
+            pltpu.SemaphoreType.DMA((2,)),
+            pltpu.SemaphoreType.DMA((2,)),
         ],
         compiler_params=pltpu.CompilerParams(collective_id=0, has_side_effects=True),
     )(block)
@@ -334,8 +388,7 @@
     total_rows = local_rows * groups
     rim_cells = 2 * block_width
     panel = gather_term(chaos_field, block_width)
-    extended = with_halo(panel, (("space", 0),), rim_cells // block_width)
-    extended = extended.reshape(block_rows + 4, load_count * total_rows, block_width)
+    extended = panel.reshape(block_rows + 4, load_count * total_rows, block_width)
     block_size = triple_blocks.shape[2]
     levels = jnp.arange(total_rows // block_size, dtype=jnp.int32)
     row_hot = (triple_pattern[:, :, 0:1] == levels).astype(jnp.float32)

time: 80.6 us -> 78.8 us (0.978)
  Pallas kernels: 56 us -> 71.8 us
  starting transfers between devices: 9.13 us -> 0 us
  waiting for transfers between devices: 8.01 us -> 0 us
  other arithmetic: 1.33 us -> 0.01 us
    pallas_call x1, Pallas kernels: 28.7 us -> 41.2 us  [gather_term(): pl.pallas_call(gather_kernel, out_shape=jax.ShapeDtypeStruct((block.shape...]
    ppermute x2 -> x0, starting transfers between devices: 9.13 us -> none  [the longest x1 7.21 us: with_halo(): lax.ppermute(lax.slice_in_dim(block, block.shape[dim] - width, None, axis...]
    ppermute x2 -> x0, waiting for transfers between devices: 8.01 us -> none  [the longest x1 7.9 us: with_halo(): lax.ppermute(lax.slice_in_dim(block, 0, width, axis=dim), axis, backward)]
    pallas_call x1, Pallas kernels: 27.3 us -> 30.6 us  [image_scatter(): pl.pallas_call(image_kernel, out_shape=jax.ShapeDtypeStruct((local_rows,...]
    concatenate x1 -> x0, other arithmetic: 1.33 us -> none  [with_halo(): block = jnp.concatenate([low, block, high], axis=dim)]
  transfers between devices with their start and end apart: 2 -> 0, of which waited for: 2 -> 0; matrix products, arithmetic and copies ran while one was open for 5% -> 0% of each run, Pallas kernels for 0% -> 0%
where the time goes in v17:
time: 78.8 us; the launch traced here: 77.9 us
  Pallas kernels  71.8 us (91%)
  local copies, waits for them, and re-layouts  5.57 us (7%)
    pallas_call x1, Pallas kernels, gather_term(): pl.pallas_call(gather_kernel, out_shape=jax.ShapeDtypeStruct((block.shape...  41.2 us
    pallas_call x1, Pallas kernels, image_scatter(): pl.pallas_call(image_kernel, out_shape=jax.ShapeDtypeStruct((local_rows,...  30.6 us
    convert_element_type x4, local copies, waits for them, and re-layouts, per_device(): dense = dense.astype(jnp.bfloat16)  2.55 us

profile of v17, /device:TPU:7, one launch (start us, length us, event | category | flops | bytes accessed | tf_op | source)
XLA Modules:
  0.0 77.9 jit_solution(12050623854535825281)
XLA Ops:
  0.0 0.0 copy-start
  0.0 0.8 fusion.8
  0.8 0.3 copy-done
  1.0 0.4 fusion
  1.5 1.0 %copy.9 = bf16[2,8,32,8,32]{2,1,4,3,0:T(8,128)(2,1)S(1)} copy(bf16[2,8,32,8,32]{4,1,2,3,0:T(8,128)(2,1)S(1)} %fusion) | data formatting | bytes 524288 | tf_op jit(solution)/shard_map/convert_element_type | solution.py:399
  2.4 0.0 copy-start.1
  2.5 0.7 convert_element_type.16
  3.2 0.8 %copy.11.triple_ref = bf16[2,256,256]{2,1,0:T(8,128)(2,1)} copy(bf16[2,256,256]{1,2,0:T(8,128)(2,1)S(1)} %bitcast.21) | data formatting | bytes 524288 | tf_op jit(solution)/shard_map/convert_element_type | solution.py:399
  4.0 41.2 %shard_map.55 = bf16[6,2,256,256]{3,2,1,0:T(8,128)(2,1)} custom-call(bf16[8,2,512]{2,1,0:T(2,128)(2,1)} %block_ref.1), custom_call_target="tpu_custom_call" | custom-call | tf_op jit(solution)/shard_map/pallas_call | solution.py:158
  45.2 0.0 copy-done.1
  45.2 0.6 reshape.13.offs_ref
  45.8 30.6 %shard_map.56 = f32[8,1024]{1,0:T(8,128)} custom-call(s32[24]{0:T(128)} %reshape.13.offs_ref, bf16[6,512,256]{2,1,0:T(8,128)(2,1)} %bitcast.19, bf16[2,2,6,256,256]{4,3,2,1,0:T(8,128)(2,1)} %stiff_ref.1, bf16[2,256,256]{2,1,0:T(8,128)(2,1)} %copy.11.triple_ref), custom_call_target="tpu_custom_call" | custom-call | tf_op jit(solution)/shard_map/pallas_call | solution.py:339
  76.5 1.4 %copy.12 = f32[8,2,512]{2,1,0:T(2,128)} copy(f32[8,2,512]{2,0,1:T(8,128)} %bitcast.22) | data formatting | bytes 65536 | tf_op jit(solution)/shard_map/reshape | solution.py:401
  (2 shorter events, 0.0 us)
Async XLA Ops:
  0.0 1.0 %copy-start = (bf16[2,24,32,32]{3,2,1,0:T(8,128)(2,1)S(1)}, bf16[2,24,32,32]{3,2,1,0:T(8,128)(2,1)}, u32[]{:S(2)}) copy-start(bf16[2,24,32,32]{3,2,1,0:T(8,128)(2,1)} %param.8) | copy-start | bytes 294916
  2.4 42.8 %copy-start.1 = (s32[2,2,6]{2,1,0:T(2,128)S(1)}, s32[2,2,6]{2,1,0:T(2,128)}, u32[]{:S(2)}) copy-start(s32[2,2,6]{2,1,0:T(2,128)} %param.7) | copy-start | bytes 292

commit v18 on v17

--- a/solution.py
+++ b/solution.py
@@ -236,7 +236,7 @@
 
     total = jnp.zeros((loads * rows, width), jnp.float32)
     for slot in range(band):
-        place = block + rim + offs_ref[(term * block_rows + block) * band + slot]
+        place = block + rim + offs_ref[term, block, slot]
         total += lax.dot_general(
             panel_ref[place], stiff_ref[0, 0, slot],
             (((1,), (1,)), ((), ())), preferred_element_type=jnp.float32,
@@ -361,7 +361,7 @@
             ],
         ),
         compiler_params=pltpu.CompilerParams(collective_id=1, has_side_effects=True),
-    )(offsets.reshape(-1), panel, stiff_blocks, dense)
+    )(offsets, panel, stiff_blocks, dense)
 
 
 def with_halo(block, sides, width):

time: 78.8 us -> 79 us (level)
  no operation moved by 1% of the time
where the time goes in v18:
time: 79 us; the launch traced here: 78 us
  Pallas kernels  71.8 us (91%)
  local copies, waits for them, and re-layouts  5.7 us (7%)
    pallas_call x1, Pallas kernels, gather_term(): pl.pallas_call(gather_kernel, out_shape=jax.ShapeDtypeStruct((block.shape...  41.2 us
    pallas_call x1, Pallas kernels, image_scatter(): pl.pallas_call(image_kernel, out_shape=jax.ShapeDtypeStruct((local_rows,...  30.7 us
    convert_element_type x4, local copies, waits for them, and re-layouts, per_device(): dense = dense.astype(jnp.bfloat16)  2.54 us

profile of v18, /device:TPU:7, one launch (start us, length us, event | category | flops | bytes accessed | tf_op | source)
XLA Modules:
  0.0 78.0 jit_solution(9215524691608298275)
XLA Ops:
  0.0 0.0 copy-start
  0.0 1.0 %copy-done = bf16[2,24,32,32]{3,2,1,0:T(8,128)(2,1)S(1)} copy-done((bf16[2,24,32,32]{3,2,1,0:T(8,128)(2,1)S(1)}, bf16[2,24,32,32]{3,2,1,0:T(8,128)(2,1)}, u32[]{:S(2)}) %copy-start) | copy-done | bytes 98328
  1.0 0.8 fusion.8
  1.8 0.4 fusion
  2.2 1.0 %copy.9 = bf16[2,8,32,8,32]{2,1,4,3,0:T(8,128)(2,1)S(1)} copy(bf16[2,8,32,8,32]{4,1,2,3,0:T(8,128)(2,1)S(1)} %fusion) | data formatting | bytes 524288 | tf_op jit(solution)/shard_map/convert_element_type | solution.py:399
  3.2 0.7 convert_element_type.16
  3.9 0.8 %copy.11.triple_ref = bf16[2,256,256]{2,1,0:T(8,128)(2,1)} copy(bf16[2,256,256]{1,2,0:T(8,128)(2,1)S(1)} %bitcast.21) | data formatting | bytes 524288 | tf_op jit(solution)/shard_map/convert_element_type | solution.py:399
  4.8 41.2 %shard_map.55 = bf16[6,2,256,256]{3,2,1,0:T(8,128)(2,1)} custom-call(bf16[8,2,512]{2,1,0:T(2,128)(2,1)} %block_ref.1), custom_call_target="tpu_custom_call" | custom-call | tf_op jit(solution)/shard_map/pallas_call | solution.py:158
  45.9 30.7 %shard_map.56 = f32[8,1024]{1,0:T(8,128)} custom-call(s32[2,2,6]{2,1,0:T(2,128)} %offs_ref.1, bf16[6,512,256]{2,1,0:T(8,128)(2,1)} %bitcast.19, bf16[2,2,6,256,256]{4,3,2,1,0:T(8,128)(2,1)} %stiff_ref.1, bf16[2,256,256]{2,1,0:T(8,128)(2,1)} %copy.11.triple_ref), custom_call_target="tpu_custom_call" | custom-call | tf_op jit(solution)/shard_map/pallas_call | solution.py:339
  76.6 1.4 %copy.12 = f32[8,2,512]{2,1,0:T(2,128)} copy(f32[8,2,512]{2,0,1:T(8,128)} %bitcast.22) | data formatting | bytes 65536 | tf_op jit(solution)/shard_map/reshape | solution.py:401
  (2 shorter events, 0.0 us)
Async XLA Ops:
  0.0 1.0 %copy-start = (bf16[2,24,32,32]{3,2,1,0:T(8,128)(2,1)S(1)}, bf16[2,24,32,32]{3,2,1,0:T(8,128)(2,1)}, u32[]{:S(2)}) copy-start(bf16[2,24,32,32]{3,2,1,0:T(8,128)(2,1)} %param.8) | copy-start | bytes 294916
